TPU v7x, 256 devices: a whole 4x4x8 slice. The times are simulated.
256 devices in a mesh: leaf: 32 (over z, y), front: 8 (over x, core).
Axes of the slice: x: 4, y: 4, z: 8, core: 2. Of those that a mesh axis runs over, the one named last changes fastest.
Arguments:
- section_updates: bfloat16 [32768, 256], P(('leaf', 'front')), may hold values from -6 to 6
- upper_rhs: float32 [126976, 256], P(('leaf', 'front')), may hold values from -6 to 6
- pivot_inverse: bfloat16 [126976, 4096], P('leaf', 'front'), may hold values from -0.09375 to 0.09375
- coupling: bfloat16 [1024, 122880], P('front', 'leaf'), may hold values from -0.09375 to 0.09375
- extend_lists: int32 [62, 8], replicated, may hold values from 0 to 39, as said below
Outputs:
- solution: float32 [126976, 256], P(('leaf', 'front'))
- interface: bfloat16 [32768, 256], P(('leaf', 'front'))
Inputs may be any that keep to these rules, and one draw needn't show every extreme that they name: `extend_lists`: each row names 8 different blocks of the parent's frame; the rows of the root's two children name pivot blocks only, below 32.
All inputs are finite; a program needn't handle non-finite values.
Results may differ from a plain program's by a relative error of at most 0.022.
Values may be sent and summed in bfloat16 or wider, within the bound.
A program may use at most 64 MiB of HBM per device.

v0:
```python
import jax
import jax.numpy as jnp
from jax import lax
from jax.sharding import PartitionSpec as P

PIV = 4096
UPD = 1024
BLK = 128


def partner(block, axis, stride):
    count = lax.axis_size(axis)
    route = []
    for low in range(count):
        high = low | 1 << stride
        if high != low and high < count:
            route += [(low, high), (high, low)]
    return lax.ppermute(block, axis, route)


def child_base(leaves, height):
    total_rows = 0
    for depth in range(height - 1):
        total_rows = total_rows + leaves // 2**depth
    return total_rows


def list_row(extend_lists, row_index):
    return lax.dynamic_slice_in_dim(extend_lists, row_index, 1, 0)[0]


def upper_bit(position, bit_index):
    return position >> bit_index & 1 == 1


def joined(position, bit_index, portion, partner_rows):
    return jnp.where(
        upper_bit(position, bit_index),
        jnp.concatenate([partner_rows, portion], 0),
        jnp.concatenate([portion, partner_rows], 0),
    )


def gather_own(portion, height, position):
    for bit_index in range(height):
        partner_rows = partner(portion.astype(jnp.bfloat16), "leaf", bit_index).astype(
            portion.dtype
        )
        portion = joined(position, bit_index, portion, partner_rows)
    return portion


def sum_updates(summand, height):
    for bit_index in range(height):
        summand = summand + partner(summand.astype(jnp.bfloat16), "leaf", bit_index).astype(
            summand.dtype
        )
    return summand


def sum_solution(summand, height):
    for bit_index in range(height):
        summand = summand + partner(summand.astype(jnp.bfloat16), "leaf", bit_index).astype(
            summand.dtype
        )
    return summand


def per_device(section_updates, upper_rhs, pivot_inverse, coupling, extend_lists):
    leaves = lax.axis_size("leaf")
    fronts = lax.axis_size("front")
    levels = leaves.bit_length() - 1
    position = lax.axis_index("leaf")
    column = lax.axis_index("front")
    rhs_width = upper_rhs.shape[1]
    piv_dev = PIV // fronts
    upd_dev = UPD // fronts
    piv_blocks = piv_dev // BLK
    upd_blocks = upd_dev // BLK
    block_count = UPD // BLK
    local_blocks = jnp.concatenate(
        [
            column * piv_blocks + jnp.arange(piv_blocks, dtype=jnp.int32),
            PIV // BLK + column * upd_blocks + jnp.arange(upd_blocks, dtype=jnp.int32),
        ]
    )
    local_count = piv_blocks + upd_blocks
    carried = section_updates
    saved_part = []
    saved_half = []
    for height in range(1, levels + 1):
        group_size = 2**height
        span_rows = PIV // group_size
        band_start = PIV - PIV // 2 ** (height - 1)
        rhs_len = piv_dev // group_size
        rhs_start = piv_dev - piv_dev // 2 ** (height - 1)
        member = position & group_size - 1
        own_child = child_base(leaves, height) + (position >> height - 1)
        sibling = partner(carried, "leaf", height - 1)
        pair_blocks = lax.all_gather(jnp.stack([carried, sibling]), "front", axis=1, tiled=True)
        pair_lists = jnp.stack(
            [list_row(extend_lists, own_child), list_row(extend_lists, own_child ^ 1)]
        )
        chooser = (pair_lists.reshape(2 * block_count)[None, :] == local_blocks[:, None]).astype(
            jnp.bfloat16
        )
        assembled = jnp.dot(
            chooser,
            pair_blocks.reshape(2 * block_count, BLK * rhs_width),
            preferred_element_type=jnp.float32,
        ).reshape(local_count * BLK, rhs_width)
        own_rows = gather_own(upper_rhs[rhs_start : rhs_start + rhs_len], height, position)
        rows_half = (own_rows + assembled[:piv_dev]).astype(jnp.bfloat16)
        g_share = pivot_inverse[band_start : band_start + span_rows]
        pivot_part = lax.psum(
            jnp.dot(g_share, rows_half, preferred_element_type=jnp.float32).astype(jnp.bfloat16),
            "front",
        ).astype(jnp.float32)
        pivot_half = pivot_part.astype(jnp.bfloat16)
        saved_part.append(pivot_part)
        saved_half.append(pivot_half)
        if height < levels:
            c_share = coupling[:, band_start : band_start + span_rows]
            summand = jnp.dot(c_share, pivot_half, preferred_element_type=jnp.float32)
            frame_upd = assembled[piv_dev:]
            carried = (frame_upd - sum_updates(summand, height)).astype(jnp.bfloat16)
    from_above = carried
    outputs = []
    for height in range(levels, 0, -1):
        group_size = 2**height
        span_rows = PIV // group_size
        band_start = PIV - PIV // 2 ** (height - 1)
        member = position & group_size - 1
        pivot_part = saved_part[height - 1]
        if height < levels:
            c_share = coupling[:, band_start : band_start + span_rows]
            back_total = lax.psum(
                jnp.einsum(
                    "up,ur->pr", c_share, from_above, preferred_element_type=jnp.float32
                ).astype(jnp.bfloat16),
                "front",
            ).astype(jnp.float32)
            weight_half = (pivot_part - back_total).astype(jnp.bfloat16)
            upper_rows = from_above
        else:
            weight_half = saved_half[height - 1]
            upper_rows = jnp.zeros((upd_dev, rhs_width), jnp.bfloat16)
        g_share = pivot_inverse[band_start : band_start + span_rows]
        solve_term = jnp.einsum(
            "cp,cr->pr", g_share, weight_half, preferred_element_type=jnp.float32
        )
        part_len = piv_dev // group_size
        summed = sum_solution(solve_term, height)
        portion = lax.dynamic_slice_in_dim(summed, member * part_len, part_len, 0)
        rows_half = summed.astype(jnp.bfloat16)
        outputs.append(portion)
        frame_half = jnp.concatenate([rows_half, upper_rows], 0).reshape(
            local_count, BLK * rhs_width
        )
        child_list = list_row(extend_lists, child_base(leaves, height) + (position >> height - 1))
        picker = (child_list[:, None] == local_blocks[None, :]).astype(jnp.bfloat16)
        outgoing = (
            jnp.dot(picker, frame_half, preferred_element_type=jnp.float32)
            .astype(jnp.bfloat16)
            .reshape(fronts, upd_dev, rhs_width)
        )
        incoming = lax.all_to_all(outgoing, "front", split_axis=0, concat_axis=0, tiled=True)
        from_above = jnp.sum(incoming, axis=0, dtype=jnp.float32).astype(jnp.bfloat16)
    solution = jnp.concatenate(outputs[::-1], 0)
    return (solution, from_above)


def solution(mesh):
    placed = (
        P(("leaf", "front"), None),
        P(("leaf", "front"), None),
        P("leaf", "front"),
        P("front", "leaf"),
        P(),
    )
    return jax.shard_map(
        per_device,
        mesh=mesh,
        in_specs=placed,
        out_specs=(P(("leaf", "front"), None), P(("leaf", "front"), None)),
        check_vma=False,
    )
```

profile of v0, /device:TPU:1, one launch (start us, length us, event | category | flops | bytes accessed | tf_op | source)
XLA Modules:
  0.0 1092.0 jit_solution(5823587160174523353)
XLA Ops:
  18.5 25.0 %all-gather.6.cloned.1.call-done = bf16[2,1024,256]{2,1,0:T(8,128)(2,1)} async-done(((bf16[2,128,256]{2,1,0:T(8,128)(2,1)}), bf16[2,1024,256]{2,1,0:T(8,128)(2,1)}) %all-gather.6.cloned.1.call-update) | async-done | bytes 1048592 | tf_op jit(solution)/shard_map/all_gather | solution.py:100
  49.5 65.4 %all-reduce.11.cloned.1.call-done = bf16[2048,256]{0,1:T(8,128)(2,1)} async-done(((bf16[2048,256]{0,1:T(8,128)(2,1)}), bf16[2048,256]{0,1:T(8,128)(2,1)}) %all-reduce.11.cloned.1.call-update) | async-done | bytes 1048592 | tf_op jit(solution)/shard_map/psum | solution.py:115
  135.2 20.1 %all-gather.8.cloned.1.call-done = bf16[2,1024,256]{1,2,0:T(8,128)(2,1)} async-done(((bf16[2,128,256]{1,2,0:T(8,128)(2,1)}), bf16[2,1024,256]{1,2,0:T(8,128)(2,1)}) %all-gather.8.cloned.1.call-update) | async-done | bytes 1048592 | tf_op jit(solution)/shard_map/all_gather | solution.py:100
  161.8 64.7 %all-reduce.13.cloned.1.call-done = bf16[1024,256]{0,1:T(8,128)(2,1)} async-done(((bf16[1024,256]{0,1:T(8,128)(2,1)}), bf16[1024,256]{0,1:T(8,128)(2,1)}) %all-reduce.13.cloned.1.call-update) | async-done | bytes 524304 | tf_op jit(solution)/shard_map/psum | solution.py:115
  252.5 18.5 %all-gather.10.cloned.1.call-done = bf16[2,1024,256]{1,2,0:T(8,128)(2,1)} async-done(((bf16[2,128,256]{1,2,0:T(8,128)(2,1)}), bf16[2,1024,256]{1,2,0:T(8,128)(2,1)}) %all-gather.10.cloned.1.call-update) | async-done | bytes 1048592 | tf_op jit(solution)/shard_map/all_gather | solution.py:100
  277.1 63.9 %all-reduce.15.cloned.1.call-done = bf16[512,256]{0,1:T(8,128)(2,1)} async-done(((bf16[512,256]{0,1:T(8,128)(2,1)}), bf16[512,256]{0,1:T(8,128)(2,1)}) %all-reduce.15.cloned.1.call-update) | async-done | bytes 262160 | tf_op jit(solution)/shard_map/psum | solution.py:115
  376.0 15.2 %all-gather.12.cloned.1.call-done = bf16[2,1024,256]{1,2,0:T(8,128)(2,1)} async-done(((bf16[2,128,256]{1,2,0:T(8,128)(2,1)}), bf16[2,1024,256]{1,2,0:T(8,128)(2,1)}) %all-gather.12.cloned.1.call-update) | async-done | bytes 1048592 | tf_op jit(solution)/shard_map/all_gather | solution.py:100
  397.1 63.6 %all-reduce.17.cloned.1.call-done = bf16[256,256]{0,1:T(8,128)(2,1)} async-done(((bf16[256,256]{0,1:T(8,128)(2,1)}), bf16[256,256]{0,1:T(8,128)(2,1)}) %all-reduce.17.cloned.1.call-update) | async-done | bytes 131088 | tf_op jit(solution)/shard_map/psum | solution.py:115
  477.2 6.3 collective-permute-start.29
  501.5 5.0 collective-permute-start.24
  509.4 11.0 %all-gather.14.cloned.1.call-done = bf16[2,1024,256]{1,2,0:T(8,128)(2,1)} async-done(((bf16[2,128,256]{1,2,0:T(8,128)(2,1)}), bf16[2,1024,256]{1,2,0:T(8,128)(2,1)}) %all-gather.14.cloned.1.call-update) | async-done | bytes 1048592 | tf_op jit(solution)/shard_map/all_gather | solution.py:100
  525.2 66.1 %all-reduce.19.cloned.1.call-done = bf16[128,256]{0,1:T(8,128)(2,1)} async-done(((bf16[128,256]{0,1:T(8,128)(2,1)}), bf16[128,256]{0,1:T(8,128)(2,1)}) %all-reduce.19.cloned.1.call-update) | async-done | bytes 65552 | tf_op jit(solution)/shard_map/psum | solution.py:115
  593.5 4.2 collective-permute-done.30
  600.4 5.5 collective-permute-done.31
  613.8 6.7 collective-permute-done.33
  620.6 5.5 collective-permute-start.34
  626.2 6.8 collective-permute-done.34
  634.9 30.3 %all_to_all.25 = bf16[8,128,256]{2,1,0:T(8,128)(2,1)S(1)} all-to-all(bf16[8,128,256]{2,1,0:T(8,128)(2,1)S(1)} %copy.50), channel_id=1, replica_groups=mesh['leaf'=32,'front'=8] {'front'}, dimensions={0} | all-to-all | bytes 1048576 | tf_op jit(solution)/shard_map/all_to_all | solution.py:167
  666.2 59.3 %all-reduce.21.cloned.1.call-done = bf16[256,256]{0,1:T(8,128)(2,1)} async-done(((bf16[256,256]{0,1:T(8,128)(2,1)}), bf16[256,256]{0,1:T(8,128)(2,1)}) %all-reduce.21.cloned.1.call-update) | async-done | bytes 131088 | tf_op jit(solution)/shard_map/psum | solution.py:137
  728.0 4.1 collective-permute-done.35
  734.9 5.4 collective-permute-done.36
  748.6 6.6 collective-permute-done.38
  757.2 24.9 %all_to_all.26 = bf16[8,128,256]{2,1,0:T(8,128)(2,1)S(1)} all-to-all(bf16[8,128,256]{2,1,0:T(8,128)(2,1)S(1)} %copy.54), channel_id=1, replica_groups=mesh['leaf'=32,'front'=8] {'front'}, dimensions={0} | all-to-all | bytes 1048576 | tf_op jit(solution)/shard_map/all_to_all | solution.py:167
  783.2 62.7 %all-reduce.23.cloned.1.call-done = bf16[512,256]{0,1:T(8,128)(2,1)} async-done(((bf16[512,256]{0,1:T(8,128)(2,1)}), bf16[512,256]{0,1:T(8,128)(2,1)}) %all-reduce.23.cloned.1.call-update) | async-done | bytes 262160 | tf_op jit(solution)/shard_map/psum | solution.py:137
  855.5 5.4 collective-permute-done.40
  868.3 20.9 %all_to_all.27 = bf16[8,128,256]{2,1,0:T(8,128)(2,1)S(1)} all-to-all(bf16[8,128,256]{2,1,0:T(8,128)(2,1)S(1)} %copy.58), channel_id=1, replica_groups=mesh['leaf'=32,'front'=8] {'front'}, dimensions={0} | all-to-all | bytes 1048576 | tf_op jit(solution)/shard_map/all_to_all | solution.py:167
  890.4 63.8 %all-reduce.25.cloned.1.call-done = bf16[1024,256]{0,1:T(8,128)(2,1)} async-done(((bf16[1024,256]{0,1:T(8,128)(2,1)}), bf16[1024,256]{0,1:T(8,128)(2,1)}) %all-reduce.25.cloned.1.call-update) | async-done | bytes 524304 | tf_op jit(solution)/shard_map/psum | solution.py:137
  964.4 5.2 collective-permute-done.43
  970.8 19.0 %all_to_all.28 = bf16[8,128,256]{2,1,0:T(8,128)(2,1)S(1)} all-to-all(bf16[8,128,256]{2,1,0:T(8,128)(2,1)S(1)} %copy.62), channel_id=1, replica_groups=mesh['leaf'=32,'front'=8] {'front'}, dimensions={0} | all-to-all | bytes 1048576 | tf_op jit(solution)/shard_map/all_to_all | solution.py:167
  991.3 65.7 %all-reduce.27.cloned.1.call-done = bf16[2048,256]{0,1:T(8,128)(2,1)} async-done(((bf16[2048,256]{0,1:T(8,128)(2,1)}), bf16[2048,256]{0,1:T(8,128)(2,1)}) %all-reduce.27.cloned.1.call-update) | async-done | bytes 1048592 | tf_op jit(solution)/shard_map/psum | solution.py:137
  1066.9 8.3 all-to-all-start.4
  1078.4 6.1 all-to-all-done.4
  (307 shorter events, 235.7 us)
Async XLA Ops:
  7.2 36.2 %all-gather.6.cloned.1.call-start = ((), (), s32[]{:S(2)}) async-start(), calls=%async_computation.5 | async-start | bytes 1179648 | tf_op jit(solution)/shard_map/all_gather | solution.py:100
  12.8 102.0 %all-reduce.11.cloned.1.call-start = ((), (), s32[]{:S(2)}) async-start(), calls=%async_computation.6 | async-start | bytes 2097152 | tf_op jit(solution)/shard_map/psum | solution.py:115
  49.5 105.8 %all-gather.8.cloned.1.call-start = ((), (), s32[]{:S(2)}) async-start(), calls=%async_computation.7 | async-start | bytes 1179648 | tf_op jit(solution)/shard_map/all_gather | solution.py:100
  125.3 101.3 %all-reduce.13.cloned.1.call-start = ((), (), s32[]{:S(2)}) async-start(), calls=%async_computation.8 | async-start | bytes 1048576 | tf_op jit(solution)/shard_map/psum | solution.py:115
  129.8 5.3 collective-permute-start.3
  161.7 109.2 %all-gather.10.cloned.1.call-start = ((), (), s32[]{:S(2)}) async-start(), calls=%async_computation.9 | async-start | bytes 1179648 | tf_op jit(solution)/shard_map/all_gather | solution.py:100
  239.7 101.2 %all-reduce.15.cloned.1.call-start = ((), (), s32[]{:S(2)}) async-start(), calls=%async_computation.10 | async-start | bytes 524288 | tf_op jit(solution)/shard_map/psum | solution.py:115
  277.0 114.2 %all-gather.12.cloned.1.call-start = ((), (), s32[]{:S(2)}) async-start(), calls=%async_computation.11 | async-start | bytes 1179648 | tf_op jit(solution)/shard_map/all_gather | solution.py:100
  358.2 102.5 %all-reduce.17.cloned.1.call-start = ((), (), s32[]{:S(2)}) async-start(), calls=%async_computation.12 | async-start | bytes 262144 | tf_op jit(solution)/shard_map/psum | solution.py:115
  369.3 6.6 collective-permute-start.15
  397.1 123.3 %all-gather.14.cloned.1.call-start = ((), (), s32[]{:S(2)}) async-start(), calls=%async_computation.13 | async-start | bytes 1179648 | tf_op jit(solution)/shard_map/all_gather | solution.py:100
  477.2 8.1 collective-permute-start.29
  485.9 105.4 %all-reduce.19.cloned.1.call-start = ((), (), s32[]{:S(2)}) async-start(), calls=%async_computation.14 | async-start | bytes 131072 | tf_op jit(solution)/shard_map/psum | solution.py:115
  501.5 7.8 collective-permute-start.24
  525.1 200.5 %all-reduce.21.cloned.1.call-start = ((), (), s32[]{:S(2)}) async-start(), calls=%async_computation.15 | async-start | bytes 262144 | tf_op jit(solution)/shard_map/psum | solution.py:137
  597.8 8.2 collective-permute-start.31
  606.1 5.3 collective-permute-start.32
  611.5 9.1 collective-permute-start.33
  620.6 12.3 %collective-permute-start.34 = (bf16[512,256]{0,1:T(8,128)(2,1)S(1)}, bf16[512,256]{0,1:T(8,128)(2,1)S(1)}, u32[]{:S(2)}, u32[]{:S(2)}) collective-permute-start(bf16[512,256]{0,1:T(8,128)(2,1)S(1)} %fusion.51), channel_id=1, source_target_pairs={{0,128},{128,0},{8,136},{136,8},{16,144},{144,16},{24,152},{152,24... | collective-permute-start | bytes 786440 | tf_op jit(solution)/shard_map/ppermute | solution.py:18
  666.2 179.7 %all-reduce.23.cloned.1.call-start = ((), (), s32[]{:S(2)}) async-start(), calls=%async_computation.16 | async-start | bytes 524288 | tf_op jit(solution)/shard_map/psum | solution.py:137
  726.8 5.3 collective-permute-start.35
  732.2 8.2 collective-permute-start.36
  740.5 5.3 collective-permute-start.37
  745.9 9.3 collective-permute-start.38
  783.1 171.1 %all-reduce.25.cloned.1.call-start = ((), (), s32[]{:S(2)}) async-start(), calls=%async_computation.17 | async-start | bytes 1048576 | tf_op jit(solution)/shard_map/psum | solution.py:137
  847.3 5.3 collective-permute-start.39
  852.7 8.2 collective-permute-start.40
  861.0 5.3 collective-permute-start.41
  890.4 166.6 %all-reduce.27.cloned.1.call-start = ((), (), s32[]{:S(2)}) async-start(), calls=%async_computation.18 | async-start | bytes 2097152 | tf_op jit(solution)/shard_map/psum | solution.py:137
  961.5 8.2 collective-permute-start.43
  1059.6 5.3 collective-permute-start.44
  1066.9 17.6 %all-to-all-start.4 = ((bf16[8,128,256]{2,1,0:T(8,128)(2,1)}), bf16[8,128,256]{2,1,0:T(8,128)(2,1)S(1)}, u32[]{:S(2)}, u32[]{:S(2)}) async-start(bf16[8,128,256]{2,1,0:T(8,128)(2,1)} %copy.66), calls=%async_computation.4 | async-start | bytes 1048576 | tf_op jit(solution)/shard_map/all_to_all | solution.py:167
  (43 other events, 1283.6 us)
Sparse Core Ops, SparseCore 0:
  12.9 30.4 all-gather.5
  49.6 65.2 all-reduce.10
  125.4 29.7 all-gather.7
  161.8 64.6 all-reduce.12
  239.9 31.0 all-gather.9
  277.1 63.8 all-reduce.14
  358.3 32.8 all-gather.11
  397.2 63.4 all-reduce.16
  486.0 34.3 all-gather.13
  525.2 66.0 all-reduce.18
  666.3 59.1 all-reduce.20
  783.3 62.6 all-reduce.22
  890.5 63.6 all-reduce.24
  991.4 65.4 all-reduce.26
where the time goes:
time: 1100 us; the launch traced here: 1090 us
  waiting for transfers between devices  799 us (73%)
  starting transfers between devices  105 us (10%)
  blocking collectives  95 us (9%)
  matrix products  34.2 us (3%)
  local copies, waits for them, and re-layouts  29.3 us (3%)
  between operations  15.1 us (1%)
  other arithmetic  13.8 us (1%)
    psum x5, waiting for transfers between devices, per_device(): lax.psum(jnp.dot(g_share, rows_half, preferred_element_type=jnp.float32)....  324 us
    psum x4, waiting for transfers between devices, per_device(): lax.psum(jnp.einsum('up,ur->pr', c_share, from_above, preferred_element_t...  252 us
    ppermute x45, waiting for transfers between devices, partner(): return lax.ppermute(block, axis, route)  128 us
    ppermute x45, starting transfers between devices, partner(): return lax.ppermute(block, axis, route)  96.3 us
    all_to_all x4, blocking collectives, per_device(): lax.all_to_all(outgoing, 'front', split_axis=0, concat_axis=0, tiled=True)  95 us
    all_gather x5, waiting for transfers between devices, per_device(): lax.all_gather(jnp.stack([carried, sibling]), 'front', axis=1, tiled=True)  89.7 us
  transfers between devices with their start and end apart: 60, of which 60 were waited for; matrix products, arithmetic and copies ran while one was open for 1% of the time, Pallas kernels for 0%

commit v1 on v0

--- a/solution.py
+++ b/solution.py
@@ -66,6 +66,16 @@
     return summand
 
 
+def front_sum(summand):
+    bits = lax.axis_size("front").bit_length() - 1
+    for bit_index in range(bits):
+        half = summand.astype(jnp.bfloat16)
+        summand = half.astype(jnp.float32) + partner(half, "front", bit_index).astype(
+            jnp.float32
+        )
+    return summand
+
+
 def per_device(section_updates, upper_rhs, pivot_inverse, coupling, extend_lists):
     leaves = lax.axis_size("leaf")
     fronts = lax.axis_size("front")
@@ -112,10 +122,9 @@
         own_rows = gather_own(upper_rhs[rhs_start : rhs_start + rhs_len], height, position)
         rows_half = (own_rows + assembled[:piv_dev]).astype(jnp.bfloat16)
         g_share = pivot_inverse[band_start : band_start + span_rows]
-        pivot_part = lax.psum(
-            jnp.dot(g_share, rows_half, preferred_element_type=jnp.float32).astype(jnp.bfloat16),
-            "front",
-        ).astype(jnp.float32)
+        pivot_part = front_sum(
+            jnp.dot(g_share, rows_half, preferred_element_type=jnp.float32)
+        )
         pivot_half = pivot_part.astype(jnp.bfloat16)
         saved_part.append(pivot_part)
         saved_half.append(pivot_half)
@@ -134,12 +143,9 @@
         pivot_part = saved_part[height - 1]
         if height < levels:
             c_share = coupling[:, band_start : band_start + span_rows]
-            back_total = lax.psum(
-                jnp.einsum(
-                    "up,ur->pr", c_share, from_above, preferred_element_type=jnp.float32
-                ).astype(jnp.bfloat16),
-                "front",
-            ).astype(jnp.float32)
+            back_total = front_sum(
+                jnp.einsum("up,ur->pr", c_share, from_above, preferred_element_type=jnp.float32)
+            )
             weight_half = (pivot_part - back_total).astype(jnp.bfloat16)
             upper_rows = from_above
         else:

time: 1100 us -> 760 us (0.69)
  waiting for transfers between devices: 799 us -> 448 us
  blocking collectives: 95 us -> 71.6 us
  starting transfers between devices: 105 us -> 124 us
  other arithmetic: 13.8 us -> 25.6 us
    psum x9 -> x0, waiting for transfers between devices: 575 us -> none  [the longest x5 324 us: per_device(): lax.psum(jnp.dot(g_share, rows_half, preferred_element_type=jnp.float32)....]
    ppermute x45 -> x72, waiting for transfers between devices: 128 us -> 352 us  [partner(): return lax.ppermute(block, axis, route)]
    all_to_all x4, blocking collectives: 95 us -> 71.6 us  [per_device(): lax.all_to_all(outgoing, 'front', split_axis=0, concat_axis=0, tiled=True)]
    ppermute x45 -> x72, starting transfers between devices: 96.3 us -> 118 us  [partner(): return lax.ppermute(block, axis, route)]
  transfers between devices with their start and end apart: 60 -> 78, of which waited for: 60 -> 76; matrix products, arithmetic and copies ran while one was open for 1% -> 3% of each run, Pallas kernels for 0% -> 0%
where the time goes in v1:
time: 760 us; the launch traced here: 750 us
  waiting for transfers between devices  448 us (59%)
  starting transfers between devices  124 us (16%)
  blocking collectives  71.6 us (9%)
  local copies, waits for them, and re-layouts  38.9 us (5%)
  matrix products  26.5 us (3%)
  other arithmetic  25.6 us (3%)
  between operations  15.4 us (2%)
    ppermute x72, waiting for transfers between devices, partner(): return lax.ppermute(block, axis, route)  352 us
    ppermute x72, starting transfers between devices, partner(): return lax.ppermute(block, axis, route)  118 us
    all_gather x5, waiting for transfers between devices, per_device(): lax.all_gather(jnp.stack([carried, sibling]), 'front', axis=1, tiled=True)  90.4 us
    all_to_all x4, blocking collectives, per_device(): lax.all_to_all(outgoing, 'front', split_axis=0, concat_axis=0, tiled=True)  71.6 us
  transfers between devices with their start and end apart: 78, of which 76 were waited for; matrix products, arithmetic and copies ran while one was open for 3% of the time, Pallas kernels for 0%

profile of v1, /device:TPU:1, one launch (start us, length us, event | category | flops | bytes accessed | tf_op | source)
XLA Modules:
  0.0 750.0 jit_solution(16977858934660072619)
XLA Ops:
  18.9 24.5 %all-gather.6.cloned.1.call-done = bf16[2,1024,256]{2,1,0:T(8,128)(2,1)} async-done(((bf16[2,128,256]{2,1,0:T(8,128)(2,1)}), bf16[2,1024,256]{2,1,0:T(8,128)(2,1)}) %all-gather.6.cloned.1.call-update) | async-done | bytes 1048592 | tf_op jit(solution)/shard_map/all_gather | solution.py:110
  51.7 24.4 %collective-permute-done.3 = bf16[2048,256]{0,1:T(8,128)(2,1)S(1)} collective-permute-done((bf16[2048,256]{0,1:T(8,128)(2,1)S(1)}, bf16[2048,256]{0,1:T(8,128)(2,1)S(1)}, u32[]{:S(2)}, u32[]{:S(2)}) %collective-permute-start.3) | collective-permute-done | bytes 1048608 | tf_op jit(solution)/shard_map/ppermute | solution.py:18
  78.0 23.8 %collective-permute-done.4 = bf16[2048,256]{0,1:T(8,128)(2,1)S(1)} collective-permute-done((bf16[2048,256]{0,1:T(8,128)(2,1)S(1)}, bf16[2048,256]{0,1:T(8,128)(2,1)S(1)}, u32[]{:S(2)}, u32[]{:S(2)}) %collective-permute-start.4) | collective-permute-done | bytes 1048608 | tf_op jit(solution)/shard_map/ppermute | solution.py:18
  121.7 20.2 %all-gather.8.cloned.1.call-done = bf16[2,1024,256]{1,2,0:T(8,128)(2,1)} async-done(((bf16[2,128,256]{1,2,0:T(8,128)(2,1)}), bf16[2,1024,256]{1,2,0:T(8,128)(2,1)}) %all-gather.8.cloned.1.call-update) | async-done | bytes 1048592 | tf_op jit(solution)/shard_map/all_gather | solution.py:110
  149.8 12.6 %collective-permute-done.10 = bf16[1024,256]{0,1:T(8,128)(2,1)S(1)} collective-permute-done((bf16[1024,256]{0,1:T(8,128)(2,1)S(1)}, bf16[1024,256]{0,1:T(8,128)(2,1)S(1)}, u32[]{:S(2)}, u32[]{:S(2)}) %collective-permute-start.10) | collective-permute-done | bytes 524320 | tf_op jit(solution)/shard_map/ppermute | solution.py:18
  165.1 11.4 %collective-permute-done.11 = bf16[1024,256]{0,1:T(8,128)(2,1)S(1)} collective-permute-done((bf16[1024,256]{0,1:T(8,128)(2,1)S(1)}, bf16[1024,256]{0,1:T(8,128)(2,1)S(1)}, u32[]{:S(2)}, u32[]{:S(2)}) %collective-permute-start.11) | collective-permute-done | bytes 524320 | tf_op jit(solution)/shard_map/ppermute | solution.py:18
  203.7 19.2 %all-gather.10.cloned.1.call-done = bf16[2,1024,256]{1,2,0:T(8,128)(2,1)} async-done(((bf16[2,128,256]{1,2,0:T(8,128)(2,1)}), bf16[2,1024,256]{1,2,0:T(8,128)(2,1)}) %all-gather.10.cloned.1.call-update) | async-done | bytes 1048592 | tf_op jit(solution)/shard_map/all_gather | solution.py:110
  232.7 6.9 collective-permute-done.19
  242.2 5.8 collective-permute-done.20
  285.7 15.7 %all-gather.12.cloned.1.call-done = bf16[2,1024,256]{1,2,0:T(8,128)(2,1)} async-done(((bf16[2,128,256]{1,2,0:T(8,128)(2,1)}), bf16[2,1024,256]{1,2,0:T(8,128)(2,1)}) %all-gather.12.cloned.1.call-update) | async-done | bytes 1048592 | tf_op jit(solution)/shard_map/all_gather | solution.py:110
  340.1 6.2 collective-permute-start.41
  372.6 10.8 %all-gather.14.cloned.1.call-done = bf16[2,1024,256]{1,2,0:T(8,128)(2,1)} async-done(((bf16[2,128,256]{1,2,0:T(8,128)(2,1)}), bf16[2,1024,256]{1,2,0:T(8,128)(2,1)}) %all-gather.14.cloned.1.call-update) | async-done | bytes 1048592 | tf_op jit(solution)/shard_map/all_gather | solution.py:110
  409.7 5.5 collective-permute-done.46
  423.4 6.6 collective-permute-done.48
  430.1 5.8 collective-permute-start.49
  435.9 7.3 collective-permute-done.49
  445.2 26.8 %all_to_all.25 = bf16[8,128,256]{2,1,0:T(8,128)(2,1)S(1)} all-to-all(bf16[8,128,256]{2,1,0:T(8,128)(2,1)S(1)} %copy.50), channel_id=1, replica_groups=mesh['leaf'=32,'front'=8] {'front'}, dimensions={0} | all-to-all | bytes 1048576 | tf_op jit(solution)/shard_map/all_to_all | solution.py:173
  494.4 5.6 collective-permute-done.54
  508.5 11.3 %collective-permute-done.56 = bf16[512,256]{0,1:T(8,128)(2,1)} collective-permute-done((bf16[512,256]{0,1:T(8,128)(2,1)}, bf16[512,256]{0,1:T(8,128)(2,1)}, u32[]{:S(2)}, u32[]{:S(2)}) %collective-permute-start.56) | collective-permute-done | bytes 262176 | tf_op jit(solution)/shard_map/ppermute | solution.py:18
  522.9 14.7 %all_to_all.26 = bf16[8,128,256]{2,1,0:T(8,128)(2,1)} all-to-all(bf16[8,128,256]{2,1,0:T(8,128)(2,1)S(1)} %copy.54), channel_id=1, replica_groups=mesh['leaf'=32,'front'=8] {'front'}, dimensions={0} | all-to-all | bytes 1048576 | tf_op jit(solution)/shard_map/all_to_all | solution.py:173
  541.8 7.2 collective-permute-done.58
  550.0 7.3 collective-permute-done.59
  568.7 5.6 collective-permute-done.61
  576.0 5.4 collective-permute-done.62
  584.4 15.5 %all_to_all.27 = bf16[8,128,256]{2,1,0:T(8,128)(2,1)S(1)} all-to-all(bf16[8,128,256]{2,1,0:T(8,128)(2,1)S(1)} %copy.58), channel_id=1, replica_groups=mesh['leaf'=32,'front'=8] {'front'}, dimensions={0} | all-to-all | bytes 1048576 | tf_op jit(solution)/shard_map/all_to_all | solution.py:173
  603.5 12.8 %collective-permute-done.64 = bf16[1024,256]{0,1:T(8,128)(2,1)S(1)} collective-permute-done((bf16[1024,256]{0,1:T(8,128)(2,1)S(1)}, bf16[1024,256]{0,1:T(8,128)(2,1)S(1)}, u32[]{:S(2)}, u32[]{:S(2)}) %collective-permute-start.64) | collective-permute-done | bytes 524320 | tf_op jit(solution)/shard_map/ppermute | solution.py:18
  617.5 12.9 %collective-permute-done.65 = bf16[1024,256]{0,1:T(8,128)(2,1)S(1)} collective-permute-done((bf16[1024,256]{0,1:T(8,128)(2,1)S(1)}, bf16[1024,256]{0,1:T(8,128)(2,1)S(1)}, u32[]{:S(2)}, u32[]{:S(2)}) %collective-permute-start.65) | collective-permute-done | bytes 524320 | tf_op jit(solution)/shard_map/ppermute | solution.py:18
  641.7 5.5 collective-permute-done.67
  649.2 14.6 %all_to_all.28 = bf16[8,128,256]{2,1,0:T(8,128)(2,1)S(1)} all-to-all(bf16[8,128,256]{2,1,0:T(8,128)(2,1)S(1)} %copy.62), channel_id=1, replica_groups=mesh['leaf'=32,'front'=8] {'front'}, dimensions={0} | all-to-all | bytes 1048576 | tf_op jit(solution)/shard_map/all_to_all | solution.py:173
  668.5 24.1 %collective-permute-done.69 = bf16[2048,256]{0,1:T(8,128)(2,1)S(1)} collective-permute-done((bf16[2048,256]{0,1:T(8,128)(2,1)S(1)}, bf16[2048,256]{0,1:T(8,128)(2,1)S(1)}, u32[]{:S(2)}, u32[]{:S(2)}) %collective-permute-start.69) | collective-permute-done | bytes 1048608 | tf_op jit(solution)/shard_map/ppermute | solution.py:18
  693.9 24.1 %collective-permute-done.70 = bf16[2048,256]{0,1:T(8,128)(2,1)S(1)} collective-permute-done((bf16[2048,256]{0,1:T(8,128)(2,1)S(1)}, bf16[2048,256]{0,1:T(8,128)(2,1)S(1)}, u32[]{:S(2)}, u32[]{:S(2)}) %collective-permute-start.70) | collective-permute-done | bytes 1048608 | tf_op jit(solution)/shard_map/ppermute | solution.py:18
  726.6 6.3 all-to-all-start.4
  (390 shorter events, 328.2 us)
Async XLA Ops:
  7.2 36.2 %all-gather.6.cloned.1.call-start = ((), (), s32[]{:S(2)}) async-start(), calls=%async_computation.5 | async-start | bytes 1179648 | tf_op jit(solution)/shard_map/all_gather | solution.py:110
  12.8 129.1 %all-gather.8.cloned.1.call-start = ((), (), s32[]{:S(2)}) async-start(), calls=%async_computation.6 | async-start | bytes 1179648 | tf_op jit(solution)/shard_map/all_gather | solution.py:110
  51.6 24.5 %collective-permute-start.3 = (bf16[2048,256]{0,1:T(8,128)(2,1)S(1)}, bf16[2048,256]{0,1:T(8,128)(2,1)S(1)}, u32[]{:S(2)}, u32[]{:S(2)}) collective-permute-start(bf16[2048,256]{0,1:T(8,128)(2,1)S(1)} %add_convert_fusion.3), channel_id=1, source_target_pairs={{0,2},{2,0},{1,3},{3,1},{4,6},{6,4},{5,7},{7,5},{8,10},{10,8},{9,1... | collective-permute-start | bytes 3145736 | tf_op jit(solution)/shard_map/ppermute | solution.py:18
  76.6 25.2 %collective-permute-start.4 = (bf16[2048,256]{0,1:T(8,128)(2,1)S(1)}, bf16[2048,256]{0,1:T(8,128)(2,1)S(1)}, u32[]{:S(2)}, u32[]{:S(2)}) collective-permute-start(bf16[2048,256]{0,1:T(8,128)(2,1)S(1)} %add_convert_fusion.2), channel_id=1, source_target_pairs={{0,4},{4,0},{1,5},{5,1},{2,6},{6,2},{3,7},{7,3},{8,12},{12,8},{9,1... | collective-permute-start | bytes 3145736 | tf_op jit(solution)/shard_map/ppermute | solution.py:18
  111.9 111.0 %all-gather.10.cloned.1.call-start = ((), (), s32[]{:S(2)}) async-start(), calls=%async_computation.7 | async-start | bytes 1179648 | tf_op jit(solution)/shard_map/all_gather | solution.py:110
  148.9 13.5 %collective-permute-start.10 = (bf16[1024,256]{0,1:T(8,128)(2,1)S(1)}, bf16[1024,256]{0,1:T(8,128)(2,1)S(1)}, u32[]{:S(2)}, u32[]{:S(2)}) collective-permute-start(bf16[1024,256]{0,1:T(8,128)(2,1)S(1)} %add_convert_fusion.7), channel_id=1, source_target_pairs={{0,2},{2,0},{1,3},{3,1},{4,6},{6,4},{5,7},{7,5},{8,10},{10,8},{9,1... | collective-permute-start | bytes 1572872 | tf_op jit(solution)/shard_map/ppermute | solution.py:18
  162.6 13.9 %collective-permute-start.11 = (bf16[1024,256]{0,1:T(8,128)(2,1)S(1)}, bf16[1024,256]{0,1:T(8,128)(2,1)S(1)}, u32[]{:S(2)}, u32[]{:S(2)}) collective-permute-start(bf16[1024,256]{0,1:T(8,128)(2,1)S(1)} %add_convert_fusion.6), channel_id=1, source_target_pairs={{0,4},{4,0},{1,5},{5,1},{2,6},{6,2},{3,7},{7,3},{8,12},{12,8},{9,1... | collective-permute-start | bytes 1572872 | tf_op jit(solution)/shard_map/ppermute | solution.py:18
  191.1 110.3 %all-gather.12.cloned.1.call-start = ((), (), s32[]{:S(2)}) async-start(), calls=%async_computation.8 | async-start | bytes 1179648 | tf_op jit(solution)/shard_map/all_gather | solution.py:110
  232.0 7.7 %collective-permute-start.19 = (bf16[512,256]{0,1:T(8,128)(2,1)S(1)}, bf16[512,256]{0,1:T(8,128)(2,1)S(1)}, u32[]{:S(2)}, u32[]{:S(2)}) collective-permute-start(bf16[512,256]{0,1:T(8,128)(2,1)S(1)} %add_convert_fusion.11), channel_id=1, source_target_pairs={{0,2},{2,0},{1,3},{3,1},{4,6},{6,4},{5,7},{7,5},{8,10},{10,8},{9,1... | collective-permute-start | bytes 786440 | tf_op jit(solution)/shard_map/ppermute | solution.py:18
  239.7 8.3 %collective-permute-start.20 = (bf16[512,256]{0,1:T(8,128)(2,1)S(1)}, bf16[512,256]{0,1:T(8,128)(2,1)S(1)}, u32[]{:S(2)}, u32[]{:S(2)}) collective-permute-start(bf16[512,256]{0,1:T(8,128)(2,1)S(1)} %add_convert_fusion.10), channel_id=1, source_target_pairs={{0,4},{4,0},{1,5},{5,1},{2,6},{6,2},{3,7},{7,3},{8,12},{12,8},{9,1... | collective-permute-start | bytes 786440 | tf_op jit(solution)/shard_map/ppermute | solution.py:18
  267.6 115.7 %all-gather.14.cloned.1.call-start = ((), (), s32[]{:S(2)}) async-start(), calls=%async_computation.9 | async-start | bytes 1179648 | tf_op jit(solution)/shard_map/all_gather | solution.py:110
  279.6 6.1 collective-permute-start.24
  340.1 8.6 %collective-permute-start.41 = (bf16[128,256]{0,1:T(8,128)(2,1)S(1)}, bf16[128,256]{0,1:T(8,128)(2,1)S(1)}, u32[]{:S(2)}, u32[]{:S(2)}) collective-permute-start(bf16[128,256]{0,1:T(8,128)(2,1)S(1)} %subtract_convert_fusion.8), channel_id=1, source_target_pairs={{0,128},{128,0},{8,136},{136,8},{16,144},{144,16},{24,152},{152,24... | collective-permute-start | bytes 196616 | tf_op jit(solution)/shard_map/ppermute | solution.py:18
  364.6 8.0 %collective-permute-start.36 = (bf16[256,256]{1,0:T(8,128)(2,1)S(1)}, bf16[256,256]{1,0:T(8,128)(2,1)S(1)}, u32[]{:S(2)}, u32[]{:S(2)}) collective-permute-start(bf16[256,256]{1,0:T(8,128)(2,1)S(1)} %get-tuple-element.30), channel_id=1, source_target_pairs={{0,128},{128,0},{8,136},{136,8},{16,144},{144,16},{24,152},{152,24... | collective-permute-start | bytes 393224 | tf_op jit(solution)/shard_map/ppermute | solution.py:18
  407.5 7.7 %collective-permute-start.46 = (bf16[512,256]{0,1:T(8,128)(2,1)S(1)}, bf16[512,256]{0,1:T(8,128)(2,1)S(1)}, u32[]{:S(2)}, u32[]{:S(2)}) collective-permute-start(bf16[512,256]{0,1:T(8,128)(2,1)S(1)} %fusion.36), channel_id=1, source_target_pairs={{0,16},{16,0},{8,24},{24,8},{32,48},{48,32},{40,56},{56,40},{64,80... | collective-permute-start | bytes 786440 | tf_op jit(solution)/shard_map/ppermute | solution.py:18
  420.7 9.3 %collective-permute-start.48 = (bf16[512,256]{0,1:T(8,128)(2,1)S(1)}, bf16[512,256]{0,1:T(8,128)(2,1)S(1)}, u32[]{:S(2)}, u32[]{:S(2)}) collective-permute-start(bf16[512,256]{0,1:T(8,128)(2,1)S(1)} %fusion.37), channel_id=1, source_target_pairs={{0,64},{64,0},{8,72},{72,8},{16,80},{80,16},{24,88},{88,24},{32,96... | collective-permute-start | bytes 786440 | tf_op jit(solution)/shard_map/ppermute | solution.py:18
  430.1 13.1 %collective-permute-start.49 = (bf16[512,256]{0,1:T(8,128)(2,1)S(1)}, bf16[512,256]{0,1:T(8,128)(2,1)S(1)}, u32[]{:S(2)}, u32[]{:S(2)}) collective-permute-start(bf16[512,256]{0,1:T(8,128)(2,1)S(1)} %fusion.58), channel_id=1, source_target_pairs={{0,128},{128,0},{8,136},{136,8},{16,144},{144,16},{24,152},{152,24... | collective-permute-start | bytes 786440 | tf_op jit(solution)/shard_map/ppermute | solution.py:18
  491.3 8.7 %collective-permute-start.54 = (bf16[512,256]{0,1:T(8,128)(2,1)S(1)}, bf16[512,256]{0,1:T(8,128)(2,1)S(1)}, u32[]{:S(2)}, u32[]{:S(2)}) collective-permute-start(bf16[512,256]{0,1:T(8,128)(2,1)S(1)} %fusion.38), channel_id=1, source_target_pairs={{0,16},{16,0},{8,24},{24,8},{32,48},{48,32},{40,56},{56,40},{64,80... | collective-permute-start | bytes 786440 | tf_op jit(solution)/shard_map/ppermute | solution.py:18
  506.3 13.5 %collective-permute-start.56 = (bf16[512,256]{0,1:T(8,128)(2,1)}, bf16[512,256]{0,1:T(8,128)(2,1)}, u32[]{:S(2)}, u32[]{:S(2)}) collective-permute-start(bf16[512,256]{0,1:T(8,128)(2,1)} %fusion.39), channel_id=1, source_target_pairs={{0,64},{64,0},{8,72},{72,8},{16,80},{80,16},{24,88},{88,24},{32,96... | collective-permute-start | bytes 786440 | tf_op jit(solution)/shard_map/ppermute | solution.py:18
  541.4 7.6 %collective-permute-start.58 = (bf16[512,256]{0,1:T(8,128)(2,1)S(1)}, bf16[512,256]{0,1:T(8,128)(2,1)S(1)}, u32[]{:S(2)}, u32[]{:S(2)}) collective-permute-start(bf16[512,256]{0,1:T(8,128)(2,1)S(1)} %add_convert_fusion.9), channel_id=1, source_target_pairs={{0,2},{2,0},{1,3},{3,1},{4,6},{6,4},{5,7},{7,5},{8,10},{10,8},{9,1... | collective-permute-start | bytes 786440 | tf_op jit(solution)/shard_map/ppermute | solution.py:18
  549.1 8.2 %collective-permute-start.59 = (bf16[512,256]{0,1:T(8,128)(2,1)S(1)}, bf16[512,256]{0,1:T(8,128)(2,1)S(1)}, u32[]{:S(2)}, u32[]{:S(2)}) collective-permute-start(bf16[512,256]{0,1:T(8,128)(2,1)S(1)} %add_convert_fusion.8), channel_id=1, source_target_pairs={{0,4},{4,0},{1,5},{5,1},{2,6},{6,2},{3,7},{7,3},{8,12},{12,8},{9,1... | collective-permute-start | bytes 786440 | tf_op jit(solution)/shard_map/ppermute | solution.py:18
  558.7 5.9 collective-permute-start.60
  564.7 9.7 %collective-permute-start.61 = (bf16[512,256]{0,1:T(8,128)(2,1)S(1)}, bf16[512,256]{0,1:T(8,128)(2,1)S(1)}, u32[]{:S(2)}, u32[]{:S(2)}) collective-permute-start(bf16[512,256]{0,1:T(8,128)(2,1)S(1)} %fusion.40), channel_id=1, source_target_pairs={{0,16},{16,0},{8,24},{24,8},{32,48},{48,32},{40,56},{56,40},{64,80... | collective-permute-start | bytes 786440 | tf_op jit(solution)/shard_map/ppermute | solution.py:18
  575.9 5.5 collective-permute-start.62
  603.2 13.2 %collective-permute-start.64 = (bf16[1024,256]{0,1:T(8,128)(2,1)S(1)}, bf16[1024,256]{0,1:T(8,128)(2,1)S(1)}, u32[]{:S(2)}, u32[]{:S(2)}) collective-permute-start(bf16[1024,256]{0,1:T(8,128)(2,1)S(1)} %add_convert_fusion.5), channel_id=1, source_target_pairs={{0,2},{2,0},{1,3},{3,1},{4,6},{6,4},{5,7},{7,5},{8,10},{10,8},{9,1... | collective-permute-start | bytes 1572872 | tf_op jit(solution)/shard_map/ppermute | solution.py:18
  616.6 13.8 %collective-permute-start.65 = (bf16[1024,256]{0,1:T(8,128)(2,1)S(1)}, bf16[1024,256]{0,1:T(8,128)(2,1)S(1)}, u32[]{:S(2)}, u32[]{:S(2)}) collective-permute-start(bf16[1024,256]{0,1:T(8,128)(2,1)S(1)} %add_convert_fusion.4), channel_id=1, source_target_pairs={{0,4},{4,0},{1,5},{5,1},{2,6},{6,2},{3,7},{7,3},{8,12},{12,8},{9,1... | collective-permute-start | bytes 1572872 | tf_op jit(solution)/shard_map/ppermute | solution.py:18
  632.1 5.9 collective-permute-start.66
  638.0 9.2 %collective-permute-start.67 = (bf16[512,256]{0,1:T(8,128)(2,1)S(1)}, bf16[512,256]{0,1:T(8,128)(2,1)S(1)}, u32[]{:S(2)}, u32[]{:S(2)}) collective-permute-start(bf16[512,256]{0,1:T(8,128)(2,1)S(1)} %fusion.41), channel_id=1, source_target_pairs={{0,16},{16,0},{8,24},{24,8},{32,48},{48,32},{40,56},{56,40},{64,80... | collective-permute-start | bytes 786440 | tf_op jit(solution)/shard_map/ppermute | solution.py:18
  668.1 24.4 %collective-permute-start.69 = (bf16[2048,256]{0,1:T(8,128)(2,1)S(1)}, bf16[2048,256]{0,1:T(8,128)(2,1)S(1)}, u32[]{:S(2)}, u32[]{:S(2)}) collective-permute-start(bf16[2048,256]{0,1:T(8,128)(2,1)S(1)} %add_convert_fusion.1), channel_id=1, source_target_pairs={{0,2},{2,0},{1,3},{3,1},{4,6},{6,4},{5,7},{7,5},{8,10},{10,8},{9,1... | collective-permute-start | bytes 3145736 | tf_op jit(solution)/shard_map/ppermute | solution.py:18
  692.9 25.1 %collective-permute-start.70 = (bf16[2048,256]{0,1:T(8,128)(2,1)S(1)}, bf16[2048,256]{0,1:T(8,128)(2,1)S(1)}, u32[]{:S(2)}, u32[]{:S(2)}) collective-permute-start(bf16[2048,256]{0,1:T(8,128)(2,1)S(1)} %add_convert_fusion), channel_id=1, source_target_pairs={{0,4},{4,0},{1,5},{5,1},{2,6},{6,2},{3,7},{7,3},{8,12},{12,8},{9,1... | collective-permute-start | bytes 3145736 | tf_op jit(solution)/shard_map/ppermute | solution.py:18
  718.8 5.9 collective-permute-start.71
  726.6 15.7 %all-to-all-start.4 = ((bf16[8,128,256]{2,1,0:T(8,128)(2,1)}), bf16[8,128,256]{2,1,0:T(8,128)(2,1)S(1)}, u32[]{:S(2)}, u32[]{:S(2)}) async-start(bf16[8,128,256]{2,1,0:T(8,128)(2,1)} %copy.66), calls=%async_computation.4 | async-start | bytes 1048576 | tf_op jit(solution)/shard_map/all_to_all | solution.py:173
  (80 other events, 1109.9 us)
Sparse Core Ops, SparseCore 0:
  12.9 30.4 all-gather.5
  112.1 29.8 all-gather.7
  191.3 31.6 all-gather.9
  267.7 33.6 all-gather.11
  349.4 33.8 all-gather.13

commit v2 on v1

--- a/solution.py
+++ b/solution.py
@@ -68,12 +68,46 @@
 
 def front_sum(summand):
     bits = lax.axis_size("front").bit_length() - 1
+    if summand.shape[0] < 1024:
+        for bit_index in range(bits):
+            half = summand.astype(jnp.bfloat16)
+            summand = half.astype(jnp.float32) + partner(half, "front", bit_index).astype(
+                jnp.float32
+            )
+        return summand
+    column = lax.axis_index("front")
     for bit_index in range(bits):
-        half = summand.astype(jnp.bfloat16)
-        summand = half.astype(jnp.float32) + partner(half, "front", bit_index).astype(
+        half_rows = summand.shape[0] // 2
+        upper = column >> bit_index & 1
+        keep = lax.dynamic_slice_in_dim(summand, upper * half_rows, half_rows, 0)
+        send = lax.dynamic_slice_in_dim(summand, (1 - upper) * half_rows, half_rows, 0)
+        summand = keep + partner(send.astype(jnp.bfloat16), "front", bit_index).astype(
             jnp.float32
         )
-    return summand
+    summand = summand.astype(jnp.bfloat16)
+    for bit_index in reversed(range(bits)):
+        summand = joined(column, bit_index, summand, partner(summand, "front", bit_index))
+    return summand.astype(jnp.float32)
+
+
+def gather_all_own(upper_rhs, levels, position, piv_dev):
+    pieces = {}
+    for height in range(1, levels + 1):
+        rhs_len = piv_dev // 2**height
+        rhs_start = piv_dev - piv_dev // 2 ** (height - 1)
+        pieces[height] = upper_rhs[rhs_start : rhs_start + rhs_len]
+    for bit_index in range(levels):
+        active = [height for height in range(bit_index + 1, levels + 1)]
+        sent = jnp.concatenate([pieces[height] for height in active], 0)
+        received = partner(sent.astype(jnp.bfloat16), "leaf", bit_index).astype(sent.dtype)
+        offset = 0
+        for height in active:
+            count = pieces[height].shape[0]
+            pieces[height] = joined(
+                position, bit_index, pieces[height], received[offset : offset + count]
+            )
+            offset += count
+    return pieces
 
 
 def per_device(section_updates, upper_rhs, pivot_inverse, coupling, extend_lists):
@@ -96,6 +130,7 @@
     )
     local_count = piv_blocks + upd_blocks
     carried = section_updates
+    own_pieces = gather_all_own(upper_rhs, levels, position, piv_dev)
     saved_part = []
     saved_half = []
     for height in range(1, levels + 1):
@@ -119,7 +154,7 @@
             pair_blocks.reshape(2 * block_count, BLK * rhs_width),
             preferred_element_type=jnp.float32,
         ).reshape(local_count * BLK, rhs_width)
-        own_rows = gather_own(upper_rhs[rhs_start : rhs_start + rhs_len], height, position)
+        own_rows = own_pieces[height]
         rows_half = (own_rows + assembled[:piv_dev]).astype(jnp.bfloat16)
         g_share = pivot_inverse[band_start : band_start + span_rows]
         pivot_part = front_sum(

time: 760 us -> 697 us (0.917)
  waiting for transfers between devices: 448 us -> 390 us
  starting transfers between devices: 124 us -> 139 us
  other arithmetic: 25.6 us -> 17.8 us
    ppermute x72 -> x74, waiting for transfers between devices: 352 us -> 262 us  [partner(): return lax.ppermute(block, axis, route)]
    all_gather x5, waiting for transfers between devices: 90.4 us -> 121 us  [per_device(): lax.all_gather(jnp.stack([carried, sibling]), 'front', axis=1, tiled=True)]
    ppermute x72 -> x74, starting transfers between devices: 118 us -> 134 us  [partner(): return lax.ppermute(block, axis, route)]
  transfers between devices with their start and end apart: 78 -> 80, of which waited for: 76 -> 80; matrix products, arithmetic and copies ran while one was open for 3% -> 3% of each run, Pallas kernels for 0% -> 0%
where the time goes in v2:
time: 697 us; the launch traced here: 687 us
  waiting for transfers between devices  390 us (56%)
  starting transfers between devices  139 us (20%)
  blocking collectives  69 us (10%)
  local copies, waits for them, and re-layouts  32.6 us (5%)
  matrix products  23.2 us (3%)
  other arithmetic  17.8 us (3%)
  between operations  15.8 us (2%)
    ppermute x74, waiting for transfers between devices, partner(): return lax.ppermute(block, axis, route)  262 us
    ppermute x74, starting transfers between devices, partner(): return lax.ppermute(block, axis, route)  134 us
    all_gather x5, waiting for transfers between devices, per_device(): lax.all_gather(jnp.stack([carried, sibling]), 'front', axis=1, tiled=True)  121 us
    all_to_all x4, blocking collectives, per_device(): lax.all_to_all(outgoing, 'front', split_axis=0, concat_axis=0, tiled=True)  69 us
  transfers between devices with their start and end apart: 80, of which 80 were waited for; matrix products, arithmetic and copies ran while one was open for 3% of the time, Pallas kernels for 0%

profile of v2, /device:TPU:1, one launch (start us, length us, event | category | flops | bytes accessed | tf_op | source)
XLA Modules:
  0.0 687.2 jit_solution(12780465916150519774)
XLA Ops:
  19.9 23.6 %all-gather.6.cloned.1.call-done = bf16[2,1024,256]{2,1,0:T(8,128)(2,1)} async-done(((bf16[2,128,256]{2,1,0:T(8,128)(2,1)}), bf16[2,1024,256]{2,1,0:T(8,128)(2,1)}) %all-gather.6.cloned.1.call-update) | async-done | bytes 1048592 | tf_op jit(solution)/shard_map/all_gather | solution.py:145
  52.8 7.6 %collective-permute-done.3 = bf16[512,256]{0,1:T(8,128)(2,1)S(1)} collective-permute-done((bf16[512,256]{0,1:T(8,128)(2,1)S(1)}, bf16[512,256]{0,1:T(8,128)(2,1)S(1)}, u32[]{:S(2)}, u32[]{:S(2)}) %collective-permute-start.3) | collective-permute-done | bytes 262176 | tf_op jit(solution)/shard_map/ppermute | solution.py:18
  101.5 19.3 %all-gather.8.cloned.1.call-done = bf16[2,1024,256]{1,2,0:T(8,128)(2,1)} async-done(((bf16[2,128,256]{1,2,0:T(8,128)(2,1)}), bf16[2,1024,256]{1,2,0:T(8,128)(2,1)}) %all-gather.8.cloned.1.call-update) | async-done | bytes 1048592 | tf_op jit(solution)/shard_map/all_gather | solution.py:145
  171.9 25.7 %all-gather.10.cloned.1.call-done = bf16[2,1024,256]{1,2,0:T(8,128)(2,1)} async-done(((bf16[2,128,256]{1,2,0:T(8,128)(2,1)}), bf16[2,1024,256]{1,2,0:T(8,128)(2,1)}) %all-gather.10.cloned.1.call-update) | async-done | bytes 1048592 | tf_op jit(solution)/shard_map/all_gather | solution.py:145
  204.3 6.9 %collective-permute-done.22 = bf16[512,256]{0,1:T(8,128)(2,1)S(1)} collective-permute-done((bf16[512,256]{0,1:T(8,128)(2,1)S(1)}, bf16[512,256]{0,1:T(8,128)(2,1)S(1)}, u32[]{:S(2)}, u32[]{:S(2)}) %collective-permute-start.22) | collective-permute-done | bytes 262176 | tf_op jit(solution)/shard_map/ppermute | solution.py:18
  213.8 5.9 collective-permute-done.23
  242.6 5.6 collective-permute-done.24
  249.1 25.4 %all-gather.12.cloned.1.call-done = bf16[2,1024,256]{1,2,0:T(8,128)(2,1)} async-done(((bf16[2,128,256]{1,2,0:T(8,128)(2,1)}), bf16[2,1024,256]{1,2,0:T(8,128)(2,1)}) %all-gather.12.cloned.1.call-update) | async-done | bytes 1048592 | tf_op jit(solution)/shard_map/all_gather | solution.py:145
  308.3 6.1 collective-permute-start.37
  317.1 5.5 collective-permute-start.32
  325.0 27.2 %all-gather.14.cloned.1.call-done = bf16[2,1024,256]{1,2,0:T(8,128)(2,1)} async-done(((bf16[2,128,256]{1,2,0:T(8,128)(2,1)}), bf16[2,1024,256]{1,2,0:T(8,128)(2,1)}) %all-gather.14.cloned.1.call-update) | async-done | bytes 1048592 | tf_op jit(solution)/shard_map/all_gather | solution.py:145
  374.8 5.1 collective-permute-done.42
  387.8 6.7 collective-permute-done.44
  394.6 5.5 collective-permute-start.45
  400.1 6.9 %collective-permute-done.45 = bf16[512,256]{0,1:T(8,128)(2,1)S(1)} collective-permute-done((bf16[512,256]{0,1:T(8,128)(2,1)S(1)}, bf16[512,256]{0,1:T(8,128)(2,1)S(1)}, u32[]{:S(2)}, u32[]{:S(2)}) %collective-permute-start.45) | collective-permute-done | bytes 262176 | tf_op jit(solution)/shard_map/ppermute | solution.py:18
  408.2 26.0 %all_to_all.25 = bf16[8,128,256]{2,1,0:T(8,128)(2,1)S(1)} all-to-all(bf16[8,128,256]{2,1,0:T(8,128)(2,1)S(1)} %copy.50), channel_id=1, replica_groups=mesh['leaf'=32,'front'=8] {'front'}, dimensions={0} | all-to-all | bytes 1048576 | tf_op jit(solution)/shard_map/all_to_all | solution.py:208
  459.7 5.6 collective-permute-done.50
  465.5 5.2 collective-permute-done.51
  472.0 12.5 %collective-permute-done.52 = bf16[512,256]{0,1:T(8,128)(2,1)} collective-permute-done((bf16[512,256]{0,1:T(8,128)(2,1)S(1)}, bf16[512,256]{0,1:T(8,128)(2,1)}, u32[]{:S(2)}, u32[]{:S(2)}) %collective-permute-start.52) | collective-permute-done | bytes 262176 | tf_op jit(solution)/shard_map/ppermute | solution.py:18
  487.5 14.2 %all_to_all.26 = bf16[8,128,256]{2,1,0:T(8,128)(2,1)S(1)} all-to-all(bf16[8,128,256]{2,1,0:T(8,128)(2,1)S(1)} %copy.54), channel_id=1, replica_groups=mesh['leaf'=32,'front'=8] {'front'}, dimensions={0} | all-to-all | bytes 1048576 | tf_op jit(solution)/shard_map/all_to_all | solution.py:208
  504.7 7.2 %collective-permute-done.54 = bf16[512,256]{0,1:T(8,128)(2,1)S(1)} collective-permute-done((bf16[512,256]{0,1:T(8,128)(2,1)S(1)}, bf16[512,256]{0,1:T(8,128)(2,1)S(1)}, u32[]{:S(2)}, u32[]{:S(2)}) %collective-permute-start.54) | collective-permute-done | bytes 262176 | tf_op jit(solution)/shard_map/ppermute | solution.py:18
  513.2 7.3 %collective-permute-done.55 = bf16[512,256]{0,1:T(8,128)(2,1)S(1)} collective-permute-done((bf16[512,256]{0,1:T(8,128)(2,1)S(1)}, bf16[512,256]{0,1:T(8,128)(2,1)S(1)}, u32[]{:S(2)}, u32[]{:S(2)}) %collective-permute-start.55) | collective-permute-done | bytes 262176 | tf_op jit(solution)/shard_map/ppermute | solution.py:18
  522.7 5.0 collective-permute-done.56
  532.3 5.6 collective-permute-done.57
  538.2 5.1 collective-permute-done.58
  545.3 15.5 %all_to_all.27 = bf16[8,128,256]{2,1,0:T(8,128)(2,1)S(1)} all-to-all(bf16[8,128,256]{2,1,0:T(8,128)(2,1)S(1)} %copy.58), channel_id=1, replica_groups=mesh['leaf'=32,'front'=8] {'front'}, dimensions={0} | all-to-all | bytes 1048576 | tf_op jit(solution)/shard_map/all_to_all | solution.py:208
  590.5 6.7 collective-permute-done.65
  600.9 5.6 collective-permute-done.66
  607.7 13.3 %all_to_all.28 = bf16[8,128,256]{2,1,0:T(8,128)(2,1)S(1)} all-to-all(bf16[8,128,256]{2,1,0:T(8,128)(2,1)S(1)} %copy.62), channel_id=1, replica_groups=mesh['leaf'=32,'front'=8] {'front'}, dimensions={0} | all-to-all | bytes 1048576 | tf_op jit(solution)/shard_map/all_to_all | solution.py:208
  624.9 7.2 %collective-permute-done.68 = bf16[512,256]{0,1:T(8,128)(2,1)S(1)} collective-permute-done((bf16[512,256]{0,1:T(8,128)(2,1)S(1)}, bf16[512,256]{0,1:T(8,128)(2,1)S(1)}, u32[]{:S(2)}, u32[]{:S(2)}) %collective-permute-start.68) | collective-permute-done | bytes 262176 | tf_op jit(solution)/shard_map/ppermute | solution.py:18
  656.8 6.7 collective-permute-done.73
  673.3 6.2 all-to-all-done.4
  (433 shorter events, 333.7 us)
Async XLA Ops:
  7.2 36.3 %all-gather.6.cloned.1.call-start = ((), (), s32[]{:S(2)}) async-start(), calls=%async_computation.5 | async-start | bytes 1179648 | tf_op jit(solution)/shard_map/all_gather | solution.py:145
  12.8 108.0 %all-gather.8.cloned.1.call-start = ((), (), s32[]{:S(2)}) async-start(), calls=%async_computation.6 | async-start | bytes 1179648 | tf_op jit(solution)/shard_map/all_gather | solution.py:145
  52.7 7.7 %collective-permute-start.3 = (bf16[512,256]{0,1:T(8,128)(2,1)S(1)}, bf16[512,256]{0,1:T(8,128)(2,1)S(1)}, u32[]{:S(2)}, u32[]{:S(2)}) collective-permute-start(bf16[512,256]{0,1:T(8,128)(2,1)S(1)} %dynamic-slice_convert_fusion.5), channel_id=1, source_target_pairs={{0,2},{2,0},{1,3},{3,1},{4,6},{6,4},{5,7},{7,5},{8,10},{10,8},{9,1... | collective-permute-start | bytes 786440 | tf_op jit(solution)/shard_map/ppermute | solution.py:18
  76.9 6.2 collective-permute-start.7
  92.6 105.0 %all-gather.10.cloned.1.call-start = ((), (), s32[]{:S(2)}) async-start(), calls=%async_computation.7 | async-start | bytes 1179648 | tf_op jit(solution)/shard_map/all_gather | solution.py:145
  94.1 6.6 collective-permute-start.8
  147.0 5.8 collective-permute-start.16
  166.7 107.7 %all-gather.12.cloned.1.call-start = ((), (), s32[]{:S(2)}) async-start(), calls=%async_computation.8 | async-start | bytes 1179648 | tf_op jit(solution)/shard_map/all_gather | solution.py:145
  203.5 7.7 %collective-permute-start.22 = (bf16[512,256]{0,1:T(8,128)(2,1)S(1)}, bf16[512,256]{0,1:T(8,128)(2,1)S(1)}, u32[]{:S(2)}, u32[]{:S(2)}) collective-permute-start(bf16[512,256]{0,1:T(8,128)(2,1)S(1)} %add_convert_fusion.3), channel_id=1, source_target_pairs={{0,2},{2,0},{1,3},{3,1},{4,6},{6,4},{5,7},{7,5},{8,10},{10,8},{9,1... | collective-permute-start | bytes 786440 | tf_op jit(solution)/shard_map/ppermute | solution.py:18
  211.3 8.3 %collective-permute-start.23 = (bf16[512,256]{0,1:T(8,128)(2,1)S(1)}, bf16[512,256]{0,1:T(8,128)(2,1)S(1)}, u32[]{:S(2)}, u32[]{:S(2)}) collective-permute-start(bf16[512,256]{0,1:T(8,128)(2,1)S(1)} %add_convert_fusion.2), channel_id=1, source_target_pairs={{0,4},{4,0},{1,5},{5,1},{2,6},{6,2},{3,7},{7,3},{8,12},{12,8},{9,1... | collective-permute-start | bytes 786440 | tf_op jit(solution)/shard_map/ppermute | solution.py:18
  238.1 114.1 %all-gather.14.cloned.1.call-start = ((), (), s32[]{:S(2)}) async-start(), calls=%async_computation.9 | async-start | bytes 1179648 | tf_op jit(solution)/shard_map/all_gather | solution.py:145
  239.6 8.7 %collective-permute-start.24 = (bf16[384,256]{1,0:T(8,128)(2,1)S(1)}, bf16[384,256]{1,0:T(8,128)(2,1)S(1)}, u32[]{:S(2)}, u32[]{:S(2)}) collective-permute-start(bf16[384,256]{1,0:T(8,128)(2,1)S(1)} %pad_maximum_fusion.6), channel_id=1, source_target_pairs={{0,64},{64,0},{8,72},{72,8},{16,80},{80,16},{24,88},{88,24},{32,96... | collective-permute-start | bytes 589832 | tf_op jit(solution)/shard_map/ppermute | solution.py:18
  308.3 7.8 %collective-permute-start.37 = (bf16[128,256]{0,1:T(8,128)(2,1)S(1)}, bf16[128,256]{0,1:T(8,128)(2,1)S(1)}, u32[]{:S(2)}, u32[]{:S(2)}) collective-permute-start(bf16[128,256]{0,1:T(8,128)(2,1)S(1)} %subtract_convert_fusion.8), channel_id=1, source_target_pairs={{0,128},{128,0},{8,136},{136,8},{16,144},{144,16},{24,152},{152,24... | collective-permute-start | bytes 196616 | tf_op jit(solution)/shard_map/ppermute | solution.py:18
  317.1 7.8 %collective-permute-start.32 = (bf16[256,256]{1,0:T(8,128)(2,1)S(1)}, bf16[256,256]{1,0:T(8,128)(2,1)S(1)}, u32[]{:S(2)}, u32[]{:S(2)}) collective-permute-start(bf16[256,256]{1,0:T(8,128)(2,1)S(1)} %get-tuple-element.30), channel_id=1, source_target_pairs={{0,128},{128,0},{8,136},{136,8},{16,144},{144,16},{24,152},{152,24... | collective-permute-start | bytes 393224 | tf_op jit(solution)/shard_map/ppermute | solution.py:18
  372.0 8.0 %collective-permute-start.42 = (bf16[512,256]{0,1:T(8,128)(2,1)S(1)}, bf16[512,256]{0,1:T(8,128)(2,1)S(1)}, u32[]{:S(2)}, u32[]{:S(2)}) collective-permute-start(bf16[512,256]{0,1:T(8,128)(2,1)S(1)} %fusion.45), channel_id=1, source_target_pairs={{0,16},{16,0},{8,24},{24,8},{32,48},{48,32},{40,56},{56,40},{64,80... | collective-permute-start | bytes 786440 | tf_op jit(solution)/shard_map/ppermute | solution.py:18
  385.5 9.1 %collective-permute-start.44 = (bf16[512,256]{0,1:T(8,128)(2,1)S(1)}, bf16[512,256]{0,1:T(8,128)(2,1)S(1)}, u32[]{:S(2)}, u32[]{:S(2)}) collective-permute-start(bf16[512,256]{0,1:T(8,128)(2,1)S(1)} %fusion.46), channel_id=1, source_target_pairs={{0,64},{64,0},{8,72},{72,8},{16,80},{80,16},{24,88},{88,24},{32,96... | collective-permute-start | bytes 786440 | tf_op jit(solution)/shard_map/ppermute | solution.py:18
  394.6 12.4 %collective-permute-start.45 = (bf16[512,256]{0,1:T(8,128)(2,1)S(1)}, bf16[512,256]{0,1:T(8,128)(2,1)S(1)}, u32[]{:S(2)}, u32[]{:S(2)}) collective-permute-start(bf16[512,256]{0,1:T(8,128)(2,1)S(1)} %fusion.70), channel_id=1, source_target_pairs={{0,128},{128,0},{8,136},{136,8},{16,144},{144,16},{24,152},{152,24... | collective-permute-start | bytes 786440 | tf_op jit(solution)/shard_map/ppermute | solution.py:18
  448.1 7.8 %collective-permute-start.49 = (bf16[512,256]{0,1:T(8,128)(2,1)S(1)}, bf16[512,256]{0,1:T(8,128)(2,1)S(1)}, u32[]{:S(2)}, u32[]{:S(2)}) collective-permute-start(bf16[512,256]{0,1:T(8,128)(2,1)S(1)} %get-tuple-element.73), channel_id=1, source_target_pairs={{0,8},{8,0},{16,24},{24,16},{32,40},{40,32},{48,56},{56,48},{64,72... | collective-permute-start | bytes 786440 | tf_op jit(solution)/shard_map/ppermute | solution.py:18
  456.0 9.4 %collective-permute-start.50 = (bf16[512,256]{0,1:T(8,128)(2,1)S(1)}, bf16[512,256]{0,1:T(8,128)(2,1)S(1)}, u32[]{:S(2)}, u32[]{:S(2)}) collective-permute-start(bf16[512,256]{0,1:T(8,128)(2,1)S(1)} %fusion.47), channel_id=1, source_target_pairs={{0,16},{16,0},{8,24},{24,8},{32,48},{48,32},{40,56},{56,40},{64,80... | collective-permute-start | bytes 786440 | tf_op jit(solution)/shard_map/ppermute | solution.py:18
  470.9 13.6 %collective-permute-start.52 = (bf16[512,256]{0,1:T(8,128)(2,1)S(1)}, bf16[512,256]{0,1:T(8,128)(2,1)}, u32[]{:S(2)}, u32[]{:S(2)}) collective-permute-start(bf16[512,256]{0,1:T(8,128)(2,1)S(1)} %fusion.48), channel_id=1, source_target_pairs={{0,64},{64,0},{8,72},{72,8},{16,80},{80,16},{24,88},{88,24},{32,96... | collective-permute-start | bytes 786440 | tf_op jit(solution)/shard_map/ppermute | solution.py:18
  504.4 7.6 %collective-permute-start.54 = (bf16[512,256]{0,1:T(8,128)(2,1)S(1)}, bf16[512,256]{0,1:T(8,128)(2,1)S(1)}, u32[]{:S(2)}, u32[]{:S(2)}) collective-permute-start(bf16[512,256]{0,1:T(8,128)(2,1)S(1)} %add_convert_fusion.1), channel_id=1, source_target_pairs={{0,2},{2,0},{1,3},{3,1},{4,6},{6,4},{5,7},{7,5},{8,10},{10,8},{9,1... | collective-permute-start | bytes 786440 | tf_op jit(solution)/shard_map/ppermute | solution.py:18
  512.0 8.4 %collective-permute-start.55 = (bf16[512,256]{0,1:T(8,128)(2,1)S(1)}, bf16[512,256]{0,1:T(8,128)(2,1)S(1)}, u32[]{:S(2)}, u32[]{:S(2)}) collective-permute-start(bf16[512,256]{0,1:T(8,128)(2,1)S(1)} %add_convert_fusion), channel_id=1, source_target_pairs={{0,4},{4,0},{1,5},{5,1},{2,6},{6,2},{3,7},{7,3},{8,12},{12,8},{9,1... | collective-permute-start | bytes 786440 | tf_op jit(solution)/shard_map/ppermute | solution.py:18
  521.8 5.9 collective-permute-start.56
  527.7 10.1 %collective-permute-start.57 = (bf16[512,256]{0,1:T(8,128)(2,1)S(1)}, bf16[512,256]{0,1:T(8,128)(2,1)S(1)}, u32[]{:S(2)}, u32[]{:S(2)}) collective-permute-start(bf16[512,256]{0,1:T(8,128)(2,1)S(1)} %fusion.49), channel_id=1, source_target_pairs={{0,16},{16,0},{8,24},{24,8},{32,48},{48,32},{40,56},{56,40},{64,80... | collective-permute-start | bytes 786440 | tf_op jit(solution)/shard_map/ppermute | solution.py:18
  582.0 5.9 collective-permute-start.64
  589.6 7.6 %collective-permute-start.65 = (bf16[512,256]{0,1:T(8,128)(2,1)S(1)}, bf16[512,256]{0,1:T(8,128)(2,1)S(1)}, u32[]{:S(2)}, u32[]{:S(2)}) collective-permute-start(bf16[512,256]{0,1:T(8,128)(2,1)S(1)} %get-tuple-element.77), channel_id=1, source_target_pairs={{0,8},{8,0},{16,24},{24,16},{32,40},{40,32},{48,56},{56,48},{64,72... | collective-permute-start | bytes 786440 | tf_op jit(solution)/shard_map/ppermute | solution.py:18
  597.3 9.2 %collective-permute-start.66 = (bf16[512,256]{0,1:T(8,128)(2,1)S(1)}, bf16[512,256]{0,1:T(8,128)(2,1)S(1)}, u32[]{:S(2)}, u32[]{:S(2)}) collective-permute-start(bf16[512,256]{0,1:T(8,128)(2,1)S(1)} %fusion.50), channel_id=1, source_target_pairs={{0,16},{16,0},{8,24},{24,8},{32,48},{48,32},{40,56},{56,40},{64,80... | collective-permute-start | bytes 786440 | tf_op jit(solution)/shard_map/ppermute | solution.py:18
  624.5 7.6 %collective-permute-start.68 = (bf16[512,256]{0,1:T(8,128)(2,1)S(1)}, bf16[512,256]{0,1:T(8,128)(2,1)S(1)}, u32[]{:S(2)}, u32[]{:S(2)}) collective-permute-start(bf16[512,256]{0,1:T(8,128)(2,1)S(1)} %dynamic-slice_convert_fusion.2), channel_id=1, source_target_pairs={{0,2},{2,0},{1,3},{3,1},{4,6},{6,4},{5,7},{7,5},{8,10},{10,8},{9,1... | collective-permute-start | bytes 786440 | tf_op jit(solution)/shard_map/ppermute | solution.py:18
  632.2 5.7 collective-permute-start.69
  648.9 6.3 collective-permute-start.72
  656.0 7.6 %collective-permute-start.73 = (bf16[512,256]{0,1:T(8,128)(2,1)S(1)}, bf16[512,256]{0,1:T(8,128)(2,1)S(1)}, u32[]{:S(2)}, u32[]{:S(2)}) collective-permute-start(bf16[512,256]{0,1:T(8,128)(2,1)S(1)} %get-tuple-element.79), channel_id=1, source_target_pairs={{0,8},{8,0},{16,24},{24,16},{32,40},{40,32},{48,56},{56,48},{64,72... | collective-permute-start | bytes 786440 | tf_op jit(solution)/shard_map/ppermute | solution.py:18
  665.5 14.0 %all-to-all-start.4 = ((bf16[8,128,256]{2,1,0:T(8,128)(2,1)}), bf16[8,128,256]{2,1,0:T(8,128)(2,1)S(1)}, u32[]{:S(2)}, u32[]{:S(2)}) async-start(bf16[8,128,256]{2,1,0:T(8,128)(2,1)} %copy.66), calls=%async_computation.4 | async-start | bytes 1048576 | tf_op jit(solution)/shard_map/all_to_all | solution.py:208
  (90 other events, 814.3 us)
Sparse Core Ops, SparseCore 0:
  12.9 30.4 all-gather.5
  92.7 28.0 all-gather.7
  166.8 30.7 all-gather.9
  238.2 36.2 all-gather.11
  316.9 35.2 all-gather.13

commit v3 on v2

--- a/solution.py
+++ b/solution.py
@@ -88,6 +88,39 @@
     for bit_index in reversed(range(bits)):
         summand = joined(column, bit_index, summand, partner(summand, "front", bit_index))
     return summand.astype(jnp.float32)
+
+
+def front_gather(blocks):
+    bits = lax.axis_size("front").bit_length() - 1
+    column = lax.axis_index("front")
+    for bit_index in reversed(range(bits)):
+        received = partner(blocks, "front", bit_index)
+        blocks = jnp.where(
+            upper_bit(column, bit_index),
+            jnp.concatenate([received, blocks], 1),
+            jnp.concatenate([blocks, received], 1),
+        )
+    return blocks
+
+
+def gathered_order(count):
+    bits = count.bit_length() - 1
+    return [int(format(index, f"0{bits}b")[::-1], 2) for index in range(count)]
+
+
+def front_scatter_sum(outgoing):
+    bits = lax.axis_size("front").bit_length() - 1
+    column = lax.axis_index("front")
+    rest = outgoing.shape[1:]
+    split = outgoing.reshape((2,) * bits + rest)
+    for bit_index in range(bits):
+        axis = bits - 1 - bit_index
+        mine = column >> bit_index & 1
+        keep = lax.dynamic_index_in_dim(split, mine, axis, keepdims=False)
+        send = lax.dynamic_index_in_dim(split, 1 - mine, axis, keepdims=False)
+        received = partner(send, "front", bit_index)
+        split = (keep.astype(jnp.float32) + received.astype(jnp.float32)).astype(outgoing.dtype)
+    return split
 
 
 def gather_all_own(upper_rhs, levels, position, piv_dev):
@@ -142,10 +175,10 @@
         member = position & group_size - 1
         own_child = child_base(leaves, height) + (position >> height - 1)
         sibling = partner(carried, "leaf", height - 1)
-        pair_blocks = lax.all_gather(jnp.stack([carried, sibling]), "front", axis=1, tiled=True)
+        pair_blocks = front_gather(jnp.stack([carried, sibling]))
         pair_lists = jnp.stack(
             [list_row(extend_lists, own_child), list_row(extend_lists, own_child ^ 1)]
-        )
+        )[:, jnp.array(gathered_order(fronts), jnp.int32)]
         chooser = (pair_lists.reshape(2 * block_count)[None, :] == local_blocks[:, None]).astype(
             jnp.bfloat16
         )
@@ -205,8 +238,7 @@
             .astype(jnp.bfloat16)
             .reshape(fronts, upd_dev, rhs_width)
         )
-        incoming = lax.all_to_all(outgoing, "front", split_axis=0, concat_axis=0, tiled=True)
-        from_above = jnp.sum(incoming, axis=0, dtype=jnp.float32).astype(jnp.bfloat16)
+        from_above = front_scatter_sum(outgoing)
     solution = jnp.concatenate(outputs[::-1], 0)
     return (solution, from_above)
 

time: 697 us -> 659 us (0.945)
  starting transfers between devices: 139 us -> 212 us
  blocking collectives: 69 us -> 0 us
  waiting for transfers between devices: 390 us -> 365 us
  between operations: 15.8 us -> 2.95 us
    all_gather x5 -> x0, waiting for transfers between devices: 121 us -> none  [per_device(): lax.all_gather(jnp.stack([carried, sibling]), 'front', axis=1, tiled=True)]
    ppermute x74 -> x104, waiting for transfers between devices: 262 us -> 365 us  [partner(): return lax.ppermute(block, axis, route)]
    ppermute x74 -> x104, starting transfers between devices: 134 us -> 212 us  [partner(): return lax.ppermute(block, axis, route)]
    all_to_all x4 -> x0, blocking collectives: 69 us -> none  [per_device(): lax.all_to_all(outgoing, 'front', split_axis=0, concat_axis=0, tiled=True)]
  transfers between devices with their start and end apart: 80 -> 104, of which waited for: 80 -> 98; matrix products, arithmetic and copies ran while one was open for 3% -> 3% of each run, Pallas kernels for 0% -> 0%
where the time goes in v3:
time: 659 us; the launch traced here: 649 us
  waiting for transfers between devices  365 us (55%)
  starting transfers between devices  212 us (32%)
  local copies, waits for them, and re-layouts  28.4 us (4%)
  matrix products  23.2 us (4%)
  other arithmetic  17.8 us (3%)
    ppermute x104, waiting for transfers between devices, partner(): return lax.ppermute(block, axis, route)  365 us
    ppermute x104, starting transfers between devices, partner(): return lax.ppermute(block, axis, route)  212 us
  transfers between devices with their start and end apart: 104, of which 98 were waited for; matrix products, arithmetic and copies ran while one was open for 3% of the time, Pallas kernels for 0%

profile of v3, /device:TPU:1, one launch (start us, length us, event | category | flops | bytes accessed | tf_op | source)
XLA Modules:
  0.0 649.1 jit_solution(10033210547504719324)
XLA Ops:
  17.5 6.1 collective-permute-start.4
  35.3 7.7 %collective-permute-done.6 = bf16[512,256]{0,1:T(8,128)(2,1)S(1)} collective-permute-done((bf16[512,256]{0,1:T(8,128)(2,1)S(1)}, bf16[512,256]{0,1:T(8,128)(2,1)S(1)}, u32[]{:S(2)}, u32[]{:S(2)}) %collective-permute-start.6) | collective-permute-done | bytes 262176 | tf_op jit(solution)/shard_map/ppermute | solution.py:18
  94.4 6.3 collective-permute-done.11
  150.9 6.1 collective-permute-done.28
  157.2 5.2 collective-permute-start.29
  177.0 7.1 %collective-permute-done.31 = bf16[512,256]{0,1:T(8,128)(2,1)S(1)} collective-permute-done((bf16[512,256]{0,1:T(8,128)(2,1)S(1)}, bf16[512,256]{0,1:T(8,128)(2,1)S(1)}, u32[]{:S(2)}, u32[]{:S(2)}) %collective-permute-start.31) | collective-permute-done | bytes 262176 | tf_op jit(solution)/shard_map/ppermute | solution.py:18
  187.7 5.5 collective-permute-done.32
  217.3 5.2 collective-permute-done.39
  222.7 8.2 %collective-permute-start.40 = (bf16[2,512,256]{2,1,0:T(8,128)(2,1)S(1)}, bf16[2,512,256]{2,1,0:T(8,128)(2,1)S(1)}, u32[]{:S(2)}, u32[]{:S(2)}) collective-permute-start(bf16[2,512,256]{2,1,0:T(8,128)(2,1)S(1)} %maximum_select_fusion.17), channel_id=1, source_target_pairs={{0,1},{1,0},{2,3},{3,2},{4,5},{5,4},{6,7},{7,6},{8,9},{9,8},{10,11... | collective-permute-start | bytes 1572872 | tf_op jit(solution)/shard_map/ppermute | solution.py:18
  236.1 8.5 %collective-permute-done.33 = bf16[384,256]{1,0:T(8,128)(2,1)S(1)} collective-permute-done((bf16[384,256]{1,0:T(8,128)(2,1)S(1)}, bf16[384,256]{1,0:T(8,128)(2,1)S(1)}, u32[]{:S(2)}, u32[]{:S(2)}) %collective-permute-start.33) | collective-permute-done | bytes 196640 | tf_op jit(solution)/shard_map/ppermute | solution.py:18
  278.4 7.2 %collective-permute-start.49 = (bf16[128,256]{1,0:T(8,128)(2,1)S(1)}, bf16[128,256]{1,0:T(8,128)(2,1)S(1)}, u32[]{:S(2)}, u32[]{:S(2)}) collective-permute-start(bf16[128,256]{1,0:T(8,128)(2,1)S(1)} %subtract_convert_fusion.8), channel_id=1, source_target_pairs={{0,128},{128,0},{8,136},{136,8},{16,144},{144,16},{24,152},{152,24... | collective-permute-start | bytes 196616 | tf_op jit(solution)/shard_map/ppermute | solution.py:18
  298.3 10.6 %collective-permute-start.52 = (bf16[2,512,256]{2,1,0:T(8,128)(2,1)S(1)}, bf16[2,512,256]{2,1,0:T(8,128)(2,1)S(1)}, u32[]{:S(2)}, u32[]{:S(2)}) collective-permute-start(bf16[2,512,256]{2,1,0:T(8,128)(2,1)S(1)} %maximum_select_fusion.19), channel_id=1, source_target_pairs={{0,1},{1,0},{2,3},{3,2},{4,5},{5,4},{6,7},{7,6},{8,9},{9,8},{10,11... | collective-permute-start | bytes 1572872 | tf_op jit(solution)/shard_map/ppermute | solution.py:18
  310.1 5.7 collective-permute-start.44
  315.9 6.6 %collective-permute-done.44 = bf16[256,256]{1,0:T(8,128)(2,1)S(1)} collective-permute-done((bf16[256,256]{1,0:T(8,128)(2,1)S(1)}, bf16[256,256]{1,0:T(8,128)(2,1)S(1)}, u32[]{:S(2)}, u32[]{:S(2)}) %collective-permute-start.44) | collective-permute-done | bytes 131104 | tf_op jit(solution)/shard_map/ppermute | solution.py:18
  344.0 5.7 collective-permute-done.57
  350.0 5.2 collective-permute-done.58
  355.4 8.8 %collective-permute-done.59 = bf16[512,256]{0,1:T(8,128)(2,1)S(1)} collective-permute-done((bf16[512,256]{0,1:T(8,128)(2,1)S(1)}, bf16[512,256]{0,1:T(8,128)(2,1)S(1)}, u32[]{:S(2)}, u32[]{:S(2)}) %collective-permute-start.59) | collective-permute-done | bytes 262176 | tf_op jit(solution)/shard_map/ppermute | solution.py:18
  367.6 8.6 %collective-permute-done.60 = bf16[512,256]{0,1:T(8,128)(2,1)S(1)} collective-permute-done((bf16[512,256]{0,1:T(8,128)(2,1)S(1)}, bf16[512,256]{0,1:T(8,128)(2,1)S(1)}, u32[]{:S(2)}, u32[]{:S(2)}) %collective-permute-start.60) | collective-permute-done | bytes 262176 | tf_op jit(solution)/shard_map/ppermute | solution.py:18
  377.6 10.8 %collective-permute-start.61 = (bf16[2,2,128,256]{2,3,0,1:T(8,128)(2,1)S(1)}, bf16[2,2,128,256]{2,3,0,1:T(8,128)(2,1)S(1)}, u32[]{:S(2)}, u32[]{:S(2)}) collective-permute-start(bf16[2,2,128,256]{2,3,0,1:T(8,128)(2,1)S(1)} %bitcast.186), channel_id=1, source_target_pairs={{0,1},{1,0},{2,3},{3,2},{4,5},{5,4},{6,7},{7,6},{8,9},{9,8},{10,11... | collective-permute-start | bytes 786440 | tf_op jit(solution)/shard_map/ppermute | solution.py:18
  394.5 5.7 collective-permute-start.63
  428.2 5.6 collective-permute-done.68
  434.0 5.2 collective-permute-done.69
  439.9 12.7 %collective-permute-done.70 = bf16[512,256]{0,1:T(8,128)(2,1)S(1)} collective-permute-done((bf16[512,256]{0,1:T(8,128)(2,1)S(1)}, bf16[512,256]{0,1:T(8,128)(2,1)S(1)}, u32[]{:S(2)}, u32[]{:S(2)}) %collective-permute-start.70) | collective-permute-done | bytes 262176 | tf_op jit(solution)/shard_map/ppermute | solution.py:18
  472.5 6.9 %collective-permute-done.75 = bf16[512,256]{0,1:T(8,128)(2,1)S(1)} collective-permute-done((bf16[512,256]{0,1:T(8,128)(2,1)S(1)}, bf16[512,256]{0,1:T(8,128)(2,1)S(1)}, u32[]{:S(2)}, u32[]{:S(2)}) %collective-permute-start.75) | collective-permute-done | bytes 262176 | tf_op jit(solution)/shard_map/ppermute | solution.py:18
  480.8 6.9 %collective-permute-done.76 = bf16[512,256]{0,1:T(8,128)(2,1)S(1)} collective-permute-done((bf16[512,256]{0,1:T(8,128)(2,1)S(1)}, bf16[512,256]{0,1:T(8,128)(2,1)S(1)}, u32[]{:S(2)}, u32[]{:S(2)}) %collective-permute-start.76) | collective-permute-done | bytes 262176 | tf_op jit(solution)/shard_map/ppermute | solution.py:18
  500.1 5.6 collective-permute-done.78
  505.9 5.2 collective-permute-done.79
  558.2 6.6 %collective-permute-done.89 = bf16[512,256]{0,1:T(8,128)(2,1)S(1)} collective-permute-done((bf16[512,256]{0,1:T(8,128)(2,1)S(1)}, bf16[512,256]{0,1:T(8,128)(2,1)S(1)}, u32[]{:S(2)}, u32[]{:S(2)}) %collective-permute-start.89) | collective-permute-done | bytes 262176 | tf_op jit(solution)/shard_map/ppermute | solution.py:18
  568.8 5.7 collective-permute-done.90
  595.2 6.4 collective-permute-done.95
  618.1 5.3 collective-permute-start.99
  626.3 6.9 %collective-permute-done.100 = bf16[512,256]{0,1:T(8,128)(2,1)S(1)} collective-permute-done((bf16[512,256]{0,1:T(8,128)(2,1)S(1)}, bf16[512,256]{0,1:T(8,128)(2,1)S(1)}, u32[]{:S(2)}, u32[]{:S(2)}) %collective-permute-start.100) | collective-permute-done | bytes 262176 | tf_op jit(solution)/shard_map/ppermute | solution.py:18
  (546 shorter events, 426.3 us)
Async XLA Ops:
  14.5 11.6 %collective-permute-start = (bf16[496,256]{1,0:T(8,128)(2,1)S(1)}, bf16[496,256]{1,0:T(8,128)(2,1)S(1)}, u32[]{:S(2)}, u32[]{:S(2)}) collective-permute-start(bf16[496,256]{1,0:T(8,128)(2,1)S(1)} %convert_element_type.702), channel_id=1, source_target_pairs={{0,8},{8,0},{16,24},{24,16},{32,40},{40,32},{48,56},{56,48},{64,72... | collective-permute-start | bytes 761864 | tf_op jit(solution)/shard_map/ppermute | solution.py:18
  17.5 9.2 %collective-permute-start.4 = (bf16[2,512,256]{2,1,0:T(8,128)(2,1)S(1)}, bf16[2,512,256]{2,1,0:T(8,128)(2,1)S(1)}, u32[]{:S(2)}, u32[]{:S(2)}) collective-permute-start(bf16[2,512,256]{2,1,0:T(8,128)(2,1)S(1)} %maximum_select_fusion.9), channel_id=1, source_target_pairs={{0,1},{1,0},{2,3},{3,2},{4,5},{5,4},{6,7},{7,6},{8,9},{9,8},{10,11... | collective-permute-start | bytes 1572872 | tf_op jit(solution)/shard_map/ppermute | solution.py:18
  35.2 7.8 %collective-permute-start.6 = (bf16[512,256]{0,1:T(8,128)(2,1)S(1)}, bf16[512,256]{0,1:T(8,128)(2,1)S(1)}, u32[]{:S(2)}, u32[]{:S(2)}) collective-permute-start(bf16[512,256]{0,1:T(8,128)(2,1)S(1)} %dynamic-slice_convert_fusion.5), channel_id=1, source_target_pairs={{0,2},{2,0},{1,3},{3,1},{4,6},{6,4},{5,7},{7,5},{8,10},{10,8},{9,1... | collective-permute-start | bytes 786440 | tf_op jit(solution)/shard_map/ppermute | solution.py:18
  85.9 15.7 %collective-permute-start.16 = (bf16[2,512,256]{2,1,0:T(8,128)(2,1)S(1)}, bf16[2,512,256]{2,1,0:T(8,128)(2,1)S(1)}, u32[]{:S(2)}, u32[]{:S(2)}) collective-permute-start(bf16[2,512,256]{2,1,0:T(8,128)(2,1)S(1)} %maximum_select_fusion.12), channel_id=1, source_target_pairs={{0,1},{1,0},{2,3},{3,2},{4,5},{5,4},{6,7},{7,6},{8,9},{9,8},{10,11... | collective-permute-start | bytes 1572872 | tf_op jit(solution)/shard_map/ppermute | solution.py:18
  91.6 9.1 %collective-permute-start.11 = (bf16[480,256]{1,0:T(8,128)(2,1)S(1)}, bf16[480,256]{1,0:T(8,128)(2,1)S(1)}, u32[]{:S(2)}, u32[]{:S(2)}) collective-permute-start(bf16[480,256]{1,0:T(8,128)(2,1)S(1)} %pad_maximum_fusion.4), channel_id=1, source_target_pairs={{0,16},{16,0},{8,24},{24,8},{32,48},{48,32},{40,56},{56,40},{64,80... | collective-permute-start | bytes 737288 | tf_op jit(solution)/shard_map/ppermute | solution.py:18
  150.6 6.3 collective-permute-start.28
  157.2 14.0 %collective-permute-start.29 = (bf16[2,512,256]{2,1,0:T(8,128)(2,1)S(1)}, bf16[2,512,256]{2,1,0:T(8,128)(2,1)S(1)}, u32[]{:S(2)}, u32[]{:S(2)}) collective-permute-start(bf16[2,512,256]{2,1,0:T(8,128)(2,1)S(1)} %maximum_select_fusion.15), channel_id=1, source_target_pairs={{0,1},{1,0},{2,3},{3,2},{4,5},{5,4},{6,7},{7,6},{8,9},{9,8},{10,11... | collective-permute-start | bytes 1572872 | tf_op jit(solution)/shard_map/ppermute | solution.py:18
  163.8 7.4 %collective-permute-start.23 = (bf16[448,256]{1,0:T(8,128)(2,1)S(1)}, bf16[448,256]{1,0:T(8,128)(2,1)S(1)}, u32[]{:S(2)}, u32[]{:S(2)}) collective-permute-start(bf16[448,256]{1,0:T(8,128)(2,1)S(1)} %pad_maximum_fusion.5), channel_id=1, source_target_pairs={{0,32},{32,0},{8,40},{40,8},{16,48},{48,16},{24,56},{56,24},{64,96... | collective-permute-start | bytes 688136 | tf_op jit(solution)/shard_map/ppermute | solution.py:18
  176.6 7.6 %collective-permute-start.31 = (bf16[512,256]{0,1:T(8,128)(2,1)S(1)}, bf16[512,256]{0,1:T(8,128)(2,1)S(1)}, u32[]{:S(2)}, u32[]{:S(2)}) collective-permute-start(bf16[512,256]{0,1:T(8,128)(2,1)S(1)} %add_convert_fusion.3), channel_id=1, source_target_pairs={{0,2},{2,0},{1,3},{3,1},{4,6},{6,4},{5,7},{7,5},{8,10},{10,8},{9,1... | collective-permute-start | bytes 786440 | tf_op jit(solution)/shard_map/ppermute | solution.py:18
  184.2 8.9 %collective-permute-start.32 = (bf16[512,256]{0,1:T(8,128)(2,1)S(1)}, bf16[512,256]{0,1:T(8,128)(2,1)S(1)}, u32[]{:S(2)}, u32[]{:S(2)}) collective-permute-start(bf16[512,256]{0,1:T(8,128)(2,1)S(1)} %add_convert_fusion.2), channel_id=1, source_target_pairs={{0,4},{4,0},{1,5},{5,1},{2,6},{6,2},{3,7},{7,3},{8,12},{12,8},{9,1... | collective-permute-start | bytes 786440 | tf_op jit(solution)/shard_map/ppermute | solution.py:18
  222.7 22.8 %collective-permute-start.40 = (bf16[2,512,256]{2,1,0:T(8,128)(2,1)S(1)}, bf16[2,512,256]{2,1,0:T(8,128)(2,1)S(1)}, u32[]{:S(2)}, u32[]{:S(2)}) collective-permute-start(bf16[2,512,256]{2,1,0:T(8,128)(2,1)S(1)} %maximum_select_fusion.17), channel_id=1, source_target_pairs={{0,1},{1,0},{2,3},{3,2},{4,5},{5,4},{6,7},{7,6},{8,9},{9,8},{10,11... | collective-permute-start | bytes 1572872 | tf_op jit(solution)/shard_map/ppermute | solution.py:18
  232.3 12.4 %collective-permute-start.33 = (bf16[384,256]{1,0:T(8,128)(2,1)S(1)}, bf16[384,256]{1,0:T(8,128)(2,1)S(1)}, u32[]{:S(2)}, u32[]{:S(2)}) collective-permute-start(bf16[384,256]{1,0:T(8,128)(2,1)S(1)} %pad_maximum_fusion.6), channel_id=1, source_target_pairs={{0,64},{64,0},{8,72},{72,8},{16,80},{80,16},{24,88},{88,24},{32,96... | collective-permute-start | bytes 589832 | tf_op jit(solution)/shard_map/ppermute | solution.py:18
  278.4 8.8 %collective-permute-start.49 = (bf16[128,256]{1,0:T(8,128)(2,1)S(1)}, bf16[128,256]{1,0:T(8,128)(2,1)S(1)}, u32[]{:S(2)}, u32[]{:S(2)}) collective-permute-start(bf16[128,256]{1,0:T(8,128)(2,1)S(1)} %subtract_convert_fusion.8), channel_id=1, source_target_pairs={{0,128},{128,0},{8,136},{136,8},{16,144},{144,16},{24,152},{152,24... | collective-permute-start | bytes 196616 | tf_op jit(solution)/shard_map/ppermute | solution.py:18
  298.3 24.2 %collective-permute-start.52 = (bf16[2,512,256]{2,1,0:T(8,128)(2,1)S(1)}, bf16[2,512,256]{2,1,0:T(8,128)(2,1)S(1)}, u32[]{:S(2)}, u32[]{:S(2)}) collective-permute-start(bf16[2,512,256]{2,1,0:T(8,128)(2,1)S(1)} %maximum_select_fusion.19), channel_id=1, source_target_pairs={{0,1},{1,0},{2,3},{3,2},{4,5},{5,4},{6,7},{7,6},{8,9},{9,8},{10,11... | collective-permute-start | bytes 1572872 | tf_op jit(solution)/shard_map/ppermute | solution.py:18
  310.1 12.4 %collective-permute-start.44 = (bf16[256,256]{1,0:T(8,128)(2,1)S(1)}, bf16[256,256]{1,0:T(8,128)(2,1)S(1)}, u32[]{:S(2)}, u32[]{:S(2)}) collective-permute-start(bf16[256,256]{1,0:T(8,128)(2,1)S(1)} %get-tuple-element.20), channel_id=1, source_target_pairs={{0,128},{128,0},{8,136},{136,8},{16,144},{144,16},{24,152},{152,24... | collective-permute-start | bytes 393224 | tf_op jit(solution)/shard_map/ppermute | solution.py:18
  341.3 8.5 %collective-permute-start.57 = (bf16[512,256]{0,1:T(8,128)(2,1)S(1)}, bf16[512,256]{0,1:T(8,128)(2,1)S(1)}, u32[]{:S(2)}, u32[]{:S(2)}) collective-permute-start(bf16[512,256]{0,1:T(8,128)(2,1)S(1)} %fusion.50), channel_id=1, source_target_pairs={{0,16},{16,0},{8,24},{24,8},{32,48},{48,32},{40,56},{56,40},{64,80... | collective-permute-start | bytes 786440 | tf_op jit(solution)/shard_map/ppermute | solution.py:18
  355.3 8.9 %collective-permute-start.59 = (bf16[512,256]{0,1:T(8,128)(2,1)S(1)}, bf16[512,256]{0,1:T(8,128)(2,1)S(1)}, u32[]{:S(2)}, u32[]{:S(2)}) collective-permute-start(bf16[512,256]{0,1:T(8,128)(2,1)S(1)} %fusion.51), channel_id=1, source_target_pairs={{0,64},{64,0},{8,72},{72,8},{16,80},{80,16},{24,88},{88,24},{32,96... | collective-permute-start | bytes 786440 | tf_op jit(solution)/shard_map/ppermute | solution.py:18
  364.2 12.0 %collective-permute-start.60 = (bf16[512,256]{0,1:T(8,128)(2,1)S(1)}, bf16[512,256]{0,1:T(8,128)(2,1)S(1)}, u32[]{:S(2)}, u32[]{:S(2)}) collective-permute-start(bf16[512,256]{0,1:T(8,128)(2,1)S(1)} %fusion.80), channel_id=1, source_target_pairs={{0,128},{128,0},{8,136},{136,8},{16,144},{144,16},{24,152},{152,24... | collective-permute-start | bytes 786440 | tf_op jit(solution)/shard_map/ppermute | solution.py:18
  377.6 12.0 %collective-permute-start.61 = (bf16[2,2,128,256]{2,3,0,1:T(8,128)(2,1)S(1)}, bf16[2,2,128,256]{2,3,0,1:T(8,128)(2,1)S(1)}, u32[]{:S(2)}, u32[]{:S(2)}) collective-permute-start(bf16[2,2,128,256]{2,3,0,1:T(8,128)(2,1)S(1)} %bitcast.186), channel_id=1, source_target_pairs={{0,1},{1,0},{2,3},{3,2},{4,5},{5,4},{6,7},{7,6},{8,9},{9,8},{10,11... | collective-permute-start | bytes 786440 | tf_op jit(solution)/shard_map/ppermute | solution.py:18
  394.5 7.3 %collective-permute-start.63 = (bf16[128,256]{0,1:T(8,128)(2,1)S(1)}, bf16[128,256]{0,1:T(8,128)(2,1)S(1)}, u32[]{:S(2)}, u32[]{:S(2)}) collective-permute-start(bf16[128,256]{0,1:T(8,128)(2,1)S(1)} %dynamic-slice_bitcast_fusion.9), channel_id=1, source_target_pairs={{0,4},{4,0},{1,5},{5,1},{2,6},{6,2},{3,7},{7,3},{8,12},{12,8},{9,1... | collective-permute-start | bytes 196616 | tf_op jit(solution)/shard_map/ppermute | solution.py:18
  417.0 7.6 %collective-permute-start.67 = (bf16[512,256]{0,1:T(8,128)(2,1)S(1)}, bf16[512,256]{0,1:T(8,128)(2,1)S(1)}, u32[]{:S(2)}, u32[]{:S(2)}) collective-permute-start(bf16[512,256]{0,1:T(8,128)(2,1)S(1)} %get-tuple-element.70), channel_id=1, source_target_pairs={{0,8},{8,0},{16,24},{24,16},{32,40},{40,32},{48,56},{56,48},{64,72... | collective-permute-start | bytes 786440 | tf_op jit(solution)/shard_map/ppermute | solution.py:18
  424.7 9.2 %collective-permute-start.68 = (bf16[512,256]{0,1:T(8,128)(2,1)S(1)}, bf16[512,256]{0,1:T(8,128)(2,1)S(1)}, u32[]{:S(2)}, u32[]{:S(2)}) collective-permute-start(bf16[512,256]{0,1:T(8,128)(2,1)S(1)} %fusion.52), channel_id=1, source_target_pairs={{0,16},{16,0},{8,24},{24,8},{32,48},{48,32},{40,56},{56,40},{64,80... | collective-permute-start | bytes 786440 | tf_op jit(solution)/shard_map/ppermute | solution.py:18
  439.4 13.2 %collective-permute-start.70 = (bf16[512,256]{0,1:T(8,128)(2,1)S(1)}, bf16[512,256]{0,1:T(8,128)(2,1)S(1)}, u32[]{:S(2)}, u32[]{:S(2)}) collective-permute-start(bf16[512,256]{0,1:T(8,128)(2,1)S(1)} %fusion.53), channel_id=1, source_target_pairs={{0,64},{64,0},{8,72},{72,8},{16,80},{80,16},{24,88},{88,24},{32,96... | collective-permute-start | bytes 786440 | tf_op jit(solution)/shard_map/ppermute | solution.py:18
  471.5 7.8 %collective-permute-start.75 = (bf16[512,256]{0,1:T(8,128)(2,1)S(1)}, bf16[512,256]{0,1:T(8,128)(2,1)S(1)}, u32[]{:S(2)}, u32[]{:S(2)}) collective-permute-start(bf16[512,256]{0,1:T(8,128)(2,1)S(1)} %add_convert_fusion.1), channel_id=1, source_target_pairs={{0,2},{2,0},{1,3},{3,1},{4,6},{6,4},{5,7},{7,5},{8,10},{10,8},{9,1... | collective-permute-start | bytes 786440 | tf_op jit(solution)/shard_map/ppermute | solution.py:18
  479.4 8.2 %collective-permute-start.76 = (bf16[512,256]{0,1:T(8,128)(2,1)S(1)}, bf16[512,256]{0,1:T(8,128)(2,1)S(1)}, u32[]{:S(2)}, u32[]{:S(2)}) collective-permute-start(bf16[512,256]{0,1:T(8,128)(2,1)S(1)} %add_convert_fusion), channel_id=1, source_target_pairs={{0,4},{4,0},{1,5},{5,1},{2,6},{6,2},{3,7},{7,3},{8,12},{12,8},{9,1... | collective-permute-start | bytes 786440 | tf_op jit(solution)/shard_map/ppermute | solution.py:18
  489.0 6.7 %collective-permute-start.77 = (bf16[512,256]{0,1:T(8,128)(2,1)S(1)}, bf16[512,256]{0,1:T(8,128)(2,1)S(1)}, u32[]{:S(2)}, u32[]{:S(2)}) collective-permute-start(bf16[512,256]{0,1:T(8,128)(2,1)S(1)} %get-tuple-element.72), channel_id=1, source_target_pairs={{0,8},{8,0},{16,24},{24,16},{32,40},{40,32},{48,56},{56,48},{64,72... | collective-permute-start | bytes 786440 | tf_op jit(solution)/shard_map/ppermute | solution.py:18
  495.8 10.0 %collective-permute-start.78 = (bf16[512,256]{0,1:T(8,128)(2,1)S(1)}, bf16[512,256]{0,1:T(8,128)(2,1)S(1)}, u32[]{:S(2)}, u32[]{:S(2)}) collective-permute-start(bf16[512,256]{0,1:T(8,128)(2,1)S(1)} %fusion.54), channel_id=1, source_target_pairs={{0,16},{16,0},{8,24},{24,8},{32,48},{48,32},{40,56},{56,40},{64,80... | collective-permute-start | bytes 786440 | tf_op jit(solution)/shard_map/ppermute | solution.py:18
  557.2 7.6 %collective-permute-start.89 = (bf16[512,256]{0,1:T(8,128)(2,1)S(1)}, bf16[512,256]{0,1:T(8,128)(2,1)S(1)}, u32[]{:S(2)}, u32[]{:S(2)}) collective-permute-start(bf16[512,256]{0,1:T(8,128)(2,1)S(1)} %get-tuple-element.74), channel_id=1, source_target_pairs={{0,8},{8,0},{16,24},{24,16},{32,40},{40,32},{48,56},{56,48},{64,72... | collective-permute-start | bytes 786440 | tf_op jit(solution)/shard_map/ppermute | solution.py:18
  564.9 9.6 %collective-permute-start.90 = (bf16[512,256]{0,1:T(8,128)(2,1)S(1)}, bf16[512,256]{0,1:T(8,128)(2,1)S(1)}, u32[]{:S(2)}, u32[]{:S(2)}) collective-permute-start(bf16[512,256]{0,1:T(8,128)(2,1)S(1)} %fusion.55), channel_id=1, source_target_pairs={{0,16},{16,0},{8,24},{24,8},{32,48},{48,32},{40,56},{56,40},{64,80... | collective-permute-start | bytes 786440 | tf_op jit(solution)/shard_map/ppermute | solution.py:18
  594.0 7.6 %collective-permute-start.95 = (bf16[512,256]{0,1:T(8,128)(2,1)S(1)}, bf16[512,256]{0,1:T(8,128)(2,1)S(1)}, u32[]{:S(2)}, u32[]{:S(2)}) collective-permute-start(bf16[512,256]{0,1:T(8,128)(2,1)S(1)} %dynamic-slice_convert_fusion.2), channel_id=1, source_target_pairs={{0,2},{2,0},{1,3},{3,1},{4,6},{6,4},{5,7},{7,5},{8,10},{10,8},{9,1... | collective-permute-start | bytes 786440 | tf_op jit(solution)/shard_map/ppermute | solution.py:18
  618.1 6.8 %collective-permute-start.99 = (bf16[1024,256]{0,1:T(8,128)(2,1)S(1)}, bf16[1024,256]{0,1:T(8,128)(2,1)S(1)}, u32[]{:S(2)}, u32[]{:S(2)}) collective-permute-start(bf16[1024,256]{0,1:T(8,128)(2,1)S(1)} %maximum_select_fusion.22), channel_id=1, source_target_pairs={{0,1},{1,0},{2,3},{3,2},{4,5},{5,4},{6,7},{7,6},{8,9},{9,8},{10,11... | collective-permute-start | bytes 1572872 | tf_op jit(solution)/shard_map/ppermute | solution.py:18
  625.7 7.6 %collective-permute-start.100 = (bf16[512,256]{0,1:T(8,128)(2,1)S(1)}, bf16[512,256]{0,1:T(8,128)(2,1)S(1)}, u32[]{:S(2)}, u32[]{:S(2)}) collective-permute-start(bf16[512,256]{0,1:T(8,128)(2,1)S(1)} %get-tuple-element.76), channel_id=1, source_target_pairs={{0,8},{8,0},{16,24},{24,16},{32,40},{40,32},{48,56},{56,48},{64,72... | collective-permute-start | bytes 786440 | tf_op jit(solution)/shard_map/ppermute | solution.py:18
  (122 other events, 1161.5 us)

commit v4 on v3

--- a/solution.py
+++ b/solution.py
@@ -76,17 +76,18 @@
             )
         return summand
     column = lax.axis_index("front")
-    for bit_index in range(bits):
-        half_rows = summand.shape[0] // 2
-        upper = column >> bit_index & 1
-        keep = lax.dynamic_slice_in_dim(summand, upper * half_rows, half_rows, 0)
-        send = lax.dynamic_slice_in_dim(summand, (1 - upper) * half_rows, half_rows, 0)
-        summand = keep + partner(send.astype(jnp.bfloat16), "front", bit_index).astype(
+    half_rows = summand.shape[0] // 2
+    upper = column & 1
+    keep = lax.dynamic_slice_in_dim(summand, upper * half_rows, half_rows, 0)
+    send = lax.dynamic_slice_in_dim(summand, (1 - upper) * half_rows, half_rows, 0)
+    summand = keep + partner(send.astype(jnp.bfloat16), "front", 0).astype(jnp.float32)
+    for bit_index in range(1, bits):
+        half = summand.astype(jnp.bfloat16)
+        summand = half.astype(jnp.float32) + partner(half, "front", bit_index).astype(
             jnp.float32
         )
     summand = summand.astype(jnp.bfloat16)
-    for bit_index in reversed(range(bits)):
-        summand = joined(column, bit_index, summand, partner(summand, "front", bit_index))
+    summand = joined(column, 0, summand, partner(summand, "front", 0))
     return summand.astype(jnp.float32)
 
 

time: 659 us -> 658 us (level)
  starting transfers between devices: 212 us -> 196 us
  waiting for transfers between devices: 365 us -> 380 us
    ppermute x104 -> x96, starting transfers between devices: 212 us -> 196 us  [partner(): return lax.ppermute(block, axis, route)]
    ppermute x104 -> x96, waiting for transfers between devices: 365 us -> 380 us  [partner(): return lax.ppermute(block, axis, route)]
  transfers between devices with their start and end apart: 104 -> 96, of which waited for: 98 -> 89; matrix products, arithmetic and copies ran while one was open for 3% -> 3% of each run, Pallas kernels for 0% -> 0%
where the time goes in v4:
time: 658 us; the launch traced here: 648 us
  waiting for transfers between devices  380 us (58%)
  starting transfers between devices  196 us (30%)
  local copies, waits for them, and re-layouts  26.2 us (4%)
  matrix products  24.2 us (4%)
  other arithmetic  19.1 us (3%)
    ppermute x96, waiting for transfers between devices, partner(): return lax.ppermute(block, axis, route)  380 us
    ppermute x96, starting transfers between devices, partner(): return lax.ppermute(block, axis, route)  196 us
  transfers between devices with their start and end apart: 96, of which 89 were waited for; matrix products, arithmetic and copies ran while one was open for 3% of the time, Pallas kernels for 0%

profile of v4, /device:TPU:1, one launch (start us, length us, event | category | flops | bytes accessed | tf_op | source)
XLA Modules:
  0.0 648.1 jit_solution(120267946537847411)
XLA Ops:
  17.5 6.1 collective-permute-start.4
  36.5 13.3 %collective-permute-done.6 = bf16[1024,256]{0,1:T(8,128)(2,1)S(1)} collective-permute-done((bf16[1024,256]{0,1:T(8,128)(2,1)S(1)}, bf16[1024,256]{0,1:T(8,128)(2,1)S(1)}, u32[]{:S(2)}, u32[]{:S(2)}) %collective-permute-start.6) | collective-permute-done | bytes 524320 | tf_op jit(solution)/shard_map/ppermute | solution.py:18
  51.2 13.0 %collective-permute-done.7 = bf16[1024,256]{0,1:T(8,128)(2,1)S(1)} collective-permute-done((bf16[1024,256]{0,1:T(8,128)(2,1)S(1)}, bf16[1024,256]{0,1:T(8,128)(2,1)S(1)}, u32[]{:S(2)}, u32[]{:S(2)}) %collective-permute-start.7) | collective-permute-done | bytes 524320 | tf_op jit(solution)/shard_map/ppermute | solution.py:18
  96.3 6.4 collective-permute-done.9
  109.5 7.1 %collective-permute-done.16 = bf16[512,256]{0,1:T(8,128)(2,1)S(1)} collective-permute-done((bf16[512,256]{0,1:T(8,128)(2,1)S(1)}, bf16[512,256]{0,1:T(8,128)(2,1)S(1)}, u32[]{:S(2)}, u32[]{:S(2)}) %collective-permute-start.16) | collective-permute-done | bytes 262176 | tf_op jit(solution)/shard_map/ppermute | solution.py:18
  118.3 6.6 %collective-permute-done.17 = bf16[512,256]{0,1:T(8,128)(2,1)S(1)} collective-permute-done((bf16[512,256]{0,1:T(8,128)(2,1)S(1)}, bf16[512,256]{0,1:T(8,128)(2,1)S(1)}, u32[]{:S(2)}, u32[]{:S(2)}) %collective-permute-start.17) | collective-permute-done | bytes 262176 | tf_op jit(solution)/shard_map/ppermute | solution.py:18
  152.5 6.1 collective-permute-start.25
  169.6 9.8 %collective-permute-start.26 = (bf16[512,256]{0,1:T(8,128)(2,1)S(1)}, bf16[512,256]{0,1:T(8,128)(2,1)S(1)}, u32[]{:S(2)}, u32[]{:S(2)}) collective-permute-start(bf16[512,256]{0,1:T(8,128)(2,1)S(1)} %fusion.7), channel_id=1, source_target_pairs={{0,1},{1,0},{2,3},{3,2},{4,5},{5,4},{6,7},{7,6},{8,9},{9,8},{10,11... | collective-permute-start | bytes 786440 | tf_op jit(solution)/shard_map/ppermute | solution.py:18
  181.7 6.5 %collective-permute-done.27 = bf16[512,256]{0,1:T(8,128)(2,1)S(1)} collective-permute-done((bf16[512,256]{0,1:T(8,128)(2,1)S(1)}, bf16[512,256]{0,1:T(8,128)(2,1)S(1)}, u32[]{:S(2)}, u32[]{:S(2)}) %collective-permute-start.27) | collective-permute-done | bytes 262176 | tf_op jit(solution)/shard_map/ppermute | solution.py:18
  220.7 5.4 collective-permute-done.35
  226.4 8.2 %collective-permute-start.36 = (bf16[2,512,256]{2,1,0:T(8,128)(2,1)S(1)}, bf16[2,512,256]{2,1,0:T(8,128)(2,1)S(1)}, u32[]{:S(2)}, u32[]{:S(2)}) collective-permute-start(bf16[2,512,256]{2,1,0:T(8,128)(2,1)S(1)} %maximum_select_fusion.16), channel_id=1, source_target_pairs={{0,1},{1,0},{2,3},{3,2},{4,5},{5,4},{6,7},{7,6},{8,9},{9,8},{10,11... | collective-permute-start | bytes 1572872 | tf_op jit(solution)/shard_map/ppermute | solution.py:18
  239.8 8.5 %collective-permute-done.29 = bf16[384,256]{1,0:T(8,128)(2,1)S(1)} collective-permute-done((bf16[384,256]{1,0:T(8,128)(2,1)S(1)}, bf16[384,256]{1,0:T(8,128)(2,1)S(1)}, u32[]{:S(2)}, u32[]{:S(2)}) %collective-permute-start.29) | collective-permute-done | bytes 196640 | tf_op jit(solution)/shard_map/ppermute | solution.py:18
  281.7 7.2 %collective-permute-start.45 = (bf16[128,256]{1,0:T(8,128)(2,1)S(1)}, bf16[128,256]{1,0:T(8,128)(2,1)S(1)}, u32[]{:S(2)}, u32[]{:S(2)}) collective-permute-start(bf16[128,256]{1,0:T(8,128)(2,1)S(1)} %subtract_convert_fusion.8), channel_id=1, source_target_pairs={{0,128},{128,0},{8,136},{136,8},{16,144},{144,16},{24,152},{152,24... | collective-permute-start | bytes 196616 | tf_op jit(solution)/shard_map/ppermute | solution.py:18
  301.7 11.0 %collective-permute-start.48 = (bf16[2,512,256]{2,1,0:T(8,128)(2,1)S(1)}, bf16[2,512,256]{2,1,0:T(8,128)(2,1)S(1)}, u32[]{:S(2)}, u32[]{:S(2)}) collective-permute-start(bf16[2,512,256]{2,1,0:T(8,128)(2,1)S(1)} %maximum_select_fusion.18), channel_id=1, source_target_pairs={{0,1},{1,0},{2,3},{3,2},{4,5},{5,4},{6,7},{7,6},{8,9},{9,8},{10,11... | collective-permute-start | bytes 1572872 | tf_op jit(solution)/shard_map/ppermute | solution.py:18
  314.5 5.6 collective-permute-start.40
  320.8 5.9 collective-permute-done.40
  349.0 5.8 collective-permute-done.53
  360.5 8.7 %collective-permute-done.55 = bf16[512,256]{0,1:T(8,128)(2,1)S(1)} collective-permute-done((bf16[512,256]{0,1:T(8,128)(2,1)S(1)}, bf16[512,256]{0,1:T(8,128)(2,1)S(1)}, u32[]{:S(2)}, u32[]{:S(2)}) %collective-permute-start.55) | collective-permute-done | bytes 262176 | tf_op jit(solution)/shard_map/ppermute | solution.py:18
  372.2 11.5 %collective-permute-done.56 = bf16[512,256]{0,1:T(8,128)(2,1)S(1)} collective-permute-done((bf16[512,256]{0,1:T(8,128)(2,1)S(1)}, bf16[512,256]{0,1:T(8,128)(2,1)S(1)}, u32[]{:S(2)}, u32[]{:S(2)}) %collective-permute-start.56) | collective-permute-done | bytes 262176 | tf_op jit(solution)/shard_map/ppermute | solution.py:18
  385.9 10.8 %collective-permute-start.57 = (bf16[2,2,128,256]{2,3,0,1:T(8,128)(2,1)S(1)}, bf16[2,2,128,256]{2,3,0,1:T(8,128)(2,1)S(1)}, u32[]{:S(2)}, u32[]{:S(2)}) collective-permute-start(bf16[2,2,128,256]{2,3,0,1:T(8,128)(2,1)S(1)} %bitcast.195), channel_id=1, source_target_pairs={{0,1},{1,0},{2,3},{3,2},{4,5},{5,4},{6,7},{7,6},{8,9},{9,8},{10,11... | collective-permute-start | bytes 786440 | tf_op jit(solution)/shard_map/ppermute | solution.py:18
  433.6 5.6 collective-permute-done.64
  444.9 12.8 %collective-permute-done.66 = bf16[512,256]{0,1:T(8,128)(2,1)S(1)} collective-permute-done((bf16[512,256]{0,1:T(8,128)(2,1)S(1)}, bf16[512,256]{0,1:T(8,128)(2,1)S(1)}, u32[]{:S(2)}, u32[]{:S(2)}) %collective-permute-start.66) | collective-permute-done | bytes 262176 | tf_op jit(solution)/shard_map/ppermute | solution.py:18
  477.3 7.2 %collective-permute-done.71 = bf16[512,256]{0,1:T(8,128)(2,1)S(1)} collective-permute-done((bf16[512,256]{0,1:T(8,128)(2,1)S(1)}, bf16[512,256]{0,1:T(8,128)(2,1)S(1)}, u32[]{:S(2)}, u32[]{:S(2)}) %collective-permute-start.71) | collective-permute-done | bytes 262176 | tf_op jit(solution)/shard_map/ppermute | solution.py:18
  486.0 6.8 %collective-permute-done.72 = bf16[512,256]{0,1:T(8,128)(2,1)S(1)} collective-permute-done((bf16[512,256]{0,1:T(8,128)(2,1)S(1)}, bf16[512,256]{0,1:T(8,128)(2,1)S(1)}, u32[]{:S(2)}, u32[]{:S(2)}) %collective-permute-start.72) | collective-permute-done | bytes 262176 | tf_op jit(solution)/shard_map/ppermute | solution.py:18
  504.8 5.6 collective-permute-done.74
  536.2 7.5 %collective-permute-done.80 = bf16[512,256]{0,1:T(8,128)(2,1)S(1)} collective-permute-done((bf16[512,256]{0,1:T(8,128)(2,1)S(1)}, bf16[512,256]{0,1:T(8,128)(2,1)S(1)}, u32[]{:S(2)}, u32[]{:S(2)}) %collective-permute-start.80) | collective-permute-done | bytes 262176 | tf_op jit(solution)/shard_map/ppermute | solution.py:18
  545.5 6.5 %collective-permute-done.81 = bf16[512,256]{0,1:T(8,128)(2,1)S(1)} collective-permute-done((bf16[512,256]{0,1:T(8,128)(2,1)S(1)}, bf16[512,256]{0,1:T(8,128)(2,1)S(1)}, u32[]{:S(2)}, u32[]{:S(2)}) %collective-permute-start.81) | collective-permute-done | bytes 262176 | tf_op jit(solution)/shard_map/ppermute | solution.py:18
  558.1 6.6 %collective-permute-done.83 = bf16[512,256]{0,1:T(8,128)(2,1)S(1)} collective-permute-done((bf16[512,256]{0,1:T(8,128)(2,1)S(1)}, bf16[512,256]{0,1:T(8,128)(2,1)S(1)}, u32[]{:S(2)}, u32[]{:S(2)}) %collective-permute-start.83) | collective-permute-done | bytes 262176 | tf_op jit(solution)/shard_map/ppermute | solution.py:18
  568.4 5.7 collective-permute-done.84
  593.1 13.1 %collective-permute-done.89 = bf16[1024,256]{0,1:T(8,128)(2,1)S(1)} collective-permute-done((bf16[1024,256]{0,1:T(8,128)(2,1)S(1)}, bf16[1024,256]{0,1:T(8,128)(2,1)S(1)}, u32[]{:S(2)}, u32[]{:S(2)}) %collective-permute-start.89) | collective-permute-done | bytes 524320 | tf_op jit(solution)/shard_map/ppermute | solution.py:18
  608.1 12.1 %collective-permute-done.90 = bf16[1024,256]{0,1:T(8,128)(2,1)S(1)} collective-permute-done((bf16[1024,256]{0,1:T(8,128)(2,1)S(1)}, bf16[1024,256]{0,1:T(8,128)(2,1)S(1)}, u32[]{:S(2)}, u32[]{:S(2)}) %collective-permute-start.90) | collective-permute-done | bytes 524320 | tf_op jit(solution)/shard_map/ppermute | solution.py:18
  625.5 6.9 %collective-permute-done.92 = bf16[512,256]{0,1:T(8,128)(2,1)S(1)} collective-permute-done((bf16[512,256]{0,1:T(8,128)(2,1)S(1)}, bf16[512,256]{0,1:T(8,128)(2,1)S(1)}, u32[]{:S(2)}, u32[]{:S(2)}) %collective-permute-start.92) | collective-permute-done | bytes 262176 | tf_op jit(solution)/shard_map/ppermute | solution.py:18
  (500 shorter events, 385.3 us)
Async XLA Ops:
  14.5 11.6 %collective-permute-start = (bf16[496,256]{1,0:T(8,128)(2,1)S(1)}, bf16[496,256]{1,0:T(8,128)(2,1)S(1)}, u32[]{:S(2)}, u32[]{:S(2)}) collective-permute-start(bf16[496,256]{1,0:T(8,128)(2,1)S(1)} %convert_element_type.726), channel_id=1, source_target_pairs={{0,8},{8,0},{16,24},{24,16},{32,40},{40,32},{48,56},{56,48},{64,72... | collective-permute-start | bytes 761864 | tf_op jit(solution)/shard_map/ppermute | solution.py:18
  17.5 9.4 %collective-permute-start.4 = (bf16[2,512,256]{2,1,0:T(8,128)(2,1)S(1)}, bf16[2,512,256]{2,1,0:T(8,128)(2,1)S(1)}, u32[]{:S(2)}, u32[]{:S(2)}) collective-permute-start(bf16[2,512,256]{2,1,0:T(8,128)(2,1)S(1)} %maximum_select_fusion.9), channel_id=1, source_target_pairs={{0,1},{1,0},{2,3},{3,2},{4,5},{5,4},{6,7},{7,6},{8,9},{9,8},{10,11... | collective-permute-start | bytes 1572872 | tf_op jit(solution)/shard_map/ppermute | solution.py:18
  36.4 13.4 %collective-permute-start.6 = (bf16[1024,256]{0,1:T(8,128)(2,1)S(1)}, bf16[1024,256]{0,1:T(8,128)(2,1)S(1)}, u32[]{:S(2)}, u32[]{:S(2)}) collective-permute-start(bf16[1024,256]{0,1:T(8,128)(2,1)S(1)} %fusion.18), channel_id=1, source_target_pairs={{0,2},{2,0},{1,3},{3,1},{4,6},{6,4},{5,7},{7,5},{8,10},{10,8},{9,1... | collective-permute-start | bytes 1572872 | tf_op jit(solution)/shard_map/ppermute | solution.py:18
  50.0 14.1 %collective-permute-start.7 = (bf16[1024,256]{0,1:T(8,128)(2,1)S(1)}, bf16[1024,256]{0,1:T(8,128)(2,1)S(1)}, u32[]{:S(2)}, u32[]{:S(2)}) collective-permute-start(bf16[1024,256]{0,1:T(8,128)(2,1)S(1)} %add_convert_fusion.3), channel_id=1, source_target_pairs={{0,4},{4,0},{1,5},{5,1},{2,6},{6,2},{3,7},{7,3},{8,12},{12,8},{9,1... | collective-permute-start | bytes 1572872 | tf_op jit(solution)/shard_map/ppermute | solution.py:18
  88.2 14.6 %collective-permute-start.14 = (bf16[2,512,256]{2,1,0:T(8,128)(2,1)S(1)}, bf16[2,512,256]{2,1,0:T(8,128)(2,1)S(1)}, u32[]{:S(2)}, u32[]{:S(2)}) collective-permute-start(bf16[2,512,256]{2,1,0:T(8,128)(2,1)S(1)} %maximum_select_fusion.11), channel_id=1, source_target_pairs={{0,1},{1,0},{2,3},{3,2},{4,5},{5,4},{6,7},{7,6},{8,9},{9,8},{10,11... | collective-permute-start | bytes 1572872 | tf_op jit(solution)/shard_map/ppermute | solution.py:18
  93.6 9.1 %collective-permute-start.9 = (bf16[480,256]{1,0:T(8,128)(2,1)S(1)}, bf16[480,256]{1,0:T(8,128)(2,1)S(1)}, u32[]{:S(2)}, u32[]{:S(2)}) collective-permute-start(bf16[480,256]{1,0:T(8,128)(2,1)S(1)} %pad_maximum_fusion.4), channel_id=1, source_target_pairs={{0,16},{16,0},{8,24},{24,8},{32,48},{48,32},{40,56},{56,40},{64,80... | collective-permute-start | bytes 737288 | tf_op jit(solution)/shard_map/ppermute | solution.py:18
  109.0 7.6 %collective-permute-start.16 = (bf16[512,256]{0,1:T(8,128)(2,1)S(1)}, bf16[512,256]{0,1:T(8,128)(2,1)S(1)}, u32[]{:S(2)}, u32[]{:S(2)}) collective-permute-start(bf16[512,256]{0,1:T(8,128)(2,1)S(1)} %fusion.46), channel_id=1, source_target_pairs={{0,2},{2,0},{1,3},{3,1},{4,6},{6,4},{5,7},{7,5},{8,10},{10,8},{9,1... | collective-permute-start | bytes 786440 | tf_op jit(solution)/shard_map/ppermute | solution.py:18
  116.7 8.2 %collective-permute-start.17 = (bf16[512,256]{0,1:T(8,128)(2,1)S(1)}, bf16[512,256]{0,1:T(8,128)(2,1)S(1)}, u32[]{:S(2)}, u32[]{:S(2)}) collective-permute-start(bf16[512,256]{0,1:T(8,128)(2,1)S(1)} %add_convert_fusion.11), channel_id=1, source_target_pairs={{0,4},{4,0},{1,5},{5,1},{2,6},{6,2},{3,7},{7,3},{8,12},{12,8},{9,1... | collective-permute-start | bytes 786440 | tf_op jit(solution)/shard_map/ppermute | solution.py:18
  152.5 14.1 %collective-permute-start.25 = (bf16[2,512,256]{2,1,0:T(8,128)(2,1)S(1)}, bf16[2,512,256]{2,1,0:T(8,128)(2,1)S(1)}, u32[]{:S(2)}, u32[]{:S(2)}) collective-permute-start(bf16[2,512,256]{2,1,0:T(8,128)(2,1)S(1)} %maximum_select_fusion.14), channel_id=1, source_target_pairs={{0,1},{1,0},{2,3},{3,2},{4,5},{5,4},{6,7},{7,6},{8,9},{9,8},{10,11... | collective-permute-start | bytes 1572872 | tf_op jit(solution)/shard_map/ppermute | solution.py:18
  169.6 11.0 %collective-permute-start.26 = (bf16[512,256]{0,1:T(8,128)(2,1)S(1)}, bf16[512,256]{0,1:T(8,128)(2,1)S(1)}, u32[]{:S(2)}, u32[]{:S(2)}) collective-permute-start(bf16[512,256]{0,1:T(8,128)(2,1)S(1)} %fusion.7), channel_id=1, source_target_pairs={{0,1},{1,0},{2,3},{3,2},{4,5},{5,4},{6,7},{7,6},{8,9},{9,8},{10,11... | collective-permute-start | bytes 786440 | tf_op jit(solution)/shard_map/ppermute | solution.py:18
  180.7 7.6 %collective-permute-start.27 = (bf16[512,256]{0,1:T(8,128)(2,1)S(1)}, bf16[512,256]{0,1:T(8,128)(2,1)S(1)}, u32[]{:S(2)}, u32[]{:S(2)}) collective-permute-start(bf16[512,256]{0,1:T(8,128)(2,1)S(1)} %add_convert_fusion.9), channel_id=1, source_target_pairs={{0,2},{2,0},{1,3},{3,1},{4,6},{6,4},{5,7},{7,5},{8,10},{10,8},{9,1... | collective-permute-start | bytes 786440 | tf_op jit(solution)/shard_map/ppermute | solution.py:18
  188.3 8.2 %collective-permute-start.28 = (bf16[512,256]{0,1:T(8,128)(2,1)S(1)}, bf16[512,256]{0,1:T(8,128)(2,1)S(1)}, u32[]{:S(2)}, u32[]{:S(2)}) collective-permute-start(bf16[512,256]{0,1:T(8,128)(2,1)S(1)} %add_convert_fusion.8), channel_id=1, source_target_pairs={{0,4},{4,0},{1,5},{5,1},{2,6},{6,2},{3,7},{7,3},{8,12},{12,8},{9,1... | collective-permute-start | bytes 786440 | tf_op jit(solution)/shard_map/ppermute | solution.py:18
  226.4 22.6 %collective-permute-start.36 = (bf16[2,512,256]{2,1,0:T(8,128)(2,1)S(1)}, bf16[2,512,256]{2,1,0:T(8,128)(2,1)S(1)}, u32[]{:S(2)}, u32[]{:S(2)}) collective-permute-start(bf16[2,512,256]{2,1,0:T(8,128)(2,1)S(1)} %maximum_select_fusion.16), channel_id=1, source_target_pairs={{0,1},{1,0},{2,3},{3,2},{4,5},{5,4},{6,7},{7,6},{8,9},{9,8},{10,11... | collective-permute-start | bytes 1572872 | tf_op jit(solution)/shard_map/ppermute | solution.py:18
  236.0 12.3 %collective-permute-start.29 = (bf16[384,256]{1,0:T(8,128)(2,1)S(1)}, bf16[384,256]{1,0:T(8,128)(2,1)S(1)}, u32[]{:S(2)}, u32[]{:S(2)}) collective-permute-start(bf16[384,256]{1,0:T(8,128)(2,1)S(1)} %pad_maximum_fusion.6), channel_id=1, source_target_pairs={{0,64},{64,0},{8,72},{72,8},{16,80},{80,16},{24,88},{88,24},{32,96... | collective-permute-start | bytes 589832 | tf_op jit(solution)/shard_map/ppermute | solution.py:18
  281.7 8.9 %collective-permute-start.45 = (bf16[128,256]{1,0:T(8,128)(2,1)S(1)}, bf16[128,256]{1,0:T(8,128)(2,1)S(1)}, u32[]{:S(2)}, u32[]{:S(2)}) collective-permute-start(bf16[128,256]{1,0:T(8,128)(2,1)S(1)} %subtract_convert_fusion.8), channel_id=1, source_target_pairs={{0,128},{128,0},{8,136},{136,8},{16,144},{144,16},{24,152},{152,24... | collective-permute-start | bytes 196616 | tf_op jit(solution)/shard_map/ppermute | solution.py:18
  301.7 25.1 %collective-permute-start.48 = (bf16[2,512,256]{2,1,0:T(8,128)(2,1)S(1)}, bf16[2,512,256]{2,1,0:T(8,128)(2,1)S(1)}, u32[]{:S(2)}, u32[]{:S(2)}) collective-permute-start(bf16[2,512,256]{2,1,0:T(8,128)(2,1)S(1)} %maximum_select_fusion.18), channel_id=1, source_target_pairs={{0,1},{1,0},{2,3},{3,2},{4,5},{5,4},{6,7},{7,6},{8,9},{9,8},{10,11... | collective-permute-start | bytes 1572872 | tf_op jit(solution)/shard_map/ppermute | solution.py:18
  314.5 12.2 %collective-permute-start.40 = (bf16[256,256]{1,0:T(8,128)(2,1)S(1)}, bf16[256,256]{1,0:T(8,128)(2,1)S(1)}, u32[]{:S(2)}, u32[]{:S(2)}) collective-permute-start(bf16[256,256]{1,0:T(8,128)(2,1)S(1)} %get-tuple-element.20), channel_id=1, source_target_pairs={{0,128},{128,0},{8,136},{136,8},{16,144},{144,16},{24,152},{152,24... | collective-permute-start | bytes 393224 | tf_op jit(solution)/shard_map/ppermute | solution.py:18
  346.2 8.6 %collective-permute-start.53 = (bf16[512,256]{0,1:T(8,128)(2,1)S(1)}, bf16[512,256]{0,1:T(8,128)(2,1)S(1)}, u32[]{:S(2)}, u32[]{:S(2)}) collective-permute-start(bf16[512,256]{0,1:T(8,128)(2,1)S(1)} %fusion.54), channel_id=1, source_target_pairs={{0,16},{16,0},{8,24},{24,8},{32,48},{48,32},{40,56},{56,40},{64,80... | collective-permute-start | bytes 786440 | tf_op jit(solution)/shard_map/ppermute | solution.py:18
  360.3 8.9 %collective-permute-start.55 = (bf16[512,256]{0,1:T(8,128)(2,1)S(1)}, bf16[512,256]{0,1:T(8,128)(2,1)S(1)}, u32[]{:S(2)}, u32[]{:S(2)}) collective-permute-start(bf16[512,256]{0,1:T(8,128)(2,1)S(1)} %fusion.55), channel_id=1, source_target_pairs={{0,64},{64,0},{8,72},{72,8},{16,80},{80,16},{24,88},{88,24},{32,96... | collective-permute-start | bytes 786440 | tf_op jit(solution)/shard_map/ppermute | solution.py:18
  369.3 14.4 %collective-permute-start.56 = (bf16[512,256]{0,1:T(8,128)(2,1)S(1)}, bf16[512,256]{0,1:T(8,128)(2,1)S(1)}, u32[]{:S(2)}, u32[]{:S(2)}) collective-permute-start(bf16[512,256]{0,1:T(8,128)(2,1)S(1)} %fusion.84), channel_id=1, source_target_pairs={{0,128},{128,0},{8,136},{136,8},{16,144},{144,16},{24,152},{152,24... | collective-permute-start | bytes 786440 | tf_op jit(solution)/shard_map/ppermute | solution.py:18
  385.9 12.0 %collective-permute-start.57 = (bf16[2,2,128,256]{2,3,0,1:T(8,128)(2,1)S(1)}, bf16[2,2,128,256]{2,3,0,1:T(8,128)(2,1)S(1)}, u32[]{:S(2)}, u32[]{:S(2)}) collective-permute-start(bf16[2,2,128,256]{2,3,0,1:T(8,128)(2,1)S(1)} %bitcast.195), channel_id=1, source_target_pairs={{0,1},{1,0},{2,3},{3,2},{4,5},{5,4},{6,7},{7,6},{8,9},{9,8},{10,11... | collective-permute-start | bytes 786440 | tf_op jit(solution)/shard_map/ppermute | solution.py:18
  422.8 7.7 %collective-permute-start.63 = (bf16[512,256]{0,1:T(8,128)(2,1)S(1)}, bf16[512,256]{0,1:T(8,128)(2,1)S(1)}, u32[]{:S(2)}, u32[]{:S(2)}) collective-permute-start(bf16[512,256]{0,1:T(8,128)(2,1)S(1)} %get-tuple-element.70), channel_id=1, source_target_pairs={{0,8},{8,0},{16,24},{24,16},{32,40},{40,32},{48,56},{56,48},{64,72... | collective-permute-start | bytes 786440 | tf_op jit(solution)/shard_map/ppermute | solution.py:18
  430.5 8.7 %collective-permute-start.64 = (bf16[512,256]{0,1:T(8,128)(2,1)S(1)}, bf16[512,256]{0,1:T(8,128)(2,1)S(1)}, u32[]{:S(2)}, u32[]{:S(2)}) collective-permute-start(bf16[512,256]{0,1:T(8,128)(2,1)S(1)} %fusion.56), channel_id=1, source_target_pairs={{0,16},{16,0},{8,24},{24,8},{32,48},{48,32},{40,56},{56,40},{64,80... | collective-permute-start | bytes 786440 | tf_op jit(solution)/shard_map/ppermute | solution.py:18
  444.8 12.9 %collective-permute-start.66 = (bf16[512,256]{0,1:T(8,128)(2,1)S(1)}, bf16[512,256]{0,1:T(8,128)(2,1)S(1)}, u32[]{:S(2)}, u32[]{:S(2)}) collective-permute-start(bf16[512,256]{0,1:T(8,128)(2,1)S(1)} %fusion.57), channel_id=1, source_target_pairs={{0,64},{64,0},{8,72},{72,8},{16,80},{80,16},{24,88},{88,24},{32,96... | collective-permute-start | bytes 786440 | tf_op jit(solution)/shard_map/ppermute | solution.py:18
  476.9 7.6 %collective-permute-start.71 = (bf16[512,256]{0,1:T(8,128)(2,1)S(1)}, bf16[512,256]{0,1:T(8,128)(2,1)S(1)}, u32[]{:S(2)}, u32[]{:S(2)}) collective-permute-start(bf16[512,256]{0,1:T(8,128)(2,1)S(1)} %add_convert_fusion.7), channel_id=1, source_target_pairs={{0,2},{2,0},{1,3},{3,1},{4,6},{6,4},{5,7},{7,5},{8,10},{10,8},{9,1... | collective-permute-start | bytes 786440 | tf_op jit(solution)/shard_map/ppermute | solution.py:18
  484.6 8.2 %collective-permute-start.72 = (bf16[512,256]{0,1:T(8,128)(2,1)S(1)}, bf16[512,256]{0,1:T(8,128)(2,1)S(1)}, u32[]{:S(2)}, u32[]{:S(2)}) collective-permute-start(bf16[512,256]{0,1:T(8,128)(2,1)S(1)} %add_convert_fusion.6), channel_id=1, source_target_pairs={{0,4},{4,0},{1,5},{5,1},{2,6},{6,2},{3,7},{7,3},{8,12},{12,8},{9,1... | collective-permute-start | bytes 786440 | tf_op jit(solution)/shard_map/ppermute | solution.py:18
  500.6 9.8 %collective-permute-start.74 = (bf16[512,256]{0,1:T(8,128)(2,1)S(1)}, bf16[512,256]{0,1:T(8,128)(2,1)S(1)}, u32[]{:S(2)}, u32[]{:S(2)}) collective-permute-start(bf16[512,256]{0,1:T(8,128)(2,1)S(1)} %fusion.58), channel_id=1, source_target_pairs={{0,16},{16,0},{8,24},{24,8},{32,48},{48,32},{40,56},{56,40},{64,80... | collective-permute-start | bytes 786440 | tf_op jit(solution)/shard_map/ppermute | solution.py:18
  536.1 7.6 %collective-permute-start.80 = (bf16[512,256]{0,1:T(8,128)(2,1)S(1)}, bf16[512,256]{0,1:T(8,128)(2,1)S(1)}, u32[]{:S(2)}, u32[]{:S(2)}) collective-permute-start(bf16[512,256]{0,1:T(8,128)(2,1)S(1)} %fusion.45), channel_id=1, source_target_pairs={{0,2},{2,0},{1,3},{3,1},{4,6},{6,4},{5,7},{7,5},{8,10},{10,8},{9,1... | collective-permute-start | bytes 786440 | tf_op jit(solution)/shard_map/ppermute | solution.py:18
  543.8 8.2 %collective-permute-start.81 = (bf16[512,256]{0,1:T(8,128)(2,1)S(1)}, bf16[512,256]{0,1:T(8,128)(2,1)S(1)}, u32[]{:S(2)}, u32[]{:S(2)}) collective-permute-start(bf16[512,256]{0,1:T(8,128)(2,1)S(1)} %add_convert_fusion.5), channel_id=1, source_target_pairs={{0,4},{4,0},{1,5},{5,1},{2,6},{6,2},{3,7},{7,3},{8,12},{12,8},{9,1... | collective-permute-start | bytes 786440 | tf_op jit(solution)/shard_map/ppermute | solution.py:18
  564.8 9.3 %collective-permute-start.84 = (bf16[512,256]{0,1:T(8,128)(2,1)S(1)}, bf16[512,256]{0,1:T(8,128)(2,1)S(1)}, u32[]{:S(2)}, u32[]{:S(2)}) collective-permute-start(bf16[512,256]{0,1:T(8,128)(2,1)S(1)} %fusion.59), channel_id=1, source_target_pairs={{0,16},{16,0},{8,24},{24,8},{32,48},{48,32},{40,56},{56,40},{64,80... | collective-permute-start | bytes 786440 | tf_op jit(solution)/shard_map/ppermute | solution.py:18
  592.7 13.4 %collective-permute-start.89 = (bf16[1024,256]{0,1:T(8,128)(2,1)S(1)}, bf16[1024,256]{0,1:T(8,128)(2,1)S(1)}, u32[]{:S(2)}, u32[]{:S(2)}) collective-permute-start(bf16[1024,256]{0,1:T(8,128)(2,1)S(1)} %fusion.17), channel_id=1, source_target_pairs={{0,2},{2,0},{1,3},{3,1},{4,6},{6,4},{5,7},{7,5},{8,10},{10,8},{9,1... | collective-permute-start | bytes 1572872 | tf_op jit(solution)/shard_map/ppermute | solution.py:18
  606.3 13.8 %collective-permute-start.90 = (bf16[1024,256]{0,1:T(8,128)(2,1)S(1)}, bf16[1024,256]{0,1:T(8,128)(2,1)S(1)}, u32[]{:S(2)}, u32[]{:S(2)}) collective-permute-start(bf16[1024,256]{0,1:T(8,128)(2,1)S(1)} %add_convert_fusion.1), channel_id=1, source_target_pairs={{0,4},{4,0},{1,5},{5,1},{2,6},{6,2},{3,7},{7,3},{8,12},{12,8},{9,1... | collective-permute-start | bytes 1572872 | tf_op jit(solution)/shard_map/ppermute | solution.py:18
  (107 other events, 1057.6 us)

commit v5 on v4

--- a/solution.py
+++ b/solution.py
@@ -124,24 +124,36 @@
     return split
 
 
-def gather_all_own(upper_rhs, levels, position, piv_dev):
+def own_pieces_of(upper_rhs, levels, piv_dev):
     pieces = {}
     for height in range(1, levels + 1):
         rhs_len = piv_dev // 2**height
         rhs_start = piv_dev - piv_dev // 2 ** (height - 1)
         pieces[height] = upper_rhs[rhs_start : rhs_start + rhs_len]
-    for bit_index in range(levels):
-        active = [height for height in range(bit_index + 1, levels + 1)]
-        sent = jnp.concatenate([pieces[height] for height in active], 0)
-        received = partner(sent.astype(jnp.bfloat16), "leaf", bit_index).astype(sent.dtype)
-        offset = 0
-        for height in active:
-            count = pieces[height].shape[0]
-            pieces[height] = joined(
-                position, bit_index, pieces[height], received[offset : offset + count]
-            )
-            offset += count
     return pieces
+
+
+def exchange_round(pieces, levels, position, bit_index, carried=None):
+    active = [height for height in range(bit_index + 1, levels + 1)]
+    parts = [pieces[height].astype(jnp.bfloat16) for height in active]
+    if carried is not None:
+        parts = [carried] + parts
+    received = partner(jnp.concatenate(parts, 0), "leaf", bit_index)
+    offset = 0
+    sibling = None
+    if carried is not None:
+        sibling = received[: carried.shape[0]]
+        offset = carried.shape[0]
+    for height in active:
+        count = pieces[height].shape[0]
+        pieces[height] = joined(
+            position,
+            bit_index,
+            pieces[height],
+            received[offset : offset + count].astype(pieces[height].dtype),
+        )
+        offset += count
+    return sibling
 
 
 def per_device(section_updates, upper_rhs, pivot_inverse, coupling, extend_lists):
@@ -164,7 +176,8 @@
     )
     local_count = piv_blocks + upd_blocks
     carried = section_updates
-    own_pieces = gather_all_own(upper_rhs, levels, position, piv_dev)
+    own_pieces = own_pieces_of(upper_rhs, levels, piv_dev)
+    exchange_round(own_pieces, levels, position, 0)
     saved_part = []
     saved_half = []
     for height in range(1, levels + 1):
@@ -175,7 +188,10 @@
         rhs_start = piv_dev - piv_dev // 2 ** (height - 1)
         member = position & group_size - 1
         own_child = child_base(leaves, height) + (position >> height - 1)
-        sibling = partner(carried, "leaf", height - 1)
+        if height == 1:
+            sibling = partner(carried, "leaf", height - 1)
+        else:
+            sibling = exchange_round(own_pieces, levels, position, height - 1, carried)
         pair_blocks = front_gather(jnp.stack([carried, sibling]))
         pair_lists = jnp.stack(
             [list_row(extend_lists, own_child), list_row(extend_lists, own_child ^ 1)]

time: 658 us -> 633 us (0.962)
  waiting for transfers between devices: 380 us -> 349 us
    ppermute x96 -> x92, waiting for transfers between devices: 380 us -> 349 us  [partner(): return lax.ppermute(block, axis, route)]
    convert_element_type x3 -> x18, other arithmetic: 1.81 us -> 9.78 us  [the longest x12 7.54 us: exchange_round(): received[offset:offset + count].astype(pieces[height].dtype)]
    ppermute x96 -> x92, starting transfers between devices: 196 us -> 195 us  [partner(): return lax.ppermute(block, axis, route)]
  transfers between devices with their start and end apart: 96 -> 92, of which waited for: 89 -> 84; matrix products, arithmetic and copies ran while one was open for 3% -> 4% of each run, Pallas kernels for 0% -> 0%
where the time goes in v5:
time: 633 us; the launch traced here: 622 us
  waiting for transfers between devices  349 us (55%)
  starting transfers between devices  195 us (31%)
  local copies, waits for them, and re-layouts  28.1 us (4%)
  other arithmetic  24.4 us (4%)
  matrix products  22.8 us (4%)
    ppermute x92, waiting for transfers between devices, partner(): return lax.ppermute(block, axis, route)  349 us
    ppermute x92, starting transfers between devices, partner(): return lax.ppermute(block, axis, route)  195 us
  transfers between devices with their start and end apart: 92, of which 84 were waited for; matrix products, arithmetic and copies ran while one was open for 4% of the time, Pallas kernels for 0%

profile of v5, /device:TPU:1, one launch (start us, length us, event | category | flops | bytes accessed | tf_op | source)
XLA Modules:
  0.0 622.2 jit_solution(9252124621945046526)
XLA Ops:
  18.4 5.2 collective-permute-start.4
  35.6 12.5 %collective-permute-done.6 = bf16[1024,256]{0,1:T(8,128)(2,1)S(1)} collective-permute-done((bf16[1024,256]{0,1:T(8,128)(2,1)S(1)}, bf16[1024,256]{0,1:T(8,128)(2,1)S(1)}, u32[]{:S(2)}, u32[]{:S(2)}) %collective-permute-start.6) | collective-permute-done | bytes 524320 | tf_op jit(solution)/shard_map/ppermute | solution.py:18
  50.2 12.1 %collective-permute-done.7 = bf16[1024,256]{0,1:T(8,128)(2,1)S(1)} collective-permute-done((bf16[1024,256]{0,1:T(8,128)(2,1)S(1)}, bf16[1024,256]{0,1:T(8,128)(2,1)S(1)}, u32[]{:S(2)}, u32[]{:S(2)}) %collective-permute-start.7) | collective-permute-done | bytes 524320 | tf_op jit(solution)/shard_map/ppermute | solution.py:18
  73.1 7.9 %collective-permute-done.10 = bf16[608,256]{1,0:T(8,128)(2,1)S(1)} collective-permute-done((bf16[608,256]{1,0:T(8,128)(2,1)S(1)}, bf16[608,256]{1,0:T(8,128)(2,1)S(1)}, u32[]{:S(2)}, u32[]{:S(2)}) %collective-permute-start.10) | collective-permute-done | bytes 311328 | tf_op jit(solution)/shard_map/ppermute | solution.py:18
  103.9 6.9 %collective-permute-done.15 = bf16[512,256]{0,1:T(8,128)(2,1)S(1)} collective-permute-done((bf16[512,256]{0,1:T(8,128)(2,1)S(1)}, bf16[512,256]{0,1:T(8,128)(2,1)S(1)}, u32[]{:S(2)}, u32[]{:S(2)}) %collective-permute-start.15) | collective-permute-done | bytes 262176 | tf_op jit(solution)/shard_map/ppermute | solution.py:18
  113.5 5.5 collective-permute-done.16
  132.3 5.6 collective-permute-done.20
  149.0 6.4 %collective-permute-start.23 = (bf16[2,512,256]{2,1,0:T(8,128)(2,1)S(1)}, bf16[2,512,256]{2,1,0:T(8,128)(2,1)S(1)}, u32[]{:S(2)}, u32[]{:S(2)}) collective-permute-start(bf16[2,512,256]{2,1,0:T(8,128)(2,1)S(1)} %maximum_select_fusion.14), channel_id=1, source_target_pairs={{0,1},{1,0},{2,3},{3,2},{4,5},{5,4},{6,7},{7,6},{8,9},{9,8},{10,11... | collective-permute-start | bytes 1572872 | tf_op jit(solution)/shard_map/ppermute | solution.py:18
  163.3 6.4 %collective-permute-done.25 = bf16[512,256]{0,1:T(8,128)(2,1)S(1)} collective-permute-done((bf16[512,256]{0,1:T(8,128)(2,1)S(1)}, bf16[512,256]{0,1:T(8,128)(2,1)S(1)}, u32[]{:S(2)}, u32[]{:S(2)}) %collective-permute-start.25) | collective-permute-done | bytes 262176 | tf_op jit(solution)/shard_map/ppermute | solution.py:18
  169.8 10.3 %collective-permute-start.26 = (bf16[512,256]{0,1:T(8,128)(2,1)S(1)}, bf16[512,256]{0,1:T(8,128)(2,1)S(1)}, u32[]{:S(2)}, u32[]{:S(2)}) collective-permute-start(bf16[512,256]{0,1:T(8,128)(2,1)S(1)} %add_convert_fusion.8), channel_id=1, source_target_pairs={{0,4},{4,0},{1,5},{5,1},{2,6},{6,2},{3,7},{7,3},{8,12},{12,8},{9,1... | collective-permute-start | bytes 786440 | tf_op jit(solution)/shard_map/ppermute | solution.py:18
  180.8 6.2 %collective-permute-done.26 = bf16[512,256]{0,1:T(8,128)(2,1)S(1)} collective-permute-done((bf16[512,256]{0,1:T(8,128)(2,1)S(1)}, bf16[512,256]{0,1:T(8,128)(2,1)S(1)}, u32[]{:S(2)}, u32[]{:S(2)}) %collective-permute-start.26) | collective-permute-done | bytes 262176 | tf_op jit(solution)/shard_map/ppermute | solution.py:18
  202.5 6.6 %collective-permute-done.30 = bf16[512,256]{1,0:T(8,128)(2,1)S(1)} collective-permute-done((bf16[512,256]{1,0:T(8,128)(2,1)S(1)}, bf16[512,256]{1,0:T(8,128)(2,1)S(1)}, u32[]{:S(2)}, u32[]{:S(2)}) %collective-permute-start.30) | collective-permute-done | bytes 262176 | tf_op jit(solution)/shard_map/ppermute | solution.py:18
  224.8 6.3 %collective-permute-start.33 = (bf16[2,512,256]{2,1,0:T(8,128)(2,1)S(1)}, bf16[2,512,256]{2,1,0:T(8,128)(2,1)S(1)}, u32[]{:S(2)}, u32[]{:S(2)}) collective-permute-start(bf16[2,512,256]{2,1,0:T(8,128)(2,1)S(1)} %maximum_select_fusion.16), channel_id=1, source_target_pairs={{0,1},{1,0},{2,3},{3,2},{4,5},{5,4},{6,7},{7,6},{8,9},{9,8},{10,11... | collective-permute-start | bytes 1572872 | tf_op jit(solution)/shard_map/ppermute | solution.py:18
  265.3 5.5 collective-permute-start.41
  287.1 13.9 %collective-permute-start.44 = (bf16[2,512,256]{2,1,0:T(8,128)(2,1)S(1)}, bf16[2,512,256]{2,1,0:T(8,128)(2,1)S(1)}, u32[]{:S(2)}, u32[]{:S(2)}) collective-permute-start(bf16[2,512,256]{2,1,0:T(8,128)(2,1)S(1)} %maximum_select_fusion.18), channel_id=1, source_target_pairs={{0,1},{1,0},{2,3},{3,2},{4,5},{5,4},{6,7},{7,6},{8,9},{9,8},{10,11... | collective-permute-start | bytes 1572872 | tf_op jit(solution)/shard_map/ppermute | solution.py:18
  316.9 5.8 collective-permute-done.48
  322.9 6.7 %collective-permute-done.49 = bf16[512,256]{0,1:T(8,128)(2,1)S(1)} collective-permute-done((bf16[512,256]{0,1:T(8,128)(2,1)S(1)}, bf16[512,256]{0,1:T(8,128)(2,1)S(1)}, u32[]{:S(2)}, u32[]{:S(2)}) %collective-permute-start.49) | collective-permute-done | bytes 262176 | tf_op jit(solution)/shard_map/ppermute | solution.py:18
  336.8 7.4 %collective-permute-done.51 = bf16[512,256]{0,1:T(8,128)(2,1)S(1)} collective-permute-done((bf16[512,256]{0,1:T(8,128)(2,1)S(1)}, bf16[512,256]{0,1:T(8,128)(2,1)S(1)}, u32[]{:S(2)}, u32[]{:S(2)}) %collective-permute-start.51) | collective-permute-done | bytes 262176 | tf_op jit(solution)/shard_map/ppermute | solution.py:18
  348.0 6.1 collective-permute-done.52
  356.3 12.1 %collective-permute-start.53 = (bf16[2,2,128,256]{2,3,0,1:T(8,128)(2,1)S(1)}, bf16[2,2,128,256]{2,3,0,1:T(8,128)(2,1)S(1)}, u32[]{:S(2)}, u32[]{:S(2)}) collective-permute-start(bf16[2,2,128,256]{2,3,0,1:T(8,128)(2,1)S(1)} %bitcast.199), channel_id=1, source_target_pairs={{0,1},{1,0},{2,3},{3,2},{4,5},{5,4},{6,7},{7,6},{8,9},{9,8},{10,11... | collective-permute-start | bytes 786440 | tf_op jit(solution)/shard_map/ppermute | solution.py:18
  407.9 5.6 collective-permute-done.60
  419.1 13.1 %collective-permute-done.62 = bf16[512,256]{0,1:T(8,128)(2,1)S(1)} collective-permute-done((bf16[512,256]{0,1:T(8,128)(2,1)S(1)}, bf16[512,256]{0,1:T(8,128)(2,1)S(1)}, u32[]{:S(2)}, u32[]{:S(2)}) %collective-permute-start.62) | collective-permute-done | bytes 262176 | tf_op jit(solution)/shard_map/ppermute | solution.py:18
  451.2 7.5 %collective-permute-done.67 = bf16[512,256]{0,1:T(8,128)(2,1)S(1)} collective-permute-done((bf16[512,256]{0,1:T(8,128)(2,1)S(1)}, bf16[512,256]{0,1:T(8,128)(2,1)S(1)}, u32[]{:S(2)}, u32[]{:S(2)}) %collective-permute-start.67) | collective-permute-done | bytes 262176 | tf_op jit(solution)/shard_map/ppermute | solution.py:18
  461.7 5.3 collective-permute-done.68
  479.4 5.5 collective-permute-done.70
  510.6 7.5 %collective-permute-done.76 = bf16[512,256]{0,1:T(8,128)(2,1)S(1)} collective-permute-done((bf16[512,256]{0,1:T(8,128)(2,1)S(1)}, bf16[512,256]{0,1:T(8,128)(2,1)S(1)}, u32[]{:S(2)}, u32[]{:S(2)}) %collective-permute-start.76) | collective-permute-done | bytes 262176 | tf_op jit(solution)/shard_map/ppermute | solution.py:18
  520.9 5.5 collective-permute-done.77
  532.2 6.9 %collective-permute-done.79 = bf16[512,256]{0,1:T(8,128)(2,1)S(1)} collective-permute-done((bf16[512,256]{0,1:T(8,128)(2,1)S(1)}, bf16[512,256]{0,1:T(8,128)(2,1)S(1)}, u32[]{:S(2)}, u32[]{:S(2)}) %collective-permute-start.79) | collective-permute-done | bytes 262176 | tf_op jit(solution)/shard_map/ppermute | solution.py:18
  542.5 5.5 collective-permute-done.80
  566.9 13.1 %collective-permute-done.85 = bf16[1024,256]{0,1:T(8,128)(2,1)S(1)} collective-permute-done((bf16[1024,256]{0,1:T(8,128)(2,1)S(1)}, bf16[1024,256]{0,1:T(8,128)(2,1)S(1)}, u32[]{:S(2)}, u32[]{:S(2)}) %collective-permute-start.85) | collective-permute-done | bytes 524320 | tf_op jit(solution)/shard_map/ppermute | solution.py:18
  583.2 10.8 %collective-permute-done.86 = bf16[1024,256]{0,1:T(8,128)(2,1)S(1)} collective-permute-done((bf16[1024,256]{0,1:T(8,128)(2,1)S(1)}, bf16[1024,256]{0,1:T(8,128)(2,1)S(1)}, u32[]{:S(2)}, u32[]{:S(2)}) %collective-permute-start.86) | collective-permute-done | bytes 524320 | tf_op jit(solution)/shard_map/ppermute | solution.py:18
  599.6 6.9 %collective-permute-done.88 = bf16[512,256]{0,1:T(8,128)(2,1)S(1)} collective-permute-done((bf16[512,256]{0,1:T(8,128)(2,1)S(1)}, bf16[512,256]{0,1:T(8,128)(2,1)S(1)}, u32[]{:S(2)}, u32[]{:S(2)}) %collective-permute-start.88) | collective-permute-done | bytes 262176 | tf_op jit(solution)/shard_map/ppermute | solution.py:18
  (479 shorter events, 370.9 us)
Async XLA Ops:
  14.8 9.6 %collective-permute-start = (bf16[496,256]{1,0:T(8,128)(2,1)S(1)}, bf16[496,256]{1,0:T(8,128)(2,1)S(1)}, u32[]{:S(2)}, u32[]{:S(2)}) collective-permute-start(bf16[496,256]{1,0:T(8,128)(2,1)S(1)} %constant_dynamic-update-slice_fusion), channel_id=1, source_target_pairs={{0,8},{8,0},{16,24},{24,16},{32,40},{40,32},{48,56},{56,48},{64,72... | collective-permute-start | bytes 761864 | tf_op jit(solution)/shard_map/ppermute | solution.py:18
  18.4 6.9 %collective-permute-start.4 = (bf16[2,512,256]{2,1,0:T(8,128)(2,1)S(1)}, bf16[2,512,256]{2,1,0:T(8,128)(2,1)S(1)}, u32[]{:S(2)}, u32[]{:S(2)}) collective-permute-start(bf16[2,512,256]{2,1,0:T(8,128)(2,1)S(1)} %maximum_select_fusion.9), channel_id=1, source_target_pairs={{0,1},{1,0},{2,3},{3,2},{4,5},{5,4},{6,7},{7,6},{8,9},{9,8},{10,11... | collective-permute-start | bytes 1572872 | tf_op jit(solution)/shard_map/ppermute | solution.py:18
  34.7 13.4 %collective-permute-start.6 = (bf16[1024,256]{0,1:T(8,128)(2,1)S(1)}, bf16[1024,256]{0,1:T(8,128)(2,1)S(1)}, u32[]{:S(2)}, u32[]{:S(2)}) collective-permute-start(bf16[1024,256]{0,1:T(8,128)(2,1)S(1)} %fusion.18), channel_id=1, source_target_pairs={{0,2},{2,0},{1,3},{3,1},{4,6},{6,4},{5,7},{7,5},{8,10},{10,8},{9,1... | collective-permute-start | bytes 1572872 | tf_op jit(solution)/shard_map/ppermute | solution.py:18
  48.3 14.0 %collective-permute-start.7 = (bf16[1024,256]{0,1:T(8,128)(2,1)S(1)}, bf16[1024,256]{0,1:T(8,128)(2,1)S(1)}, u32[]{:S(2)}, u32[]{:S(2)}) collective-permute-start(bf16[1024,256]{0,1:T(8,128)(2,1)S(1)} %add_convert_fusion.3), channel_id=1, source_target_pairs={{0,4},{4,0},{1,5},{5,1},{2,6},{6,2},{3,7},{7,3},{8,12},{12,8},{9,1... | collective-permute-start | bytes 1572872 | tf_op jit(solution)/shard_map/ppermute | solution.py:18
  71.5 9.6 %collective-permute-start.10 = (bf16[608,256]{1,0:T(8,128)(2,1)S(1)}, bf16[608,256]{1,0:T(8,128)(2,1)S(1)}, u32[]{:S(2)}, u32[]{:S(2)}) collective-permute-start(bf16[608,256]{1,0:T(8,128)(2,1)S(1)} %get-tuple-element.32), channel_id=1, source_target_pairs={{0,16},{16,0},{8,24},{24,8},{32,48},{48,32},{40,56},{56,40},{64,80... | collective-permute-start | bytes 933896 | tf_op jit(solution)/shard_map/ppermute | solution.py:18
  103.2 7.6 %collective-permute-start.15 = (bf16[512,256]{0,1:T(8,128)(2,1)S(1)}, bf16[512,256]{0,1:T(8,128)(2,1)S(1)}, u32[]{:S(2)}, u32[]{:S(2)}) collective-permute-start(bf16[512,256]{0,1:T(8,128)(2,1)S(1)} %fusion.46), channel_id=1, source_target_pairs={{0,2},{2,0},{1,3},{3,1},{4,6},{6,4},{5,7},{7,5},{8,10},{10,8},{9,1... | collective-permute-start | bytes 786440 | tf_op jit(solution)/shard_map/ppermute | solution.py:18
  110.8 8.2 %collective-permute-start.16 = (bf16[512,256]{0,1:T(8,128)(2,1)S(1)}, bf16[512,256]{0,1:T(8,128)(2,1)S(1)}, u32[]{:S(2)}, u32[]{:S(2)}) collective-permute-start(bf16[512,256]{0,1:T(8,128)(2,1)S(1)} %add_convert_fusion.11), channel_id=1, source_target_pairs={{0,4},{4,0},{1,5},{5,1},{2,6},{6,2},{3,7},{7,3},{8,12},{12,8},{9,1... | collective-permute-start | bytes 786440 | tf_op jit(solution)/shard_map/ppermute | solution.py:18
  149.0 8.1 %collective-permute-start.23 = (bf16[2,512,256]{2,1,0:T(8,128)(2,1)S(1)}, bf16[2,512,256]{2,1,0:T(8,128)(2,1)S(1)}, u32[]{:S(2)}, u32[]{:S(2)}) collective-permute-start(bf16[2,512,256]{2,1,0:T(8,128)(2,1)S(1)} %maximum_select_fusion.14), channel_id=1, source_target_pairs={{0,1},{1,0},{2,3},{3,2},{4,5},{5,4},{6,7},{7,6},{8,9},{9,8},{10,11... | collective-permute-start | bytes 1572872 | tf_op jit(solution)/shard_map/ppermute | solution.py:18
  161.9 7.8 %collective-permute-start.25 = (bf16[512,256]{0,1:T(8,128)(2,1)S(1)}, bf16[512,256]{0,1:T(8,128)(2,1)S(1)}, u32[]{:S(2)}, u32[]{:S(2)}) collective-permute-start(bf16[512,256]{0,1:T(8,128)(2,1)S(1)} %add_convert_fusion.9), channel_id=1, source_target_pairs={{0,2},{2,0},{1,3},{3,1},{4,6},{6,4},{5,7},{7,5},{8,10},{10,8},{9,1... | collective-permute-start | bytes 786440 | tf_op jit(solution)/shard_map/ppermute | solution.py:18
  169.8 17.2 %collective-permute-start.26 = (bf16[512,256]{0,1:T(8,128)(2,1)S(1)}, bf16[512,256]{0,1:T(8,128)(2,1)S(1)}, u32[]{:S(2)}, u32[]{:S(2)}) collective-permute-start(bf16[512,256]{0,1:T(8,128)(2,1)S(1)} %add_convert_fusion.8), channel_id=1, source_target_pairs={{0,4},{4,0},{1,5},{5,1},{2,6},{6,2},{3,7},{7,3},{8,12},{12,8},{9,1... | collective-permute-start | bytes 786440 | tf_op jit(solution)/shard_map/ppermute | solution.py:18
  199.7 9.4 %collective-permute-start.30 = (bf16[512,256]{1,0:T(8,128)(2,1)S(1)}, bf16[512,256]{1,0:T(8,128)(2,1)S(1)}, u32[]{:S(2)}, u32[]{:S(2)}) collective-permute-start(bf16[512,256]{1,0:T(8,128)(2,1)S(1)} %pad_maximum_fusion.5), channel_id=1, source_target_pairs={{0,64},{64,0},{8,72},{72,8},{16,80},{80,16},{24,88},{88,24},{32,96... | collective-permute-start | bytes 786440 | tf_op jit(solution)/shard_map/ppermute | solution.py:18
  215.6 8.9 %collective-permute-start.32 = (bf16[2,256,256]{2,1,0:T(8,128)(2,1)S(1)}, bf16[2,256,256]{2,1,0:T(8,128)(2,1)S(1)}, u32[]{:S(2)}, u32[]{:S(2)}) collective-permute-start(bf16[2,256,256]{2,1,0:T(8,128)(2,1)S(1)} %maximum_select_fusion.27), channel_id=1, source_target_pairs={{0,2},{2,0},{1,3},{3,1},{4,6},{6,4},{5,7},{7,5},{8,10},{10,8},{9,1... | collective-permute-start | bytes 786440 | tf_op jit(solution)/shard_map/ppermute | solution.py:18
  224.8 7.8 %collective-permute-start.33 = (bf16[2,512,256]{2,1,0:T(8,128)(2,1)S(1)}, bf16[2,512,256]{2,1,0:T(8,128)(2,1)S(1)}, u32[]{:S(2)}, u32[]{:S(2)}) collective-permute-start(bf16[2,512,256]{2,1,0:T(8,128)(2,1)S(1)} %maximum_select_fusion.16), channel_id=1, source_target_pairs={{0,1},{1,0},{2,3},{3,2},{4,5},{5,4},{6,7},{7,6},{8,9},{9,8},{10,11... | collective-permute-start | bytes 1572872 | tf_op jit(solution)/shard_map/ppermute | solution.py:18
  265.3 9.1 %collective-permute-start.41 = (bf16[384,256]{1,0:T(8,128)(2,1)S(1)}, bf16[384,256]{1,0:T(8,128)(2,1)S(1)}, u32[]{:S(2)}, u32[]{:S(2)}) collective-permute-start(bf16[384,256]{1,0:T(8,128)(2,1)S(1)} %pad_maximum_fusion.6), channel_id=1, source_target_pairs={{0,128},{128,0},{8,136},{136,8},{16,144},{144,16},{24,152},{152,24... | collective-permute-start | bytes 589832 | tf_op jit(solution)/shard_map/ppermute | solution.py:18
  274.4 7.1 %collective-permute-start.42 = (bf16[2,128,256]{2,1,0:T(8,128)(2,1)S(1)}, bf16[2,128,256]{2,1,0:T(8,128)(2,1)S(1)}, u32[]{:S(2)}, u32[]{:S(2)}) collective-permute-start(bf16[2,128,256]{2,1,0:T(8,128)(2,1)S(1)} %pad_maximum_fusion.11), channel_id=1, source_target_pairs={{0,4},{4,0},{1,5},{5,1},{2,6},{6,2},{3,7},{7,3},{8,12},{12,8},{9,1... | collective-permute-start | bytes 393224 | tf_op jit(solution)/shard_map/ppermute | solution.py:18
  287.1 15.5 %collective-permute-start.44 = (bf16[2,512,256]{2,1,0:T(8,128)(2,1)S(1)}, bf16[2,512,256]{2,1,0:T(8,128)(2,1)S(1)}, u32[]{:S(2)}, u32[]{:S(2)}) collective-permute-start(bf16[2,512,256]{2,1,0:T(8,128)(2,1)S(1)} %maximum_select_fusion.18), channel_id=1, source_target_pairs={{0,1},{1,0},{2,3},{3,2},{4,5},{5,4},{6,7},{7,6},{8,9},{9,8},{10,11... | collective-permute-start | bytes 1572872 | tf_op jit(solution)/shard_map/ppermute | solution.py:18
  335.1 9.0 %collective-permute-start.51 = (bf16[512,256]{0,1:T(8,128)(2,1)S(1)}, bf16[512,256]{0,1:T(8,128)(2,1)S(1)}, u32[]{:S(2)}, u32[]{:S(2)}) collective-permute-start(bf16[512,256]{0,1:T(8,128)(2,1)S(1)} %fusion.55), channel_id=1, source_target_pairs={{0,64},{64,0},{8,72},{72,8},{16,80},{80,16},{24,88},{88,24},{32,96... | collective-permute-start | bytes 786440 | tf_op jit(solution)/shard_map/ppermute | solution.py:18
  344.3 9.8 %collective-permute-start.52 = (bf16[512,256]{0,1:T(8,128)(2,1)S(1)}, bf16[512,256]{0,1:T(8,128)(2,1)S(1)}, u32[]{:S(2)}, u32[]{:S(2)}) collective-permute-start(bf16[512,256]{0,1:T(8,128)(2,1)S(1)} %fusion.84), channel_id=1, source_target_pairs={{0,128},{128,0},{8,136},{136,8},{16,144},{144,16},{24,152},{152,24... | collective-permute-start | bytes 786440 | tf_op jit(solution)/shard_map/ppermute | solution.py:18
  356.3 13.2 %collective-permute-start.53 = (bf16[2,2,128,256]{2,3,0,1:T(8,128)(2,1)S(1)}, bf16[2,2,128,256]{2,3,0,1:T(8,128)(2,1)S(1)}, u32[]{:S(2)}, u32[]{:S(2)}) collective-permute-start(bf16[2,2,128,256]{2,3,0,1:T(8,128)(2,1)S(1)} %bitcast.199), channel_id=1, source_target_pairs={{0,1},{1,0},{2,3},{3,2},{4,5},{5,4},{6,7},{7,6},{8,9},{9,8},{10,11... | collective-permute-start | bytes 786440 | tf_op jit(solution)/shard_map/ppermute | solution.py:18
  369.6 8.6 %collective-permute-start.54 = (bf16[2,128,256]{1,2,0:T(8,128)(2,1)S(1)}, bf16[2,128,256]{1,2,0:T(8,128)(2,1)S(1)}, u32[]{:S(2)}, u32[]{:S(2)}) collective-permute-start(bf16[2,128,256]{1,2,0:T(8,128)(2,1)S(1)} %dynamic-slice_bitcast_fusion.4), channel_id=1, source_target_pairs={{0,2},{2,0},{1,3},{3,1},{4,6},{6,4},{5,7},{7,5},{8,10},{10,8},{9,1... | collective-permute-start | bytes 393224 | tf_op jit(solution)/shard_map/ppermute | solution.py:18
  404.6 8.9 %collective-permute-start.60 = (bf16[512,256]{0,1:T(8,128)(2,1)S(1)}, bf16[512,256]{0,1:T(8,128)(2,1)S(1)}, u32[]{:S(2)}, u32[]{:S(2)}) collective-permute-start(bf16[512,256]{0,1:T(8,128)(2,1)S(1)} %fusion.56), channel_id=1, source_target_pairs={{0,16},{16,0},{8,24},{24,8},{32,48},{48,32},{40,56},{56,40},{64,80... | collective-permute-start | bytes 786440 | tf_op jit(solution)/shard_map/ppermute | solution.py:18
  419.0 13.2 %collective-permute-start.62 = (bf16[512,256]{0,1:T(8,128)(2,1)S(1)}, bf16[512,256]{0,1:T(8,128)(2,1)S(1)}, u32[]{:S(2)}, u32[]{:S(2)}) collective-permute-start(bf16[512,256]{0,1:T(8,128)(2,1)S(1)} %fusion.57), channel_id=1, source_target_pairs={{0,64},{64,0},{8,72},{72,8},{16,80},{80,16},{24,88},{88,24},{32,96... | collective-permute-start | bytes 786440 | tf_op jit(solution)/shard_map/ppermute | solution.py:18
  451.1 7.6 %collective-permute-start.67 = (bf16[512,256]{0,1:T(8,128)(2,1)S(1)}, bf16[512,256]{0,1:T(8,128)(2,1)S(1)}, u32[]{:S(2)}, u32[]{:S(2)}) collective-permute-start(bf16[512,256]{0,1:T(8,128)(2,1)S(1)} %add_convert_fusion.7), channel_id=1, source_target_pairs={{0,2},{2,0},{1,3},{3,1},{4,6},{6,4},{5,7},{7,5},{8,10},{10,8},{9,1... | collective-permute-start | bytes 786440 | tf_op jit(solution)/shard_map/ppermute | solution.py:18
  458.8 8.2 %collective-permute-start.68 = (bf16[512,256]{0,1:T(8,128)(2,1)S(1)}, bf16[512,256]{0,1:T(8,128)(2,1)S(1)}, u32[]{:S(2)}, u32[]{:S(2)}) collective-permute-start(bf16[512,256]{0,1:T(8,128)(2,1)S(1)} %add_convert_fusion.6), channel_id=1, source_target_pairs={{0,4},{4,0},{1,5},{5,1},{2,6},{6,2},{3,7},{7,3},{8,12},{12,8},{9,1... | collective-permute-start | bytes 786440 | tf_op jit(solution)/shard_map/ppermute | solution.py:18
  474.9 10.0 %collective-permute-start.70 = (bf16[512,256]{0,1:T(8,128)(2,1)S(1)}, bf16[512,256]{0,1:T(8,128)(2,1)S(1)}, u32[]{:S(2)}, u32[]{:S(2)}) collective-permute-start(bf16[512,256]{0,1:T(8,128)(2,1)S(1)} %fusion.58), channel_id=1, source_target_pairs={{0,16},{16,0},{8,24},{24,8},{32,48},{48,32},{40,56},{56,40},{64,80... | collective-permute-start | bytes 786440 | tf_op jit(solution)/shard_map/ppermute | solution.py:18
  510.5 7.6 %collective-permute-start.76 = (bf16[512,256]{0,1:T(8,128)(2,1)S(1)}, bf16[512,256]{0,1:T(8,128)(2,1)S(1)}, u32[]{:S(2)}, u32[]{:S(2)}) collective-permute-start(bf16[512,256]{0,1:T(8,128)(2,1)S(1)} %fusion.45), channel_id=1, source_target_pairs={{0,2},{2,0},{1,3},{3,1},{4,6},{6,4},{5,7},{7,5},{8,10},{10,8},{9,1... | collective-permute-start | bytes 786440 | tf_op jit(solution)/shard_map/ppermute | solution.py:18
  518.1 8.2 %collective-permute-start.77 = (bf16[512,256]{0,1:T(8,128)(2,1)S(1)}, bf16[512,256]{0,1:T(8,128)(2,1)S(1)}, u32[]{:S(2)}, u32[]{:S(2)}) collective-permute-start(bf16[512,256]{0,1:T(8,128)(2,1)S(1)} %add_convert_fusion.5), channel_id=1, source_target_pairs={{0,4},{4,0},{1,5},{5,1},{2,6},{6,2},{3,7},{7,3},{8,12},{12,8},{9,1... | collective-permute-start | bytes 786440 | tf_op jit(solution)/shard_map/ppermute | solution.py:18
  531.5 7.6 %collective-permute-start.79 = (bf16[512,256]{0,1:T(8,128)(2,1)S(1)}, bf16[512,256]{0,1:T(8,128)(2,1)S(1)}, u32[]{:S(2)}, u32[]{:S(2)}) collective-permute-start(bf16[512,256]{0,1:T(8,128)(2,1)S(1)} %get-tuple-element.82), channel_id=1, source_target_pairs={{0,8},{8,0},{16,24},{24,16},{32,40},{40,32},{48,56},{56,48},{64,72... | collective-permute-start | bytes 786440 | tf_op jit(solution)/shard_map/ppermute | solution.py:18
  539.1 8.8 %collective-permute-start.80 = (bf16[512,256]{0,1:T(8,128)(2,1)S(1)}, bf16[512,256]{0,1:T(8,128)(2,1)S(1)}, u32[]{:S(2)}, u32[]{:S(2)}) collective-permute-start(bf16[512,256]{0,1:T(8,128)(2,1)S(1)} %fusion.59), channel_id=1, source_target_pairs={{0,16},{16,0},{8,24},{24,8},{32,48},{48,32},{40,56},{56,40},{64,80... | collective-permute-start | bytes 786440 | tf_op jit(solution)/shard_map/ppermute | solution.py:18
  566.8 13.2 %collective-permute-start.85 = (bf16[1024,256]{0,1:T(8,128)(2,1)S(1)}, bf16[1024,256]{0,1:T(8,128)(2,1)S(1)}, u32[]{:S(2)}, u32[]{:S(2)}) collective-permute-start(bf16[1024,256]{0,1:T(8,128)(2,1)S(1)} %fusion.17), channel_id=1, source_target_pairs={{0,2},{2,0},{1,3},{3,1},{4,6},{6,4},{5,7},{7,5},{8,10},{10,8},{9,1... | collective-permute-start | bytes 1572872 | tf_op jit(solution)/shard_map/ppermute | solution.py:18
  580.2 13.8 %collective-permute-start.86 = (bf16[1024,256]{0,1:T(8,128)(2,1)S(1)}, bf16[1024,256]{0,1:T(8,128)(2,1)S(1)}, u32[]{:S(2)}, u32[]{:S(2)}) collective-permute-start(bf16[1024,256]{0,1:T(8,128)(2,1)S(1)} %add_convert_fusion.1), channel_id=1, source_target_pairs={{0,4},{4,0},{1,5},{5,1},{2,6},{6,2},{3,7},{7,3},{8,12},{12,8},{9,1... | collective-permute-start | bytes 1572872 | tf_op jit(solution)/shard_map/ppermute | solution.py:18
  598.9 7.6 %collective-permute-start.88 = (bf16[512,256]{0,1:T(8,128)(2,1)S(1)}, bf16[512,256]{0,1:T(8,128)(2,1)S(1)}, u32[]{:S(2)}, u32[]{:S(2)}) collective-permute-start(bf16[512,256]{0,1:T(8,128)(2,1)S(1)} %get-tuple-element.84), channel_id=1, source_target_pairs={{0,8},{8,0},{16,24},{24,16},{32,40},{40,32},{48,56},{56,48},{64,72... | collective-permute-start | bytes 786440 | tf_op jit(solution)/shard_map/ppermute | solution.py:18
  (94 other events, 660.1 us)

commit v6 on v5

--- a/solution.py
+++ b/solution.py
@@ -192,7 +192,9 @@
             sibling = partner(carried, "leaf", height - 1)
         else:
             sibling = exchange_round(own_pieces, levels, position, height - 1, carried)
-        pair_blocks = front_gather(jnp.stack([carried, sibling]))
+        pair_blocks = jnp.concatenate(
+            [front_gather(carried[None]), front_gather(sibling[None])], 0
+        )
         pair_lists = jnp.stack(
             [list_row(extend_lists, own_child), list_row(extend_lists, own_child ^ 1)]
         )[:, jnp.array(gathered_order(fronts), jnp.int32)]

time: 633 us -> 623 us (0.984)
  waiting for transfers between devices: 349 us -> 303 us
  starting transfers between devices: 195 us -> 217 us
  other arithmetic: 24.4 us -> 34.2 us
    ppermute x92 -> x107, waiting for transfers between devices: 349 us -> 303 us  [partner(): return lax.ppermute(block, axis, route)]
    ppermute x92 -> x107, starting transfers between devices: 195 us -> 217 us  [partner(): return lax.ppermute(block, axis, route)]
  transfers between devices with their start and end apart: 92 -> 107, of which waited for: 84 -> 87; matrix products, arithmetic and copies ran while one was open for 4% -> 7% of each run, Pallas kernels for 0% -> 0%
where the time goes in v6:
time: 623 us; the launch traced here: 612 us
  waiting for transfers between devices  303 us (49%)
  starting transfers between devices  217 us (35%)
  other arithmetic  34.2 us (5%)
  local copies, waits for them, and re-layouts  32.6 us (5%)
  matrix products  21.7 us (3%)
    ppermute x107, waiting for transfers between devices, partner(): return lax.ppermute(block, axis, route)  303 us
    ppermute x107, starting transfers between devices, partner(): return lax.ppermute(block, axis, route)  217 us
  transfers between devices with their start and end apart: 107, of which 87 were waited for; matrix products, arithmetic and copies ran while one was open for 7% of the time, Pallas kernels for 0%

profile of v6, /device:TPU:1, one launch (start us, length us, event | category | flops | bytes accessed | tf_op | source)
XLA Modules:
  0.0 611.7 jit_solution(10217774995892843667)
XLA Ops:
  38.6 12.8 %collective-permute-done.9 = bf16[1024,256]{0,1:T(8,128)(2,1)S(1)} collective-permute-done((bf16[1024,256]{0,1:T(8,128)(2,1)S(1)}, bf16[1024,256]{0,1:T(8,128)(2,1)S(1)}, u32[]{:S(2)}, u32[]{:S(2)}) %collective-permute-start.9) | collective-permute-done | bytes 524320 | tf_op jit(solution)/shard_map/ppermute | solution.py:18
  53.7 11.8 %collective-permute-done.10 = bf16[1024,256]{0,1:T(8,128)(2,1)S(1)} collective-permute-done((bf16[1024,256]{0,1:T(8,128)(2,1)S(1)}, bf16[1024,256]{0,1:T(8,128)(2,1)S(1)}, u32[]{:S(2)}, u32[]{:S(2)}) %collective-permute-start.10) | collective-permute-done | bytes 524320 | tf_op jit(solution)/shard_map/ppermute | solution.py:18
  164.4 7.5 %collective-permute-done.34 = bf16[512,256]{0,1:T(8,128)(2,1)S(1)} collective-permute-done((bf16[512,256]{0,1:T(8,128)(2,1)S(1)}, bf16[512,256]{0,1:T(8,128)(2,1)S(1)}, u32[]{:S(2)}, u32[]{:S(2)}) %collective-permute-start.34) | collective-permute-done | bytes 262176 | tf_op jit(solution)/shard_map/ppermute | solution.py:18
  175.0 5.2 collective-permute-done.35
  211.1 7.4 %collective-permute-start.42 = (bf16[1,512,256]{2,1,0:T(8,128)(2,1)S(1)}, bf16[1,512,256]{2,1,0:T(8,128)(2,1)S(1)}, u32[]{:S(2)}, u32[]{:S(2)}) collective-permute-start(bf16[1,512,256]{2,1,0:T(8,128)(2,1)S(1)} %maximum_select_fusion.36), channel_id=1, source_target_pairs={{0,1},{1,0},{2,3},{3,2},{4,5},{5,4},{6,7},{7,6},{8,9},{9,8},{10,11... | collective-permute-start | bytes 786440 | tf_op jit(solution)/shard_map/ppermute | solution.py:18
  256.6 6.6 %collective-permute-start.53 = (bf16[384,256]{1,0:T(8,128)(2,1)S(1)}, bf16[384,256]{1,0:T(8,128)(2,1)S(1)}, u32[]{:S(2)}, u32[]{:S(2)}) collective-permute-start(bf16[384,256]{1,0:T(8,128)(2,1)S(1)} %pad_maximum_fusion.11), channel_id=1, source_target_pairs={{0,128},{128,0},{8,136},{136,8},{16,144},{144,16},{24,152},{152,24... | collective-permute-start | bytes 589832 | tf_op jit(solution)/shard_map/ppermute | solution.py:18
  268.5 12.0 %collective-permute-start.56 = (bf16[1,512,256]{2,1,0:T(8,128)(2,1)S(1)}, bf16[1,512,256]{2,1,0:T(8,128)(2,1)S(1)}, u32[]{:S(2)}, u32[]{:S(2)}) collective-permute-start(bf16[1,512,256]{2,1,0:T(8,128)(2,1)S(1)} %maximum_select_fusion.41), channel_id=1, source_target_pairs={{0,1},{1,0},{2,3},{3,2},{4,5},{5,4},{6,7},{7,6},{8,9},{9,8},{10,11... | collective-permute-start | bytes 786440 | tf_op jit(solution)/shard_map/ppermute | solution.py:18
  284.6 6.4 %collective-permute-start.59 = (bf16[1,512,256]{2,1,0:T(8,128)(2,1)S(1)}, bf16[1,512,256]{2,1,0:T(8,128)(2,1)S(1)}, u32[]{:S(2)}, u32[]{:S(2)}) collective-permute-start(bf16[1,512,256]{2,1,0:T(8,128)(2,1)S(1)} %maximum_select_fusion.43), channel_id=1, source_target_pairs={{0,1},{1,0},{2,3},{3,2},{4,5},{5,4},{6,7},{7,6},{8,9},{9,8},{10,11... | collective-permute-start | bytes 786440 | tf_op jit(solution)/shard_map/ppermute | solution.py:18
  312.5 6.7 %collective-permute-done.64 = bf16[512,256]{0,1:T(8,128)(2,1)S(1)} collective-permute-done((bf16[512,256]{0,1:T(8,128)(2,1)S(1)}, bf16[512,256]{0,1:T(8,128)(2,1)S(1)}, u32[]{:S(2)}, u32[]{:S(2)}) %collective-permute-start.64) | collective-permute-done | bytes 262176 | tf_op jit(solution)/shard_map/ppermute | solution.py:18
  319.4 5.2 collective-permute-done.65
  324.8 8.6 %collective-permute-done.66 = bf16[512,256]{0,1:T(8,128)(2,1)S(1)} collective-permute-done((bf16[512,256]{0,1:T(8,128)(2,1)S(1)}, bf16[512,256]{0,1:T(8,128)(2,1)S(1)}, u32[]{:S(2)}, u32[]{:S(2)}) %collective-permute-start.66) | collective-permute-done | bytes 262176 | tf_op jit(solution)/shard_map/ppermute | solution.py:18
  337.3 6.9 %collective-permute-done.67 = bf16[512,256]{0,1:T(8,128)(2,1)S(1)} collective-permute-done((bf16[512,256]{0,1:T(8,128)(2,1)S(1)}, bf16[512,256]{0,1:T(8,128)(2,1)S(1)}, u32[]{:S(2)}, u32[]{:S(2)}) %collective-permute-start.67) | collective-permute-done | bytes 262176 | tf_op jit(solution)/shard_map/ppermute | solution.py:18
  346.3 10.1 %collective-permute-start.68 = (bf16[2,2,128,256]{2,3,0,1:T(8,128)(2,1)S(1)}, bf16[2,2,128,256]{2,3,0,1:T(8,128)(2,1)S(1)}, u32[]{:S(2)}, u32[]{:S(2)}) collective-permute-start(bf16[2,2,128,256]{2,3,0,1:T(8,128)(2,1)S(1)} %bitcast.269), channel_id=1, source_target_pairs={{0,1},{1,0},{2,3},{3,2},{4,5},{5,4},{6,7},{7,6},{8,9},{9,8},{10,11... | collective-permute-start | bytes 786440 | tf_op jit(solution)/shard_map/ppermute | solution.py:18
  357.7 6.8 %collective-permute-start.69 = (bf16[2,128,256]{1,2,0:T(8,128)(2,1)S(1)}, bf16[2,128,256]{1,2,0:T(8,128)(2,1)S(1)}, u32[]{:S(2)}, u32[]{:S(2)}) collective-permute-start(bf16[2,128,256]{1,2,0:T(8,128)(2,1)S(1)} %dynamic-slice_bitcast_fusion.4), channel_id=1, source_target_pairs={{0,2},{2,0},{1,3},{3,1},{4,6},{6,4},{5,7},{7,5},{8,10},{10,8},{9,1... | collective-permute-start | bytes 393224 | tf_op jit(solution)/shard_map/ppermute | solution.py:18
  368.1 5.4 collective-permute-start.70
  390.5 6.1 collective-permute-done.74
  397.6 5.9 collective-permute-done.75
  403.7 5.2 collective-permute-done.76
  409.8 8.0 %collective-permute-done.77 = bf16[512,256]{0,1:T(8,128)(2,1)S(1)} collective-permute-done((bf16[512,256]{0,1:T(8,128)(2,1)S(1)}, bf16[512,256]{0,1:T(8,128)(2,1)S(1)}, u32[]{:S(2)}, u32[]{:S(2)}) %collective-permute-start.77) | collective-permute-done | bytes 262176 | tf_op jit(solution)/shard_map/ppermute | solution.py:18
  420.0 6.5 %collective-permute-start.78 = (bf16[2,2,128,256]{2,3,0,1:T(8,128)(2,1)S(1)}, bf16[2,2,128,256]{2,3,0,1:T(8,128)(2,1)S(1)}, u32[]{:S(2)}, u32[]{:S(2)}) collective-permute-start(bf16[2,2,128,256]{2,3,0,1:T(8,128)(2,1)S(1)} %bitcast.270), channel_id=1, source_target_pairs={{0,1},{1,0},{2,3},{3,2},{4,5},{5,4},{6,7},{7,6},{8,9},{9,8},{10,11... | collective-permute-start | bytes 786440 | tf_op jit(solution)/shard_map/ppermute | solution.py:18
  442.6 6.6 %collective-permute-done.82 = bf16[512,256]{0,1:T(8,128)(2,1)S(1)} collective-permute-done((bf16[512,256]{0,1:T(8,128)(2,1)S(1)}, bf16[512,256]{0,1:T(8,128)(2,1)S(1)}, u32[]{:S(2)}, u32[]{:S(2)}) %collective-permute-start.82) | collective-permute-done | bytes 262176 | tf_op jit(solution)/shard_map/ppermute | solution.py:18
  452.6 5.5 collective-permute-done.83
  459.5 6.0 collective-permute-done.84
  467.2 5.3 collective-permute-done.85
  472.7 5.2 collective-permute-done.86
  501.2 6.6 %collective-permute-done.91 = bf16[512,256]{0,1:T(8,128)(2,1)S(1)} collective-permute-done((bf16[512,256]{0,1:T(8,128)(2,1)S(1)}, bf16[512,256]{0,1:T(8,128)(2,1)S(1)}, u32[]{:S(2)}, u32[]{:S(2)}) %collective-permute-start.91) | collective-permute-done | bytes 262176 | tf_op jit(solution)/shard_map/ppermute | solution.py:18
  511.0 5.2 collective-permute-done.92
  521.4 7.5 %collective-permute-done.94 = bf16[512,256]{0,1:T(8,128)(2,1)S(1)} collective-permute-done((bf16[512,256]{0,1:T(8,128)(2,1)S(1)}, bf16[512,256]{0,1:T(8,128)(2,1)S(1)}, u32[]{:S(2)}, u32[]{:S(2)}) %collective-permute-start.94) | collective-permute-done | bytes 262176 | tf_op jit(solution)/shard_map/ppermute | solution.py:18
  530.1 7.0 %collective-permute-done.95 = bf16[512,256]{0,1:T(8,128)(2,1)S(1)} collective-permute-done((bf16[512,256]{0,1:T(8,128)(2,1)S(1)}, bf16[512,256]{0,1:T(8,128)(2,1)S(1)}, u32[]{:S(2)}, u32[]{:S(2)}) %collective-permute-start.95) | collective-permute-done | bytes 262176 | tf_op jit(solution)/shard_map/ppermute | solution.py:18
  557.2 12.3 %collective-permute-done.100 = bf16[1024,256]{0,1:T(8,128)(2,1)S(1)} collective-permute-done((bf16[1024,256]{0,1:T(8,128)(2,1)S(1)}, bf16[1024,256]{0,1:T(8,128)(2,1)S(1)}, u32[]{:S(2)}, u32[]{:S(2)}) %collective-permute-start.100) | collective-permute-done | bytes 524320 | tf_op jit(solution)/shard_map/ppermute | solution.py:18
  572.7 10.8 %collective-permute-done.101 = bf16[1024,256]{0,1:T(8,128)(2,1)S(1)} collective-permute-done((bf16[1024,256]{0,1:T(8,128)(2,1)S(1)}, bf16[1024,256]{0,1:T(8,128)(2,1)S(1)}, u32[]{:S(2)}, u32[]{:S(2)}) %collective-permute-start.101) | collective-permute-done | bytes 524320 | tf_op jit(solution)/shard_map/ppermute | solution.py:18
  588.8 7.2 %collective-permute-done.103 = bf16[512,256]{0,1:T(8,128)(2,1)S(1)} collective-permute-done((bf16[512,256]{0,1:T(8,128)(2,1)S(1)}, bf16[512,256]{0,1:T(8,128)(2,1)S(1)}, u32[]{:S(2)}, u32[]{:S(2)}) %collective-permute-start.103) | collective-permute-done | bytes 262176 | tf_op jit(solution)/shard_map/ppermute | solution.py:18
  (550 shorter events, 372.3 us)
Async XLA Ops:
  0.6 13.5 %collective-permute-start.4 = (bf16[128,256]{1,0:T(8,128)(2,1)}, bf16[128,256]{1,0:T(8,128)(2,1)S(1)}, u32[]{:S(2)}, u32[]{:S(2)}) collective-permute-start(bf16[128,256]{1,0:T(8,128)(2,1)} %param.10), channel_id=1, source_target_pairs={{0,8},{8,0},{16,24},{24,16},{32,40},{40,32},{48,56},{56,48},{64,72... | collective-permute-start | bytes 196616 | tf_op jit(solution)/shard_map/ppermute | solution.py:18
  2.8 11.5 %collective-permute-start.1 = (bf16[1,128,256]{2,1,0:T(8,128)(2,1)}, bf16[1,128,256]{2,1,0:T(8,128)(2,1)S(1)}, u32[]{:S(2)}, u32[]{:S(2)}) collective-permute-start(bf16[1,128,256]{2,1,0:T(8,128)(2,1)} %bitcast.273), channel_id=1, source_target_pairs={{0,4},{4,0},{1,5},{5,1},{2,6},{6,2},{3,7},{7,3},{8,12},{12,8},{9,1... | collective-permute-start | bytes 196616 | tf_op jit(solution)/shard_map/ppermute | solution.py:18
  9.8 17.7 %collective-permute-start = (bf16[496,256]{1,0:T(8,128)(2,1)S(1)}, bf16[496,256]{1,0:T(8,128)(2,1)S(1)}, u32[]{:S(2)}, u32[]{:S(2)}) collective-permute-start(bf16[496,256]{1,0:T(8,128)(2,1)S(1)} %constant_dynamic-update-slice_fusion), channel_id=1, source_target_pairs={{0,8},{8,0},{16,24},{24,16},{32,40},{40,32},{48,56},{56,48},{64,72... | collective-permute-start | bytes 761864 | tf_op jit(solution)/shard_map/ppermute | solution.py:18
  19.9 8.4 %collective-permute-start.3 = (bf16[1,512,256]{2,1,0:T(8,128)(2,1)S(1)}, bf16[1,512,256]{2,1,0:T(8,128)(2,1)S(1)}, u32[]{:S(2)}, u32[]{:S(2)}) collective-permute-start(bf16[1,512,256]{2,1,0:T(8,128)(2,1)S(1)} %maximum_select_fusion.21), channel_id=1, source_target_pairs={{0,1},{1,0},{2,3},{3,2},{4,5},{5,4},{6,7},{7,6},{8,9},{9,8},{10,11... | collective-permute-start | bytes 786440 | tf_op jit(solution)/shard_map/ppermute | solution.py:18
  38.2 13.2 %collective-permute-start.9 = (bf16[1024,256]{0,1:T(8,128)(2,1)S(1)}, bf16[1024,256]{0,1:T(8,128)(2,1)S(1)}, u32[]{:S(2)}, u32[]{:S(2)}) collective-permute-start(bf16[1024,256]{0,1:T(8,128)(2,1)S(1)} %fusion.18), channel_id=1, source_target_pairs={{0,2},{2,0},{1,3},{3,1},{4,6},{6,4},{5,7},{7,5},{8,10},{10,8},{9,1... | collective-permute-start | bytes 1572872 | tf_op jit(solution)/shard_map/ppermute | solution.py:18
  51.6 13.9 %collective-permute-start.10 = (bf16[1024,256]{0,1:T(8,128)(2,1)S(1)}, bf16[1024,256]{0,1:T(8,128)(2,1)S(1)}, u32[]{:S(2)}, u32[]{:S(2)}) collective-permute-start(bf16[1024,256]{0,1:T(8,128)(2,1)S(1)} %add_convert_fusion.3), channel_id=1, source_target_pairs={{0,4},{4,0},{1,5},{5,1},{2,6},{6,2},{3,7},{7,3},{8,12},{12,8},{9,1... | collective-permute-start | bytes 1572872 | tf_op jit(solution)/shard_map/ppermute | solution.py:18
  76.0 9.8 %collective-permute-start.13 = (bf16[608,256]{1,0:T(8,128)(2,1)S(1)}, bf16[608,256]{1,0:T(8,128)(2,1)S(1)}, u32[]{:S(2)}, u32[]{:S(2)}) collective-permute-start(bf16[608,256]{1,0:T(8,128)(2,1)S(1)} %get-tuple-element.32), channel_id=1, source_target_pairs={{0,16},{16,0},{8,24},{24,8},{32,48},{48,32},{40,56},{56,40},{64,80... | collective-permute-start | bytes 933896 | tf_op jit(solution)/shard_map/ppermute | solution.py:18
  106.8 7.6 %collective-permute-start.21 = (bf16[512,256]{0,1:T(8,128)(2,1)S(1)}, bf16[512,256]{0,1:T(8,128)(2,1)S(1)}, u32[]{:S(2)}, u32[]{:S(2)}) collective-permute-start(bf16[512,256]{0,1:T(8,128)(2,1)S(1)} %fusion.46), channel_id=1, source_target_pairs={{0,2},{2,0},{1,3},{3,1},{4,6},{6,4},{5,7},{7,5},{8,10},{10,8},{9,1... | collective-permute-start | bytes 786440 | tf_op jit(solution)/shard_map/ppermute | solution.py:18
  114.4 8.2 %collective-permute-start.22 = (bf16[512,256]{0,1:T(8,128)(2,1)S(1)}, bf16[512,256]{0,1:T(8,128)(2,1)S(1)}, u32[]{:S(2)}, u32[]{:S(2)}) collective-permute-start(bf16[512,256]{0,1:T(8,128)(2,1)S(1)} %add_convert_fusion.11), channel_id=1, source_target_pairs={{0,4},{4,0},{1,5},{5,1},{2,6},{6,2},{3,7},{7,3},{8,12},{12,8},{9,1... | collective-permute-start | bytes 786440 | tf_op jit(solution)/shard_map/ppermute | solution.py:18
  147.7 10.4 %collective-permute-start.29 = (bf16[1,512,256]{2,1,0:T(8,128)(2,1)S(1)}, bf16[1,512,256]{2,1,0:T(8,128)(2,1)S(1)}, u32[]{:S(2)}, u32[]{:S(2)}) collective-permute-start(bf16[1,512,256]{2,1,0:T(8,128)(2,1)S(1)} %maximum_select_fusion.31), channel_id=1, source_target_pairs={{0,1},{1,0},{2,3},{3,2},{4,5},{5,4},{6,7},{7,6},{8,9},{9,8},{10,11... | collective-permute-start | bytes 786440 | tf_op jit(solution)/shard_map/ppermute | solution.py:18
  164.3 7.6 %collective-permute-start.34 = (bf16[512,256]{0,1:T(8,128)(2,1)S(1)}, bf16[512,256]{0,1:T(8,128)(2,1)S(1)}, u32[]{:S(2)}, u32[]{:S(2)}) collective-permute-start(bf16[512,256]{0,1:T(8,128)(2,1)S(1)} %add_convert_fusion.9), channel_id=1, source_target_pairs={{0,2},{2,0},{1,3},{3,1},{4,6},{6,4},{5,7},{7,5},{8,10},{10,8},{9,1... | collective-permute-start | bytes 786440 | tf_op jit(solution)/shard_map/ppermute | solution.py:18
  171.9 8.2 %collective-permute-start.35 = (bf16[512,256]{0,1:T(8,128)(2,1)S(1)}, bf16[512,256]{0,1:T(8,128)(2,1)S(1)}, u32[]{:S(2)}, u32[]{:S(2)}) collective-permute-start(bf16[512,256]{0,1:T(8,128)(2,1)S(1)} %add_convert_fusion.8), channel_id=1, source_target_pairs={{0,4},{4,0},{1,5},{5,1},{2,6},{6,2},{3,7},{7,3},{8,12},{12,8},{9,1... | collective-permute-start | bytes 786440 | tf_op jit(solution)/shard_map/ppermute | solution.py:18
  194.7 9.7 %collective-permute-start.39 = (bf16[512,256]{1,0:T(8,128)(2,1)S(1)}, bf16[512,256]{1,0:T(8,128)(2,1)S(1)}, u32[]{:S(2)}, u32[]{:S(2)}) collective-permute-start(bf16[512,256]{1,0:T(8,128)(2,1)S(1)} %pad_maximum_fusion.10), channel_id=1, source_target_pairs={{0,64},{64,0},{8,72},{72,8},{16,80},{80,16},{24,88},{88,24},{32,96... | collective-permute-start | bytes 786440 | tf_op jit(solution)/shard_map/ppermute | solution.py:18
  210.4 8.1 %collective-permute-start.44 = (bf16[1,256,256]{2,1,0:T(8,128)(2,1)S(1)}, bf16[1,256,256]{2,1,0:T(8,128)(2,1)S(1)}, u32[]{:S(2)}, u32[]{:S(2)}) collective-permute-start(bf16[1,256,256]{2,1,0:T(8,128)(2,1)S(1)} %maximum_select_fusion.64), channel_id=1, source_target_pairs={{0,2},{2,0},{1,3},{3,1},{4,6},{6,4},{5,7},{7,5},{8,10},{10,8},{9,1... | collective-permute-start | bytes 393224 | tf_op jit(solution)/shard_map/ppermute | solution.py:18
  211.1 12.5 %collective-permute-start.42 = (bf16[1,512,256]{2,1,0:T(8,128)(2,1)S(1)}, bf16[1,512,256]{2,1,0:T(8,128)(2,1)S(1)}, u32[]{:S(2)}, u32[]{:S(2)}) collective-permute-start(bf16[1,512,256]{2,1,0:T(8,128)(2,1)S(1)} %maximum_select_fusion.36), channel_id=1, source_target_pairs={{0,1},{1,0},{2,3},{3,2},{4,5},{5,4},{6,7},{7,6},{8,9},{9,8},{10,11... | collective-permute-start | bytes 786440 | tf_op jit(solution)/shard_map/ppermute | solution.py:18
  255.2 8.0 %collective-permute-start.54 = (bf16[1,128,256]{2,1,0:T(8,128)(2,1)S(1)}, bf16[1,128,256]{2,1,0:T(8,128)(2,1)S(1)}, u32[]{:S(2)}, u32[]{:S(2)}) collective-permute-start(bf16[1,128,256]{2,1,0:T(8,128)(2,1)S(1)} %bitcast.252), channel_id=1, source_target_pairs={{0,4},{4,0},{1,5},{5,1},{2,6},{6,2},{3,7},{7,3},{8,12},{12,8},{9,1... | collective-permute-start | bytes 196616 | tf_op jit(solution)/shard_map/ppermute | solution.py:18
  256.6 10.5 %collective-permute-start.53 = (bf16[384,256]{1,0:T(8,128)(2,1)S(1)}, bf16[384,256]{1,0:T(8,128)(2,1)S(1)}, u32[]{:S(2)}, u32[]{:S(2)}) collective-permute-start(bf16[384,256]{1,0:T(8,128)(2,1)S(1)} %pad_maximum_fusion.11), channel_id=1, source_target_pairs={{0,128},{128,0},{8,136},{136,8},{16,144},{144,16},{24,152},{152,24... | collective-permute-start | bytes 589832 | tf_op jit(solution)/shard_map/ppermute | solution.py:18
  267.1 13.5 %collective-permute-start.57 = (bf16[1,128,256]{2,1,0:T(8,128)(2,1)S(1)}, bf16[1,128,256]{2,1,0:T(8,128)(2,1)S(1)}, u32[]{:S(2)}, u32[]{:S(2)}) collective-permute-start(bf16[1,128,256]{2,1,0:T(8,128)(2,1)S(1)} %get-tuple-element.61), channel_id=1, source_target_pairs={{0,4},{4,0},{1,5},{5,1},{2,6},{6,2},{3,7},{7,3},{8,12},{12,8},{9,1... | collective-permute-start | bytes 196616 | tf_op jit(solution)/shard_map/ppermute | solution.py:18
  268.5 22.7 %collective-permute-start.56 = (bf16[1,512,256]{2,1,0:T(8,128)(2,1)S(1)}, bf16[1,512,256]{2,1,0:T(8,128)(2,1)S(1)}, u32[]{:S(2)}, u32[]{:S(2)}) collective-permute-start(bf16[1,512,256]{2,1,0:T(8,128)(2,1)S(1)} %maximum_select_fusion.41), channel_id=1, source_target_pairs={{0,1},{1,0},{2,3},{3,2},{4,5},{5,4},{6,7},{7,6},{8,9},{9,8},{10,11... | collective-permute-start | bytes 786440 | tf_op jit(solution)/shard_map/ppermute | solution.py:18
  324.7 8.7 %collective-permute-start.66 = (bf16[512,256]{0,1:T(8,128)(2,1)S(1)}, bf16[512,256]{0,1:T(8,128)(2,1)S(1)}, u32[]{:S(2)}, u32[]{:S(2)}) collective-permute-start(bf16[512,256]{0,1:T(8,128)(2,1)S(1)} %fusion.55), channel_id=1, source_target_pairs={{0,64},{64,0},{8,72},{72,8},{16,80},{80,16},{24,88},{88,24},{32,96... | collective-permute-start | bytes 786440 | tf_op jit(solution)/shard_map/ppermute | solution.py:18
  333.5 10.6 %collective-permute-start.67 = (bf16[512,256]{0,1:T(8,128)(2,1)S(1)}, bf16[512,256]{0,1:T(8,128)(2,1)S(1)}, u32[]{:S(2)}, u32[]{:S(2)}) collective-permute-start(bf16[512,256]{0,1:T(8,128)(2,1)S(1)} %fusion.94), channel_id=1, source_target_pairs={{0,128},{128,0},{8,136},{136,8},{16,144},{144,16},{24,152},{152,24... | collective-permute-start | bytes 786440 | tf_op jit(solution)/shard_map/ppermute | solution.py:18
  346.3 11.3 %collective-permute-start.68 = (bf16[2,2,128,256]{2,3,0,1:T(8,128)(2,1)S(1)}, bf16[2,2,128,256]{2,3,0,1:T(8,128)(2,1)S(1)}, u32[]{:S(2)}, u32[]{:S(2)}) collective-permute-start(bf16[2,2,128,256]{2,3,0,1:T(8,128)(2,1)S(1)} %bitcast.269), channel_id=1, source_target_pairs={{0,1},{1,0},{2,3},{3,2},{4,5},{5,4},{6,7},{7,6},{8,9},{9,8},{10,11... | collective-permute-start | bytes 786440 | tf_op jit(solution)/shard_map/ppermute | solution.py:18
  357.7 10.3 %collective-permute-start.69 = (bf16[2,128,256]{1,2,0:T(8,128)(2,1)S(1)}, bf16[2,128,256]{1,2,0:T(8,128)(2,1)S(1)}, u32[]{:S(2)}, u32[]{:S(2)}) collective-permute-start(bf16[2,128,256]{1,2,0:T(8,128)(2,1)S(1)} %dynamic-slice_bitcast_fusion.4), channel_id=1, source_target_pairs={{0,2},{2,0},{1,3},{3,1},{4,6},{6,4},{5,7},{7,5},{8,10},{10,8},{9,1... | collective-permute-start | bytes 393224 | tf_op jit(solution)/shard_map/ppermute | solution.py:18
  409.0 8.7 %collective-permute-start.77 = (bf16[512,256]{0,1:T(8,128)(2,1)S(1)}, bf16[512,256]{0,1:T(8,128)(2,1)S(1)}, u32[]{:S(2)}, u32[]{:S(2)}) collective-permute-start(bf16[512,256]{0,1:T(8,128)(2,1)S(1)} %fusion.57), channel_id=1, source_target_pairs={{0,64},{64,0},{8,72},{72,8},{16,80},{80,16},{24,88},{88,24},{32,96... | collective-permute-start | bytes 786440 | tf_op jit(solution)/shard_map/ppermute | solution.py:18
  420.0 7.7 %collective-permute-start.78 = (bf16[2,2,128,256]{2,3,0,1:T(8,128)(2,1)S(1)}, bf16[2,2,128,256]{2,3,0,1:T(8,128)(2,1)S(1)}, u32[]{:S(2)}, u32[]{:S(2)}) collective-permute-start(bf16[2,2,128,256]{2,3,0,1:T(8,128)(2,1)S(1)} %bitcast.270), channel_id=1, source_target_pairs={{0,1},{1,0},{2,3},{3,2},{4,5},{5,4},{6,7},{7,6},{8,9},{9,8},{10,11... | collective-permute-start | bytes 786440 | tf_op jit(solution)/shard_map/ppermute | solution.py:18
  449.3 8.8 %collective-permute-start.83 = (bf16[512,256]{0,1:T(8,128)(2,1)S(1)}, bf16[512,256]{0,1:T(8,128)(2,1)S(1)}, u32[]{:S(2)}, u32[]{:S(2)}) collective-permute-start(bf16[512,256]{0,1:T(8,128)(2,1)S(1)} %add_convert_fusion.6), channel_id=1, source_target_pairs={{0,4},{4,0},{1,5},{5,1},{2,6},{6,2},{3,7},{7,3},{8,12},{12,8},{9,1... | collective-permute-start | bytes 786440 | tf_op jit(solution)/shard_map/ppermute | solution.py:18
  500.3 7.6 %collective-permute-start.91 = (bf16[512,256]{0,1:T(8,128)(2,1)S(1)}, bf16[512,256]{0,1:T(8,128)(2,1)S(1)}, u32[]{:S(2)}, u32[]{:S(2)}) collective-permute-start(bf16[512,256]{0,1:T(8,128)(2,1)S(1)} %fusion.45), channel_id=1, source_target_pairs={{0,2},{2,0},{1,3},{3,1},{4,6},{6,4},{5,7},{7,5},{8,10},{10,8},{9,1... | collective-permute-start | bytes 786440 | tf_op jit(solution)/shard_map/ppermute | solution.py:18
  507.9 8.3 %collective-permute-start.92 = (bf16[512,256]{0,1:T(8,128)(2,1)S(1)}, bf16[512,256]{0,1:T(8,128)(2,1)S(1)}, u32[]{:S(2)}, u32[]{:S(2)}) collective-permute-start(bf16[512,256]{0,1:T(8,128)(2,1)S(1)} %add_convert_fusion.5), channel_id=1, source_target_pairs={{0,4},{4,0},{1,5},{5,1},{2,6},{6,2},{3,7},{7,3},{8,12},{12,8},{9,1... | collective-permute-start | bytes 786440 | tf_op jit(solution)/shard_map/ppermute | solution.py:18
  529.0 8.2 %collective-permute-start.95 = (bf16[512,256]{0,1:T(8,128)(2,1)S(1)}, bf16[512,256]{0,1:T(8,128)(2,1)S(1)}, u32[]{:S(2)}, u32[]{:S(2)}) collective-permute-start(bf16[512,256]{0,1:T(8,128)(2,1)S(1)} %fusion.59), channel_id=1, source_target_pairs={{0,16},{16,0},{8,24},{24,8},{32,48},{48,32},{40,56},{56,40},{64,80... | collective-permute-start | bytes 786440 | tf_op jit(solution)/shard_map/ppermute | solution.py:18
  556.3 13.2 %collective-permute-start.100 = (bf16[1024,256]{0,1:T(8,128)(2,1)S(1)}, bf16[1024,256]{0,1:T(8,128)(2,1)S(1)}, u32[]{:S(2)}, u32[]{:S(2)}) collective-permute-start(bf16[1024,256]{0,1:T(8,128)(2,1)S(1)} %fusion.17), channel_id=1, source_target_pairs={{0,2},{2,0},{1,3},{3,1},{4,6},{6,4},{5,7},{7,5},{8,10},{10,8},{9,1... | collective-permute-start | bytes 1572872 | tf_op jit(solution)/shard_map/ppermute | solution.py:18
  569.7 13.8 %collective-permute-start.101 = (bf16[1024,256]{0,1:T(8,128)(2,1)S(1)}, bf16[1024,256]{0,1:T(8,128)(2,1)S(1)}, u32[]{:S(2)}, u32[]{:S(2)}) collective-permute-start(bf16[1024,256]{0,1:T(8,128)(2,1)S(1)} %add_convert_fusion.1), channel_id=1, source_target_pairs={{0,4},{4,0},{1,5},{5,1},{2,6},{6,2},{3,7},{7,3},{8,12},{12,8},{9,1... | collective-permute-start | bytes 1572872 | tf_op jit(solution)/shard_map/ppermute | solution.py:18
  588.2 7.8 %collective-permute-start.103 = (bf16[512,256]{0,1:T(8,128)(2,1)S(1)}, bf16[512,256]{0,1:T(8,128)(2,1)S(1)}, u32[]{:S(2)}, u32[]{:S(2)}) collective-permute-start(bf16[512,256]{0,1:T(8,128)(2,1)S(1)} %get-tuple-element.89), channel_id=1, source_target_pairs={{0,8},{8,0},{16,24},{24,16},{32,40},{40,32},{48,56},{56,48},{64,72... | collective-permute-start | bytes 786440 | tf_op jit(solution)/shard_map/ppermute | solution.py:18
  (112 other events, 932.5 us)

commit v7 on v6

--- a/solution.py
+++ b/solution.py
@@ -68,7 +68,7 @@
 
 def front_sum(summand):
     bits = lax.axis_size("front").bit_length() - 1
-    if summand.shape[0] < 1024:
+    if summand.shape[0] < 512:
         for bit_index in range(bits):
             half = summand.astype(jnp.bfloat16)
             summand = half.astype(jnp.float32) + partner(half, "front", bit_index).astype(

time: 623 us -> 617 us (level)
    ppermute x107 -> x109, starting transfers between devices: 217 us -> 215 us  [partner(): return lax.ppermute(block, axis, route)]
    ppermute x107 -> x109, waiting for transfers between devices: 303 us -> 303 us  [partner(): return lax.ppermute(block, axis, route)]
  transfers between devices with their start and end apart: 107 -> 109, of which waited for: 87 -> 89; matrix products, arithmetic and copies ran while one was open for 7% -> 7% of each run, Pallas kernels for 0% -> 0%
where the time goes in v7:
time: 617 us; the launch traced here: 606 us
  waiting for transfers between devices  303 us (49%)
  starting transfers between devices  215 us (35%)
  other arithmetic  32.6 us (5%)
  local copies, waits for them, and re-layouts  31.4 us (5%)
  matrix products  21.2 us (3%)
    ppermute x109, waiting for transfers between devices, partner(): return lax.ppermute(block, axis, route)  303 us
    ppermute x109, starting transfers between devices, partner(): return lax.ppermute(block, axis, route)  215 us
  transfers between devices with their start and end apart: 109, of which 89 were waited for; matrix products, arithmetic and copies ran while one was open for 7% of the time, Pallas kernels for 0%

profile of v7, /device:TPU:1, one launch (start us, length us, event | category | flops | bytes accessed | tf_op | source)
XLA Modules:
  0.0 605.9 jit_solution(661797242405144823)
XLA Ops:
  19.7 5.1 collective-permute-start.3
  38.3 12.8 %collective-permute-done.9 = bf16[1024,256]{0,1:T(8,128)(2,1)S(1)} collective-permute-done((bf16[1024,256]{0,1:T(8,128)(2,1)S(1)}, bf16[1024,256]{0,1:T(8,128)(2,1)S(1)}, u32[]{:S(2)}, u32[]{:S(2)}) %collective-permute-start.9) | collective-permute-done | bytes 524320 | tf_op jit(solution)/shard_map/ppermute | solution.py:18
  53.4 11.8 %collective-permute-done.10 = bf16[1024,256]{0,1:T(8,128)(2,1)S(1)} collective-permute-done((bf16[1024,256]{0,1:T(8,128)(2,1)S(1)}, bf16[1024,256]{0,1:T(8,128)(2,1)S(1)}, u32[]{:S(2)}, u32[]{:S(2)}) %collective-permute-start.10) | collective-permute-done | bytes 524320 | tf_op jit(solution)/shard_map/ppermute | solution.py:18
  117.4 5.1 collective-permute-done.22
  195.5 9.8 %collective-permute-done.40 = bf16[512,256]{1,0:T(8,128)(2,1)S(1)} collective-permute-done((bf16[512,256]{1,0:T(8,128)(2,1)S(1)}, bf16[512,256]{1,0:T(8,128)(2,1)S(1)}, u32[]{:S(2)}, u32[]{:S(2)}) %collective-permute-start.40) | collective-permute-done | bytes 262176 | tf_op jit(solution)/shard_map/ppermute | solution.py:18
  225.7 4.7 collective-permute-done.48
  231.0 4.8 collective-permute-done.49
  252.6 6.4 %collective-permute-start.54 = (bf16[384,256]{1,0:T(8,128)(2,1)S(1)}, bf16[384,256]{1,0:T(8,128)(2,1)S(1)}, u32[]{:S(2)}, u32[]{:S(2)}) collective-permute-start(bf16[384,256]{1,0:T(8,128)(2,1)S(1)} %pad_maximum_fusion.11), channel_id=1, source_target_pairs={{0,128},{128,0},{8,136},{136,8},{16,144},{144,16},{24,152},{152,24... | collective-permute-start | bytes 589832 | tf_op jit(solution)/shard_map/ppermute | solution.py:18
  264.7 12.1 %collective-permute-start.57 = (bf16[1,512,256]{2,1,0:T(8,128)(2,1)S(1)}, bf16[1,512,256]{2,1,0:T(8,128)(2,1)S(1)}, u32[]{:S(2)}, u32[]{:S(2)}) collective-permute-start(bf16[1,512,256]{2,1,0:T(8,128)(2,1)S(1)} %maximum_select_fusion.42), channel_id=1, source_target_pairs={{0,1},{1,0},{2,3},{3,2},{4,5},{5,4},{6,7},{7,6},{8,9},{9,8},{10,11... | collective-permute-start | bytes 786440 | tf_op jit(solution)/shard_map/ppermute | solution.py:18
  300.0 5.0 collective-permute-done.64
  307.0 5.0 collective-permute-done.65
  312.2 5.2 collective-permute-done.66
  319.8 6.7 %collective-permute-done.67 = bf16[512,256]{0,1:T(8,128)(2,1)S(1)} collective-permute-done((bf16[512,256]{0,1:T(8,128)(2,1)S(1)}, bf16[512,256]{0,1:T(8,128)(2,1)S(1)}, u32[]{:S(2)}, u32[]{:S(2)}) %collective-permute-start.67) | collective-permute-done | bytes 262176 | tf_op jit(solution)/shard_map/ppermute | solution.py:18
  326.6 5.6 collective-permute-start.68
  332.2 7.5 %collective-permute-done.68 = bf16[512,256]{0,1:T(8,128)(2,1)S(1)} collective-permute-done((bf16[512,256]{0,1:T(8,128)(2,1)S(1)}, bf16[512,256]{0,1:T(8,128)(2,1)S(1)}, u32[]{:S(2)}, u32[]{:S(2)}) %collective-permute-start.68) | collective-permute-done | bytes 262176 | tf_op jit(solution)/shard_map/ppermute | solution.py:18
  341.9 14.0 %collective-permute-start.69 = (bf16[2,2,128,256]{2,3,0,1:T(8,128)(2,1)S(1)}, bf16[2,2,128,256]{2,3,0,1:T(8,128)(2,1)S(1)}, u32[]{:S(2)}, u32[]{:S(2)}) collective-permute-start(bf16[2,2,128,256]{2,3,0,1:T(8,128)(2,1)S(1)} %bitcast.277), channel_id=1, source_target_pairs={{0,1},{1,0},{2,3},{3,2},{4,5},{5,4},{6,7},{7,6},{8,9},{9,8},{10,11... | collective-permute-start | bytes 786440 | tf_op jit(solution)/shard_map/ppermute | solution.py:18
  370.6 4.7 collective-permute-done.73
  383.8 5.1 collective-permute-done.75
  391.7 5.4 collective-permute-done.76
  397.4 5.2 collective-permute-done.77
  402.8 12.8 %collective-permute-done.78 = bf16[512,256]{0,1:T(8,128)(2,1)S(1)} collective-permute-done((bf16[512,256]{0,1:T(8,128)(2,1)S(1)}, bf16[512,256]{0,1:T(8,128)(2,1)S(1)}, u32[]{:S(2)}, u32[]{:S(2)}) %collective-permute-start.78) | collective-permute-done | bytes 262176 | tf_op jit(solution)/shard_map/ppermute | solution.py:18
  451.2 6.2 %collective-permute-done.86 = bf16[512,256]{0,1:T(8,128)(2,1)S(1)} collective-permute-done((bf16[512,256]{0,1:T(8,128)(2,1)S(1)}, bf16[512,256]{0,1:T(8,128)(2,1)S(1)}, u32[]{:S(2)}, u32[]{:S(2)}) %collective-permute-start.86) | collective-permute-done | bytes 262176 | tf_op jit(solution)/shard_map/ppermute | solution.py:18
  457.4 4.8 collective-permute-start.87
  462.3 5.7 collective-permute-done.87
  468.3 6.3 %collective-permute-done.88 = bf16[512,256]{0,1:T(8,128)(2,1)S(1)} collective-permute-done((bf16[512,256]{0,1:T(8,128)(2,1)S(1)}, bf16[512,256]{0,1:T(8,128)(2,1)S(1)}, u32[]{:S(2)}, u32[]{:S(2)}) %collective-permute-start.88) | collective-permute-done | bytes 262176 | tf_op jit(solution)/shard_map/ppermute | solution.py:18
  495.1 7.1 %collective-permute-done.93 = bf16[512,256]{0,1:T(8,128)(2,1)S(1)} collective-permute-done((bf16[512,256]{0,1:T(8,128)(2,1)S(1)}, bf16[512,256]{0,1:T(8,128)(2,1)S(1)}, u32[]{:S(2)}, u32[]{:S(2)}) %collective-permute-start.93) | collective-permute-done | bytes 262176 | tf_op jit(solution)/shard_map/ppermute | solution.py:18
  505.6 5.5 collective-permute-done.94
  516.2 7.2 %collective-permute-done.96 = bf16[512,256]{0,1:T(8,128)(2,1)S(1)} collective-permute-done((bf16[512,256]{0,1:T(8,128)(2,1)S(1)}, bf16[512,256]{0,1:T(8,128)(2,1)S(1)}, u32[]{:S(2)}, u32[]{:S(2)}) %collective-permute-start.96) | collective-permute-done | bytes 262176 | tf_op jit(solution)/shard_map/ppermute | solution.py:18
  526.3 5.4 collective-permute-done.97
  551.3 12.7 %collective-permute-done.102 = bf16[1024,256]{0,1:T(8,128)(2,1)S(1)} collective-permute-done((bf16[1024,256]{0,1:T(8,128)(2,1)S(1)}, bf16[1024,256]{0,1:T(8,128)(2,1)S(1)}, u32[]{:S(2)}, u32[]{:S(2)}) %collective-permute-start.102) | collective-permute-done | bytes 524320 | tf_op jit(solution)/shard_map/ppermute | solution.py:18
  567.3 10.8 %collective-permute-done.103 = bf16[1024,256]{0,1:T(8,128)(2,1)S(1)} collective-permute-done((bf16[1024,256]{0,1:T(8,128)(2,1)S(1)}, bf16[1024,256]{0,1:T(8,128)(2,1)S(1)}, u32[]{:S(2)}, u32[]{:S(2)}) %collective-permute-start.103) | collective-permute-done | bytes 524320 | tf_op jit(solution)/shard_map/ppermute | solution.py:18
  583.3 7.2 %collective-permute-done.105 = bf16[512,256]{0,1:T(8,128)(2,1)S(1)} collective-permute-done((bf16[512,256]{0,1:T(8,128)(2,1)S(1)}, bf16[512,256]{0,1:T(8,128)(2,1)S(1)}, u32[]{:S(2)}, u32[]{:S(2)}) %collective-permute-start.105) | collective-permute-done | bytes 262176 | tf_op jit(solution)/shard_map/ppermute | solution.py:18
  (558 shorter events, 369.4 us)
Async XLA Ops:
  0.6 13.3 %collective-permute-start.4 = (bf16[128,256]{1,0:T(8,128)(2,1)}, bf16[128,256]{1,0:T(8,128)(2,1)S(1)}, u32[]{:S(2)}, u32[]{:S(2)}) collective-permute-start(bf16[128,256]{1,0:T(8,128)(2,1)} %param.10), channel_id=1, source_target_pairs={{0,8},{8,0},{16,24},{24,16},{32,40},{40,32},{48,56},{56,48},{64,72... | collective-permute-start | bytes 196616 | tf_op jit(solution)/shard_map/ppermute | solution.py:18
  2.8 11.2 %collective-permute-start.1 = (bf16[1,128,256]{2,1,0:T(8,128)(2,1)}, bf16[1,128,256]{2,1,0:T(8,128)(2,1)S(1)}, u32[]{:S(2)}, u32[]{:S(2)}) collective-permute-start(bf16[1,128,256]{2,1,0:T(8,128)(2,1)} %bitcast.281), channel_id=1, source_target_pairs={{0,4},{4,0},{1,5},{5,1},{2,6},{6,2},{3,7},{7,3},{8,12},{12,8},{9,1... | collective-permute-start | bytes 196616 | tf_op jit(solution)/shard_map/ppermute | solution.py:18
  9.8 17.4 %collective-permute-start = (bf16[496,256]{1,0:T(8,128)(2,1)S(1)}, bf16[496,256]{1,0:T(8,128)(2,1)S(1)}, u32[]{:S(2)}, u32[]{:S(2)}) collective-permute-start(bf16[496,256]{1,0:T(8,128)(2,1)S(1)} %constant_dynamic-update-slice_fusion), channel_id=1, source_target_pairs={{0,8},{8,0},{16,24},{24,16},{32,40},{40,32},{48,56},{56,48},{64,72... | collective-permute-start | bytes 761864 | tf_op jit(solution)/shard_map/ppermute | solution.py:18
  19.7 8.4 %collective-permute-start.3 = (bf16[1,512,256]{2,1,0:T(8,128)(2,1)S(1)}, bf16[1,512,256]{2,1,0:T(8,128)(2,1)S(1)}, u32[]{:S(2)}, u32[]{:S(2)}) collective-permute-start(bf16[1,512,256]{2,1,0:T(8,128)(2,1)S(1)} %maximum_select_fusion.21), channel_id=1, source_target_pairs={{0,1},{1,0},{2,3},{3,2},{4,5},{5,4},{6,7},{7,6},{8,9},{9,8},{10,11... | collective-permute-start | bytes 786440 | tf_op jit(solution)/shard_map/ppermute | solution.py:18
  37.9 13.2 %collective-permute-start.9 = (bf16[1024,256]{0,1:T(8,128)(2,1)S(1)}, bf16[1024,256]{0,1:T(8,128)(2,1)S(1)}, u32[]{:S(2)}, u32[]{:S(2)}) collective-permute-start(bf16[1024,256]{0,1:T(8,128)(2,1)S(1)} %fusion.16), channel_id=1, source_target_pairs={{0,2},{2,0},{1,3},{3,1},{4,6},{6,4},{5,7},{7,5},{8,10},{10,8},{9,1... | collective-permute-start | bytes 1572872 | tf_op jit(solution)/shard_map/ppermute | solution.py:18
  51.3 13.9 %collective-permute-start.10 = (bf16[1024,256]{0,1:T(8,128)(2,1)S(1)}, bf16[1024,256]{0,1:T(8,128)(2,1)S(1)}, u32[]{:S(2)}, u32[]{:S(2)}) collective-permute-start(bf16[1024,256]{0,1:T(8,128)(2,1)S(1)} %add_convert_fusion.3), channel_id=1, source_target_pairs={{0,4},{4,0},{1,5},{5,1},{2,6},{6,2},{3,7},{7,3},{8,12},{12,8},{9,1... | collective-permute-start | bytes 1572872 | tf_op jit(solution)/shard_map/ppermute | solution.py:18
  75.7 10.0 %collective-permute-start.13 = (bf16[608,256]{1,0:T(8,128)(2,1)S(1)}, bf16[608,256]{1,0:T(8,128)(2,1)S(1)}, u32[]{:S(2)}, u32[]{:S(2)}) collective-permute-start(bf16[608,256]{1,0:T(8,128)(2,1)S(1)} %get-tuple-element.32), channel_id=1, source_target_pairs={{0,16},{16,0},{8,24},{24,8},{32,48},{48,32},{40,56},{56,40},{64,80... | collective-permute-start | bytes 933896 | tf_op jit(solution)/shard_map/ppermute | solution.py:18
  91.9 7.3 %collective-permute-start.16 = (bf16[1,512,256]{2,1,0:T(8,128)(2,1)S(1)}, bf16[1,512,256]{2,1,0:T(8,128)(2,1)S(1)}, u32[]{:S(2)}, u32[]{:S(2)}) collective-permute-start(bf16[1,512,256]{2,1,0:T(8,128)(2,1)S(1)} %maximum_select_fusion.26), channel_id=1, source_target_pairs={{0,1},{1,0},{2,3},{3,2},{4,5},{5,4},{6,7},{7,6},{8,9},{9,8},{10,11... | collective-permute-start | bytes 786440 | tf_op jit(solution)/shard_map/ppermute | solution.py:18
  106.6 7.6 %collective-permute-start.21 = (bf16[512,256]{0,1:T(8,128)(2,1)S(1)}, bf16[512,256]{0,1:T(8,128)(2,1)S(1)}, u32[]{:S(2)}, u32[]{:S(2)}) collective-permute-start(bf16[512,256]{0,1:T(8,128)(2,1)S(1)} %fusion.44), channel_id=1, source_target_pairs={{0,2},{2,0},{1,3},{3,1},{4,6},{6,4},{5,7},{7,5},{8,10},{10,8},{9,1... | collective-permute-start | bytes 786440 | tf_op jit(solution)/shard_map/ppermute | solution.py:18
  114.3 8.2 %collective-permute-start.22 = (bf16[512,256]{0,1:T(8,128)(2,1)S(1)}, bf16[512,256]{0,1:T(8,128)(2,1)S(1)}, u32[]{:S(2)}, u32[]{:S(2)}) collective-permute-start(bf16[512,256]{0,1:T(8,128)(2,1)S(1)} %add_convert_fusion.7), channel_id=1, source_target_pairs={{0,4},{4,0},{1,5},{5,1},{2,6},{6,2},{3,7},{7,3},{8,12},{12,8},{9,1... | collective-permute-start | bytes 786440 | tf_op jit(solution)/shard_map/ppermute | solution.py:18
  149.0 9.3 %collective-permute-start.29 = (bf16[1,512,256]{2,1,0:T(8,128)(2,1)S(1)}, bf16[1,512,256]{2,1,0:T(8,128)(2,1)S(1)}, u32[]{:S(2)}, u32[]{:S(2)}) collective-permute-start(bf16[1,512,256]{2,1,0:T(8,128)(2,1)S(1)} %maximum_select_fusion.31), channel_id=1, source_target_pairs={{0,1},{1,0},{2,3},{3,2},{4,5},{5,4},{6,7},{7,6},{8,9},{9,8},{10,11... | collective-permute-start | bytes 786440 | tf_op jit(solution)/shard_map/ppermute | solution.py:18
  191.3 14.1 %collective-permute-start.40 = (bf16[512,256]{1,0:T(8,128)(2,1)S(1)}, bf16[512,256]{1,0:T(8,128)(2,1)S(1)}, u32[]{:S(2)}, u32[]{:S(2)}) collective-permute-start(bf16[512,256]{1,0:T(8,128)(2,1)S(1)} %pad_maximum_fusion.10), channel_id=1, source_target_pairs={{0,64},{64,0},{8,72},{72,8},{16,80},{80,16},{24,88},{88,24},{32,96... | collective-permute-start | bytes 786440 | tf_op jit(solution)/shard_map/ppermute | solution.py:18
  195.4 11.1 %collective-permute-start.42 = (bf16[1,256,256]{2,1,0:T(8,128)(2,1)S(1)}, bf16[1,256,256]{2,1,0:T(8,128)(2,1)S(1)}, u32[]{:S(2)}, u32[]{:S(2)}) collective-permute-start(bf16[1,256,256]{2,1,0:T(8,128)(2,1)S(1)} %maximum_select_fusion.65), channel_id=1, source_target_pairs={{0,2},{2,0},{1,3},{3,1},{4,6},{6,4},{5,7},{7,5},{8,10},{10,8},{9,1... | collective-permute-start | bytes 393224 | tf_op jit(solution)/shard_map/ppermute | solution.py:18
  211.3 9.0 %collective-permute-start.43 = (bf16[1,512,256]{2,1,0:T(8,128)(2,1)S(1)}, bf16[1,512,256]{2,1,0:T(8,128)(2,1)S(1)}, u32[]{:S(2)}, u32[]{:S(2)}) collective-permute-start(bf16[1,512,256]{2,1,0:T(8,128)(2,1)S(1)} %maximum_select_fusion.37), channel_id=1, source_target_pairs={{0,1},{1,0},{2,3},{3,2},{4,5},{5,4},{6,7},{7,6},{8,9},{9,8},{10,11... | collective-permute-start | bytes 786440 | tf_op jit(solution)/shard_map/ppermute | solution.py:18
  251.8 7.3 %collective-permute-start.55 = (bf16[1,128,256]{2,1,0:T(8,128)(2,1)S(1)}, bf16[1,128,256]{2,1,0:T(8,128)(2,1)S(1)}, u32[]{:S(2)}, u32[]{:S(2)}) collective-permute-start(bf16[1,128,256]{2,1,0:T(8,128)(2,1)S(1)} %bitcast.260), channel_id=1, source_target_pairs={{0,4},{4,0},{1,5},{5,1},{2,6},{6,2},{3,7},{7,3},{8,12},{12,8},{9,1... | collective-permute-start | bytes 196616 | tf_op jit(solution)/shard_map/ppermute | solution.py:18
  252.6 10.3 %collective-permute-start.54 = (bf16[384,256]{1,0:T(8,128)(2,1)S(1)}, bf16[384,256]{1,0:T(8,128)(2,1)S(1)}, u32[]{:S(2)}, u32[]{:S(2)}) collective-permute-start(bf16[384,256]{1,0:T(8,128)(2,1)S(1)} %pad_maximum_fusion.11), channel_id=1, source_target_pairs={{0,128},{128,0},{8,136},{136,8},{16,144},{144,16},{24,152},{152,24... | collective-permute-start | bytes 589832 | tf_op jit(solution)/shard_map/ppermute | solution.py:18
  263.0 13.8 %collective-permute-start.58 = (bf16[1,128,256]{2,1,0:T(8,128)(2,1)S(1)}, bf16[1,128,256]{2,1,0:T(8,128)(2,1)S(1)}, u32[]{:S(2)}, u32[]{:S(2)}) collective-permute-start(bf16[1,128,256]{2,1,0:T(8,128)(2,1)S(1)} %get-tuple-element.61), channel_id=1, source_target_pairs={{0,4},{4,0},{1,5},{5,1},{2,6},{6,2},{3,7},{7,3},{8,12},{12,8},{9,1... | collective-permute-start | bytes 196616 | tf_op jit(solution)/shard_map/ppermute | solution.py:18
  264.7 19.8 %collective-permute-start.57 = (bf16[1,512,256]{2,1,0:T(8,128)(2,1)S(1)}, bf16[1,512,256]{2,1,0:T(8,128)(2,1)S(1)}, u32[]{:S(2)}, u32[]{:S(2)}) collective-permute-start(bf16[1,512,256]{2,1,0:T(8,128)(2,1)S(1)} %maximum_select_fusion.42), channel_id=1, source_target_pairs={{0,1},{1,0},{2,3},{3,2},{4,5},{5,4},{6,7},{7,6},{8,9},{9,8},{10,11... | collective-permute-start | bytes 786440 | tf_op jit(solution)/shard_map/ppermute | solution.py:18
  317.4 9.1 %collective-permute-start.67 = (bf16[512,256]{0,1:T(8,128)(2,1)S(1)}, bf16[512,256]{0,1:T(8,128)(2,1)S(1)}, u32[]{:S(2)}, u32[]{:S(2)}) collective-permute-start(bf16[512,256]{0,1:T(8,128)(2,1)S(1)} %fusion.53), channel_id=1, source_target_pairs={{0,64},{64,0},{8,72},{72,8},{16,80},{80,16},{24,88},{88,24},{32,96... | collective-permute-start | bytes 786440 | tf_op jit(solution)/shard_map/ppermute | solution.py:18
  326.6 13.1 %collective-permute-start.68 = (bf16[512,256]{0,1:T(8,128)(2,1)S(1)}, bf16[512,256]{0,1:T(8,128)(2,1)S(1)}, u32[]{:S(2)}, u32[]{:S(2)}) collective-permute-start(bf16[512,256]{0,1:T(8,128)(2,1)S(1)} %fusion.99), channel_id=1, source_target_pairs={{0,128},{128,0},{8,136},{136,8},{16,144},{144,16},{24,152},{152,24... | collective-permute-start | bytes 786440 | tf_op jit(solution)/shard_map/ppermute | solution.py:18
  341.9 15.2 %collective-permute-start.69 = (bf16[2,2,128,256]{2,3,0,1:T(8,128)(2,1)S(1)}, bf16[2,2,128,256]{2,3,0,1:T(8,128)(2,1)S(1)}, u32[]{:S(2)}, u32[]{:S(2)}) collective-permute-start(bf16[2,2,128,256]{2,3,0,1:T(8,128)(2,1)S(1)} %bitcast.277), channel_id=1, source_target_pairs={{0,1},{1,0},{2,3},{3,2},{4,5},{5,4},{6,7},{7,6},{8,9},{9,8},{10,11... | collective-permute-start | bytes 786440 | tf_op jit(solution)/shard_map/ppermute | solution.py:18
  388.9 8.3 %collective-permute-start.76 = (bf16[512,256]{0,1:T(8,128)(2,1)S(1)}, bf16[512,256]{0,1:T(8,128)(2,1)S(1)}, u32[]{:S(2)}, u32[]{:S(2)}) collective-permute-start(bf16[512,256]{0,1:T(8,128)(2,1)S(1)} %fusion.54), channel_id=1, source_target_pairs={{0,16},{16,0},{8,24},{24,8},{32,48},{48,32},{40,56},{56,40},{64,80... | collective-permute-start | bytes 786440 | tf_op jit(solution)/shard_map/ppermute | solution.py:18
  402.7 12.9 %collective-permute-start.78 = (bf16[512,256]{0,1:T(8,128)(2,1)S(1)}, bf16[512,256]{0,1:T(8,128)(2,1)S(1)}, u32[]{:S(2)}, u32[]{:S(2)}) collective-permute-start(bf16[512,256]{0,1:T(8,128)(2,1)S(1)} %fusion.55), channel_id=1, source_target_pairs={{0,64},{64,0},{8,72},{72,8},{16,80},{80,16},{24,88},{88,24},{32,96... | collective-permute-start | bytes 786440 | tf_op jit(solution)/shard_map/ppermute | solution.py:18
  449.8 7.6 %collective-permute-start.86 = (bf16[512,256]{0,1:T(8,128)(2,1)S(1)}, bf16[512,256]{0,1:T(8,128)(2,1)S(1)}, u32[]{:S(2)}, u32[]{:S(2)}) collective-permute-start(bf16[512,256]{0,1:T(8,128)(2,1)S(1)} %get-tuple-element.85), channel_id=1, source_target_pairs={{0,8},{8,0},{16,24},{24,16},{32,40},{40,32},{48,56},{56,48},{64,72... | collective-permute-start | bytes 786440 | tf_op jit(solution)/shard_map/ppermute | solution.py:18
  457.4 10.6 %collective-permute-start.87 = (bf16[512,256]{0,1:T(8,128)(2,1)S(1)}, bf16[512,256]{0,1:T(8,128)(2,1)S(1)}, u32[]{:S(2)}, u32[]{:S(2)}) collective-permute-start(bf16[512,256]{0,1:T(8,128)(2,1)S(1)} %fusion.56), channel_id=1, source_target_pairs={{0,16},{16,0},{8,24},{24,8},{32,48},{48,32},{40,56},{56,40},{64,80... | collective-permute-start | bytes 786440 | tf_op jit(solution)/shard_map/ppermute | solution.py:18
  494.6 7.6 %collective-permute-start.93 = (bf16[512,256]{0,1:T(8,128)(2,1)S(1)}, bf16[512,256]{0,1:T(8,128)(2,1)S(1)}, u32[]{:S(2)}, u32[]{:S(2)}) collective-permute-start(bf16[512,256]{0,1:T(8,128)(2,1)S(1)} %fusion.43), channel_id=1, source_target_pairs={{0,2},{2,0},{1,3},{3,1},{4,6},{6,4},{5,7},{7,5},{8,10},{10,8},{9,1... | collective-permute-start | bytes 786440 | tf_op jit(solution)/shard_map/ppermute | solution.py:18
  502.2 8.8 %collective-permute-start.94 = (bf16[512,256]{0,1:T(8,128)(2,1)S(1)}, bf16[512,256]{0,1:T(8,128)(2,1)S(1)}, u32[]{:S(2)}, u32[]{:S(2)}) collective-permute-start(bf16[512,256]{0,1:T(8,128)(2,1)S(1)} %add_convert_fusion.5), channel_id=1, source_target_pairs={{0,4},{4,0},{1,5},{5,1},{2,6},{6,2},{3,7},{7,3},{8,12},{12,8},{9,1... | collective-permute-start | bytes 786440 | tf_op jit(solution)/shard_map/ppermute | solution.py:18
  515.8 7.6 %collective-permute-start.96 = (bf16[512,256]{0,1:T(8,128)(2,1)S(1)}, bf16[512,256]{0,1:T(8,128)(2,1)S(1)}, u32[]{:S(2)}, u32[]{:S(2)}) collective-permute-start(bf16[512,256]{0,1:T(8,128)(2,1)S(1)} %get-tuple-element.87), channel_id=1, source_target_pairs={{0,8},{8,0},{16,24},{24,16},{32,40},{40,32},{48,56},{56,48},{64,72... | collective-permute-start | bytes 786440 | tf_op jit(solution)/shard_map/ppermute | solution.py:18
  523.5 8.2 %collective-permute-start.97 = (bf16[512,256]{0,1:T(8,128)(2,1)S(1)}, bf16[512,256]{0,1:T(8,128)(2,1)S(1)}, u32[]{:S(2)}, u32[]{:S(2)}) collective-permute-start(bf16[512,256]{0,1:T(8,128)(2,1)S(1)} %fusion.57), channel_id=1, source_target_pairs={{0,16},{16,0},{8,24},{24,8},{32,48},{48,32},{40,56},{56,40},{64,80... | collective-permute-start | bytes 786440 | tf_op jit(solution)/shard_map/ppermute | solution.py:18
  550.9 13.2 %collective-permute-start.102 = (bf16[1024,256]{0,1:T(8,128)(2,1)S(1)}, bf16[1024,256]{0,1:T(8,128)(2,1)S(1)}, u32[]{:S(2)}, u32[]{:S(2)}) collective-permute-start(bf16[1024,256]{0,1:T(8,128)(2,1)S(1)} %fusion.15), channel_id=1, source_target_pairs={{0,2},{2,0},{1,3},{3,1},{4,6},{6,4},{5,7},{7,5},{8,10},{10,8},{9,1... | collective-permute-start | bytes 1572872 | tf_op jit(solution)/shard_map/ppermute | solution.py:18
  564.2 13.8 %collective-permute-start.103 = (bf16[1024,256]{0,1:T(8,128)(2,1)S(1)}, bf16[1024,256]{0,1:T(8,128)(2,1)S(1)}, u32[]{:S(2)}, u32[]{:S(2)}) collective-permute-start(bf16[1024,256]{0,1:T(8,128)(2,1)S(1)} %add_convert_fusion.1), channel_id=1, source_target_pairs={{0,4},{4,0},{1,5},{5,1},{2,6},{6,2},{3,7},{7,3},{8,12},{12,8},{9,1... | collective-permute-start | bytes 1572872 | tf_op jit(solution)/shard_map/ppermute | solution.py:18
  582.9 7.6 %collective-permute-start.105 = (bf16[512,256]{0,1:T(8,128)(2,1)S(1)}, bf16[512,256]{0,1:T(8,128)(2,1)S(1)}, u32[]{:S(2)}, u32[]{:S(2)}) collective-permute-start(bf16[512,256]{0,1:T(8,128)(2,1)S(1)} %get-tuple-element.89), channel_id=1, source_target_pairs={{0,8},{8,0},{16,24},{24,16},{32,40},{40,32},{48,56},{56,48},{64,72... | collective-permute-start | bytes 786440 | tf_op jit(solution)/shard_map/ppermute | solution.py:18
  (114 other events, 938.8 us)

commit v8 on v7

--- a/solution.py
+++ b/solution.py
@@ -93,14 +93,8 @@
 
 def front_gather(blocks):
     bits = lax.axis_size("front").bit_length() - 1
-    column = lax.axis_index("front")
     for bit_index in reversed(range(bits)):
-        received = partner(blocks, "front", bit_index)
-        blocks = jnp.where(
-            upper_bit(column, bit_index),
-            jnp.concatenate([received, blocks], 1),
-            jnp.concatenate([blocks, received], 1),
-        )
+        blocks = jnp.concatenate([blocks, partner(blocks, "front", bit_index)], 1)
     return blocks
 
 
@@ -197,7 +191,7 @@
         )
         pair_lists = jnp.stack(
             [list_row(extend_lists, own_child), list_row(extend_lists, own_child ^ 1)]
-        )[:, jnp.array(gathered_order(fronts), jnp.int32)]
+        )[:, column ^ jnp.array(gathered_order(fronts), jnp.int32)]
         chooser = (pair_lists.reshape(2 * block_count)[None, :] == local_blocks[:, None]).astype(
             jnp.bfloat16
         )

time: 617 us -> 616 us (level)
  starting transfers between devices: 215 us -> 193 us
  waiting for transfers between devices: 303 us -> 322 us
    ppermute x109, starting transfers between devices: 215 us -> 193 us  [partner(): return lax.ppermute(block, axis, route)]
    ppermute x109, waiting for transfers between devices: 303 us -> 322 us  [partner(): return lax.ppermute(block, axis, route)]
  transfers between devices with their start and end apart: 109 -> 109, of which waited for: 89 -> 84; matrix products, arithmetic and copies ran while one was open for 7% -> 6% of each run, Pallas kernels for 0% -> 0%
where the time goes in v8:
time: 616 us; the launch traced here: 605 us
  waiting for transfers between devices  322 us (52%)
  starting transfers between devices  193 us (31%)
  local copies, waits for them, and re-layouts  33.6 us (5%)
  other arithmetic  32.9 us (5%)
  matrix products  21.2 us (3%)
    ppermute x109, waiting for transfers between devices, partner(): return lax.ppermute(block, axis, route)  322 us
    ppermute x109, starting transfers between devices, partner(): return lax.ppermute(block, axis, route)  193 us
  transfers between devices with their start and end apart: 109, of which 84 were waited for; matrix products, arithmetic and copies ran while one was open for 6% of the time, Pallas kernels for 0%

profile of v8, /device:TPU:1, one launch (start us, length us, event | category | flops | bytes accessed | tf_op | source)
XLA Modules:
  0.0 605.2 jit_solution(12760645128470025949)
XLA Ops:
  19.2 5.2 collective-permute-start.3
  37.4 13.0 %collective-permute-done.9 = bf16[1024,256]{0,1:T(8,128)(2,1)S(1)} collective-permute-done((bf16[1024,256]{0,1:T(8,128)(2,1)S(1)}, bf16[1024,256]{0,1:T(8,128)(2,1)S(1)}, u32[]{:S(2)}, u32[]{:S(2)}) %collective-permute-start.9) | collective-permute-done | bytes 524320 | tf_op jit(solution)/shard_map/ppermute | solution.py:18
  52.7 12.0 %collective-permute-done.10 = bf16[1024,256]{0,1:T(8,128)(2,1)S(1)} collective-permute-done((bf16[1024,256]{0,1:T(8,128)(2,1)S(1)}, bf16[1024,256]{0,1:T(8,128)(2,1)S(1)}, u32[]{:S(2)}, u32[]{:S(2)}) %collective-permute-start.10) | collective-permute-done | bytes 524320 | tf_op jit(solution)/shard_map/ppermute | solution.py:18
  78.8 5.7 collective-permute-done.13
  106.6 7.4 %collective-permute-done.21 = bf16[512,256]{0,1:T(8,128)(2,1)S(1)} collective-permute-done((bf16[512,256]{0,1:T(8,128)(2,1)S(1)}, bf16[512,256]{0,1:T(8,128)(2,1)S(1)}, u32[]{:S(2)}, u32[]{:S(2)}) %collective-permute-start.21) | collective-permute-done | bytes 262176 | tf_op jit(solution)/shard_map/ppermute | solution.py:18
  117.0 5.3 collective-permute-done.22
  150.4 5.3 collective-permute-start.29
  193.8 10.8 %collective-permute-done.40 = bf16[512,256]{1,0:T(8,128)(2,1)S(1)} collective-permute-done((bf16[512,256]{1,0:T(8,128)(2,1)S(1)}, bf16[512,256]{1,0:T(8,128)(2,1)S(1)}, u32[]{:S(2)}, u32[]{:S(2)}) %collective-permute-start.40) | collective-permute-done | bytes 262176 | tf_op jit(solution)/shard_map/ppermute | solution.py:18
  232.2 5.3 collective-permute-done.49
  253.8 6.2 %collective-permute-start.54 = (bf16[384,256]{1,0:T(8,128)(2,1)S(1)}, bf16[384,256]{1,0:T(8,128)(2,1)S(1)}, u32[]{:S(2)}, u32[]{:S(2)}) collective-permute-start(bf16[384,256]{1,0:T(8,128)(2,1)S(1)} %pad_maximum_fusion.16), channel_id=1, source_target_pairs={{0,128},{128,0},{8,136},{136,8},{16,144},{144,16},{24,152},{152,24... | collective-permute-start | bytes 589832 | tf_op jit(solution)/shard_map/ppermute | solution.py:18
  270.4 11.8 %collective-permute-start.57 = (bf16[1,512,256]{2,1,0:T(8,128)(2,1)S(1)}, bf16[1,512,256]{2,1,0:T(8,128)(2,1)S(1)}, u32[]{:S(2)}, u32[]{:S(2)}) collective-permute-start(bf16[1,512,256]{2,1,0:T(8,128)(2,1)S(1)} %pad_maximum_fusion.14), channel_id=1, source_target_pairs={{0,1},{1,0},{2,3},{3,2},{4,5},{5,4},{6,7},{7,6},{8,9},{9,8},{10,11... | collective-permute-start | bytes 786440 | tf_op jit(solution)/shard_map/ppermute | solution.py:18
  302.8 4.7 collective-permute-done.64
  320.8 9.0 %collective-permute-done.67 = bf16[512,256]{0,1:T(8,128)(2,1)S(1)} collective-permute-done((bf16[512,256]{0,1:T(8,128)(2,1)S(1)}, bf16[512,256]{0,1:T(8,128)(2,1)S(1)}, u32[]{:S(2)}, u32[]{:S(2)}) %collective-permute-start.67) | collective-permute-done | bytes 262176 | tf_op jit(solution)/shard_map/ppermute | solution.py:18
  329.9 5.7 collective-permute-start.68
  335.5 6.4 %collective-permute-done.68 = bf16[512,256]{0,1:T(8,128)(2,1)S(1)} collective-permute-done((bf16[512,256]{0,1:T(8,128)(2,1)S(1)}, bf16[512,256]{0,1:T(8,128)(2,1)S(1)}, u32[]{:S(2)}, u32[]{:S(2)}) %collective-permute-start.68) | collective-permute-done | bytes 262176 | tf_op jit(solution)/shard_map/ppermute | solution.py:18
  344.1 13.6 %collective-permute-start.69 = (bf16[2,2,128,256]{2,3,0,1:T(8,128)(2,1)S(1)}, bf16[2,2,128,256]{2,3,0,1:T(8,128)(2,1)S(1)}, u32[]{:S(2)}, u32[]{:S(2)}) collective-permute-start(bf16[2,2,128,256]{2,3,0,1:T(8,128)(2,1)S(1)} %bitcast.223), channel_id=1, source_target_pairs={{0,1},{1,0},{2,3},{3,2},{4,5},{5,4},{6,7},{7,6},{8,9},{9,8},{10,11... | collective-permute-start | bytes 786440 | tf_op jit(solution)/shard_map/ppermute | solution.py:18
  377.4 5.1 collective-permute-done.74
  391.7 5.0 collective-permute-done.76
  397.0 5.2 collective-permute-done.77
  403.0 8.5 %collective-permute-done.78 = bf16[512,256]{0,1:T(8,128)(2,1)S(1)} collective-permute-done((bf16[512,256]{0,1:T(8,128)(2,1)S(1)}, bf16[512,256]{0,1:T(8,128)(2,1)S(1)}, u32[]{:S(2)}, u32[]{:S(2)}) %collective-permute-start.78) | collective-permute-done | bytes 262176 | tf_op jit(solution)/shard_map/ppermute | solution.py:18
  413.8 6.4 %collective-permute-start.79 = (bf16[2,2,128,256]{2,3,0,1:T(8,128)(2,1)S(1)}, bf16[2,2,128,256]{2,3,0,1:T(8,128)(2,1)S(1)}, u32[]{:S(2)}, u32[]{:S(2)}) collective-permute-start(bf16[2,2,128,256]{2,3,0,1:T(8,128)(2,1)S(1)} %bitcast.224), channel_id=1, source_target_pairs={{0,1},{1,0},{2,3},{3,2},{4,5},{5,4},{6,7},{7,6},{8,9},{9,8},{10,11... | collective-permute-start | bytes 786440 | tf_op jit(solution)/shard_map/ppermute | solution.py:18
  451.0 6.4 %collective-permute-done.86 = bf16[512,256]{0,1:T(8,128)(2,1)S(1)} collective-permute-done((bf16[512,256]{0,1:T(8,128)(2,1)S(1)}, bf16[512,256]{0,1:T(8,128)(2,1)S(1)}, u32[]{:S(2)}, u32[]{:S(2)}) %collective-permute-start.86) | collective-permute-done | bytes 262176 | tf_op jit(solution)/shard_map/ppermute | solution.py:18
  457.5 4.8 collective-permute-start.87
  462.3 5.7 collective-permute-done.87
  468.2 6.3 %collective-permute-done.88 = bf16[512,256]{0,1:T(8,128)(2,1)S(1)} collective-permute-done((bf16[512,256]{0,1:T(8,128)(2,1)S(1)}, bf16[512,256]{0,1:T(8,128)(2,1)S(1)}, u32[]{:S(2)}, u32[]{:S(2)}) %collective-permute-start.88) | collective-permute-done | bytes 262176 | tf_op jit(solution)/shard_map/ppermute | solution.py:18
  495.8 6.1 %collective-permute-done.93 = bf16[512,256]{0,1:T(8,128)(2,1)S(1)} collective-permute-done((bf16[512,256]{0,1:T(8,128)(2,1)S(1)}, bf16[512,256]{0,1:T(8,128)(2,1)S(1)}, u32[]{:S(2)}, u32[]{:S(2)}) %collective-permute-start.93) | collective-permute-done | bytes 262176 | tf_op jit(solution)/shard_map/ppermute | solution.py:18
  502.3 7.9 %collective-permute-done.94 = bf16[512,256]{0,1:T(8,128)(2,1)S(1)} collective-permute-done((bf16[512,256]{0,1:T(8,128)(2,1)S(1)}, bf16[512,256]{0,1:T(8,128)(2,1)S(1)}, u32[]{:S(2)}, u32[]{:S(2)}) %collective-permute-start.94) | collective-permute-done | bytes 262176 | tf_op jit(solution)/shard_map/ppermute | solution.py:18
  515.7 7.2 %collective-permute-done.96 = bf16[512,256]{0,1:T(8,128)(2,1)S(1)} collective-permute-done((bf16[512,256]{0,1:T(8,128)(2,1)S(1)}, bf16[512,256]{0,1:T(8,128)(2,1)S(1)}, u32[]{:S(2)}, u32[]{:S(2)}) %collective-permute-start.96) | collective-permute-done | bytes 262176 | tf_op jit(solution)/shard_map/ppermute | solution.py:18
  525.8 5.5 collective-permute-done.97
  551.8 11.8 %collective-permute-done.102 = bf16[1024,256]{0,1:T(8,128)(2,1)S(1)} collective-permute-done((bf16[1024,256]{0,1:T(8,128)(2,1)S(1)}, bf16[1024,256]{0,1:T(8,128)(2,1)S(1)}, u32[]{:S(2)}, u32[]{:S(2)}) %collective-permute-start.102) | collective-permute-done | bytes 524320 | tf_op jit(solution)/shard_map/ppermute | solution.py:18
  564.3 13.3 %collective-permute-done.103 = bf16[1024,256]{0,1:T(8,128)(2,1)S(1)} collective-permute-done((bf16[1024,256]{0,1:T(8,128)(2,1)S(1)}, bf16[1024,256]{0,1:T(8,128)(2,1)S(1)}, u32[]{:S(2)}, u32[]{:S(2)}) %collective-permute-start.103) | collective-permute-done | bytes 524320 | tf_op jit(solution)/shard_map/ppermute | solution.py:18
  582.6 7.2 %collective-permute-done.105 = bf16[512,256]{0,1:T(8,128)(2,1)S(1)} collective-permute-done((bf16[512,256]{0,1:T(8,128)(2,1)S(1)}, bf16[512,256]{0,1:T(8,128)(2,1)S(1)}, u32[]{:S(2)}, u32[]{:S(2)}) %collective-permute-start.105) | collective-permute-done | bytes 262176 | tf_op jit(solution)/shard_map/ppermute | solution.py:18
  (537 shorter events, 362.8 us)
Async XLA Ops:
  0.6 12.1 %collective-permute-start.4 = (bf16[128,256]{1,0:T(8,128)(2,1)}, bf16[128,256]{1,0:T(8,128)(2,1)S(1)}, u32[]{:S(2)}, u32[]{:S(2)}) collective-permute-start(bf16[128,256]{1,0:T(8,128)(2,1)} %param.10), channel_id=1, source_target_pairs={{0,8},{8,0},{16,24},{24,16},{32,40},{40,32},{48,56},{56,48},{64,72... | collective-permute-start | bytes 196616 | tf_op jit(solution)/shard_map/ppermute | solution.py:18
  2.8 10.2 %collective-permute-start.1 = (bf16[1,128,256]{2,1,0:T(8,128)(2,1)}, bf16[1,128,256]{2,1,0:T(8,128)(2,1)S(1)}, u32[]{:S(2)}, u32[]{:S(2)}) collective-permute-start(bf16[1,128,256]{2,1,0:T(8,128)(2,1)} %bitcast.214), channel_id=1, source_target_pairs={{0,4},{4,0},{1,5},{5,1},{2,6},{6,2},{3,7},{7,3},{8,12},{12,8},{9,1... | collective-permute-start | bytes 196616 | tf_op jit(solution)/shard_map/ppermute | solution.py:18
  9.8 17.1 %collective-permute-start = (bf16[496,256]{1,0:T(8,128)(2,1)S(1)}, bf16[496,256]{1,0:T(8,128)(2,1)S(1)}, u32[]{:S(2)}, u32[]{:S(2)}) collective-permute-start(bf16[496,256]{1,0:T(8,128)(2,1)S(1)} %constant_dynamic-update-slice_fusion), channel_id=1, source_target_pairs={{0,8},{8,0},{16,24},{24,16},{32,40},{40,32},{48,56},{56,48},{64,72... | collective-permute-start | bytes 761864 | tf_op jit(solution)/shard_map/ppermute | solution.py:18
  19.2 8.5 %collective-permute-start.3 = (bf16[1,512,256]{2,1,0:T(8,128)(2,1)S(1)}, bf16[1,512,256]{2,1,0:T(8,128)(2,1)S(1)}, u32[]{:S(2)}, u32[]{:S(2)}) collective-permute-start(bf16[1,512,256]{2,1,0:T(8,128)(2,1)S(1)} %pad_maximum_fusion.5), channel_id=1, source_target_pairs={{0,1},{1,0},{2,3},{3,2},{4,5},{5,4},{6,7},{7,6},{8,9},{9,8},{10,11... | collective-permute-start | bytes 786440 | tf_op jit(solution)/shard_map/ppermute | solution.py:18
  37.0 13.4 %collective-permute-start.9 = (bf16[1024,256]{0,1:T(8,128)(2,1)S(1)}, bf16[1024,256]{0,1:T(8,128)(2,1)S(1)}, u32[]{:S(2)}, u32[]{:S(2)}) collective-permute-start(bf16[1024,256]{0,1:T(8,128)(2,1)S(1)} %fusion.16), channel_id=1, source_target_pairs={{0,2},{2,0},{1,3},{3,1},{4,6},{6,4},{5,7},{7,5},{8,10},{10,8},{9,1... | collective-permute-start | bytes 1572872 | tf_op jit(solution)/shard_map/ppermute | solution.py:18
  50.6 14.1 %collective-permute-start.10 = (bf16[1024,256]{0,1:T(8,128)(2,1)S(1)}, bf16[1024,256]{0,1:T(8,128)(2,1)S(1)}, u32[]{:S(2)}, u32[]{:S(2)}) collective-permute-start(bf16[1024,256]{0,1:T(8,128)(2,1)S(1)} %add_convert_fusion.3), channel_id=1, source_target_pairs={{0,4},{4,0},{1,5},{5,1},{2,6},{6,2},{3,7},{7,3},{8,12},{12,8},{9,1... | collective-permute-start | bytes 1572872 | tf_op jit(solution)/shard_map/ppermute | solution.py:18
  75.0 9.5 %collective-permute-start.13 = (bf16[608,256]{1,0:T(8,128)(2,1)S(1)}, bf16[608,256]{1,0:T(8,128)(2,1)S(1)}, u32[]{:S(2)}, u32[]{:S(2)}) collective-permute-start(bf16[608,256]{1,0:T(8,128)(2,1)S(1)} %get-tuple-element.32), channel_id=1, source_target_pairs={{0,16},{16,0},{8,24},{24,8},{32,48},{48,32},{40,56},{56,40},{64,80... | collective-permute-start | bytes 933896 | tf_op jit(solution)/shard_map/ppermute | solution.py:18
  77.9 8.5 %collective-permute-start.14 = (bf16[1,128,256]{2,1,0:T(8,128)(2,1)S(1)}, bf16[1,128,256]{2,1,0:T(8,128)(2,1)S(1)}, u32[]{:S(2)}, u32[]{:S(2)}) collective-permute-start(bf16[1,128,256]{2,1,0:T(8,128)(2,1)S(1)} %bitcast.210), channel_id=1, source_target_pairs={{0,4},{4,0},{1,5},{5,1},{2,6},{6,2},{3,7},{7,3},{8,12},{12,8},{9,1... | collective-permute-start | bytes 196616 | tf_op jit(solution)/shard_map/ppermute | solution.py:18
  91.1 7.9 %collective-permute-start.16 = (bf16[1,512,256]{2,1,0:T(8,128)(2,1)S(1)}, bf16[1,512,256]{2,1,0:T(8,128)(2,1)S(1)}, u32[]{:S(2)}, u32[]{:S(2)}) collective-permute-start(bf16[1,512,256]{2,1,0:T(8,128)(2,1)S(1)} %pad_maximum_fusion.7), channel_id=1, source_target_pairs={{0,1},{1,0},{2,3},{3,2},{4,5},{5,4},{6,7},{7,6},{8,9},{9,8},{10,11... | collective-permute-start | bytes 786440 | tf_op jit(solution)/shard_map/ppermute | solution.py:18
  106.4 7.6 %collective-permute-start.21 = (bf16[512,256]{0,1:T(8,128)(2,1)S(1)}, bf16[512,256]{0,1:T(8,128)(2,1)S(1)}, u32[]{:S(2)}, u32[]{:S(2)}) collective-permute-start(bf16[512,256]{0,1:T(8,128)(2,1)S(1)} %fusion.44), channel_id=1, source_target_pairs={{0,2},{2,0},{1,3},{3,1},{4,6},{6,4},{5,7},{7,5},{8,10},{10,8},{9,1... | collective-permute-start | bytes 786440 | tf_op jit(solution)/shard_map/ppermute | solution.py:18
  114.1 8.2 %collective-permute-start.22 = (bf16[512,256]{0,1:T(8,128)(2,1)S(1)}, bf16[512,256]{0,1:T(8,128)(2,1)S(1)}, u32[]{:S(2)}, u32[]{:S(2)}) collective-permute-start(bf16[512,256]{0,1:T(8,128)(2,1)S(1)} %add_convert_fusion.7), channel_id=1, source_target_pairs={{0,4},{4,0},{1,5},{5,1},{2,6},{6,2},{3,7},{7,3},{8,12},{12,8},{9,1... | collective-permute-start | bytes 786440 | tf_op jit(solution)/shard_map/ppermute | solution.py:18
  147.9 7.9 %collective-permute-start.31 = (bf16[1,256,256]{2,1,0:T(8,128)(2,1)S(1)}, bf16[1,256,256]{2,1,0:T(8,128)(2,1)S(1)}, u32[]{:S(2)}, u32[]{:S(2)}) collective-permute-start(bf16[1,256,256]{2,1,0:T(8,128)(2,1)S(1)} %pad_maximum_fusion.22), channel_id=1, source_target_pairs={{0,2},{2,0},{1,3},{3,1},{4,6},{6,4},{5,7},{7,5},{8,10},{10,8},{9,1... | collective-permute-start | bytes 393224 | tf_op jit(solution)/shard_map/ppermute | solution.py:18
  150.4 8.5 %collective-permute-start.29 = (bf16[1,512,256]{2,1,0:T(8,128)(2,1)S(1)}, bf16[1,512,256]{2,1,0:T(8,128)(2,1)S(1)}, u32[]{:S(2)}, u32[]{:S(2)}) collective-permute-start(bf16[1,512,256]{2,1,0:T(8,128)(2,1)S(1)} %pad_maximum_fusion.9), channel_id=1, source_target_pairs={{0,1},{1,0},{2,3},{3,2},{4,5},{5,4},{6,7},{7,6},{8,9},{9,8},{10,11... | collective-permute-start | bytes 786440 | tf_op jit(solution)/shard_map/ppermute | solution.py:18
  190.7 13.9 %collective-permute-start.40 = (bf16[512,256]{1,0:T(8,128)(2,1)S(1)}, bf16[512,256]{1,0:T(8,128)(2,1)S(1)}, u32[]{:S(2)}, u32[]{:S(2)}) collective-permute-start(bf16[512,256]{1,0:T(8,128)(2,1)S(1)} %pad_maximum_fusion.11), channel_id=1, source_target_pairs={{0,64},{64,0},{8,72},{72,8},{16,80},{80,16},{24,88},{88,24},{32,96... | collective-permute-start | bytes 786440 | tf_op jit(solution)/shard_map/ppermute | solution.py:18
  193.8 11.5 %collective-permute-start.41 = (bf16[1,128,256]{2,1,0:T(8,128)(2,1)S(1)}, bf16[1,128,256]{2,1,0:T(8,128)(2,1)S(1)}, u32[]{:S(2)}, u32[]{:S(2)}) collective-permute-start(bf16[1,128,256]{2,1,0:T(8,128)(2,1)S(1)} %bitcast.206), channel_id=1, source_target_pairs={{0,4},{4,0},{1,5},{5,1},{2,6},{6,2},{3,7},{7,3},{8,12},{12,8},{9,1... | collective-permute-start | bytes 196616 | tf_op jit(solution)/shard_map/ppermute | solution.py:18
  210.1 10.5 %collective-permute-start.43 = (bf16[1,512,256]{2,1,0:T(8,128)(2,1)S(1)}, bf16[1,512,256]{2,1,0:T(8,128)(2,1)S(1)}, u32[]{:S(2)}, u32[]{:S(2)}) collective-permute-start(bf16[1,512,256]{2,1,0:T(8,128)(2,1)S(1)} %pad_maximum_fusion.12), channel_id=1, source_target_pairs={{0,1},{1,0},{2,3},{3,2},{4,5},{5,4},{6,7},{7,6},{8,9},{9,8},{10,11... | collective-permute-start | bytes 786440 | tf_op jit(solution)/shard_map/ppermute | solution.py:18
  253.8 10.0 %collective-permute-start.54 = (bf16[384,256]{1,0:T(8,128)(2,1)S(1)}, bf16[384,256]{1,0:T(8,128)(2,1)S(1)}, u32[]{:S(2)}, u32[]{:S(2)}) collective-permute-start(bf16[384,256]{1,0:T(8,128)(2,1)S(1)} %pad_maximum_fusion.16), channel_id=1, source_target_pairs={{0,128},{128,0},{8,136},{136,8},{16,144},{144,16},{24,152},{152,24... | collective-permute-start | bytes 589832 | tf_op jit(solution)/shard_map/ppermute | solution.py:18
  268.5 13.7 %collective-permute-start.59 = (bf16[1,256,256]{2,1,0:T(8,128)(2,1)S(1)}, bf16[1,256,256]{2,1,0:T(8,128)(2,1)S(1)}, u32[]{:S(2)}, u32[]{:S(2)}) collective-permute-start(bf16[1,256,256]{2,1,0:T(8,128)(2,1)S(1)} %pad_maximum_fusion.26), channel_id=1, source_target_pairs={{0,2},{2,0},{1,3},{3,1},{4,6},{6,4},{5,7},{7,5},{8,10},{10,8},{9,1... | collective-permute-start | bytes 393224 | tf_op jit(solution)/shard_map/ppermute | solution.py:18
  270.4 15.6 %collective-permute-start.57 = (bf16[1,512,256]{2,1,0:T(8,128)(2,1)S(1)}, bf16[1,512,256]{2,1,0:T(8,128)(2,1)S(1)}, u32[]{:S(2)}, u32[]{:S(2)}) collective-permute-start(bf16[1,512,256]{2,1,0:T(8,128)(2,1)S(1)} %pad_maximum_fusion.14), channel_id=1, source_target_pairs={{0,1},{1,0},{2,3},{3,2},{4,5},{5,4},{6,7},{7,6},{8,9},{9,8},{10,11... | collective-permute-start | bytes 786440 | tf_op jit(solution)/shard_map/ppermute | solution.py:18
  320.7 9.1 %collective-permute-start.67 = (bf16[512,256]{0,1:T(8,128)(2,1)S(1)}, bf16[512,256]{0,1:T(8,128)(2,1)S(1)}, u32[]{:S(2)}, u32[]{:S(2)}) collective-permute-start(bf16[512,256]{0,1:T(8,128)(2,1)S(1)} %fusion.53), channel_id=1, source_target_pairs={{0,64},{64,0},{8,72},{72,8},{16,80},{80,16},{24,88},{88,24},{32,96... | collective-permute-start | bytes 786440 | tf_op jit(solution)/shard_map/ppermute | solution.py:18
  329.9 12.1 %collective-permute-start.68 = (bf16[512,256]{0,1:T(8,128)(2,1)S(1)}, bf16[512,256]{0,1:T(8,128)(2,1)S(1)}, u32[]{:S(2)}, u32[]{:S(2)}) collective-permute-start(bf16[512,256]{0,1:T(8,128)(2,1)S(1)} %fusion.89), channel_id=1, source_target_pairs={{0,128},{128,0},{8,136},{136,8},{16,144},{144,16},{24,152},{152,24... | collective-permute-start | bytes 786440 | tf_op jit(solution)/shard_map/ppermute | solution.py:18
  344.1 14.8 %collective-permute-start.69 = (bf16[2,2,128,256]{2,3,0,1:T(8,128)(2,1)S(1)}, bf16[2,2,128,256]{2,3,0,1:T(8,128)(2,1)S(1)}, u32[]{:S(2)}, u32[]{:S(2)}) collective-permute-start(bf16[2,2,128,256]{2,3,0,1:T(8,128)(2,1)S(1)} %bitcast.223), channel_id=1, source_target_pairs={{0,1},{1,0},{2,3},{3,2},{4,5},{5,4},{6,7},{7,6},{8,9},{9,8},{10,11... | collective-permute-start | bytes 786440 | tf_op jit(solution)/shard_map/ppermute | solution.py:18
  389.1 7.7 %collective-permute-start.76 = (bf16[512,256]{0,1:T(8,128)(2,1)S(1)}, bf16[512,256]{0,1:T(8,128)(2,1)S(1)}, u32[]{:S(2)}, u32[]{:S(2)}) collective-permute-start(bf16[512,256]{0,1:T(8,128)(2,1)S(1)} %fusion.54), channel_id=1, source_target_pairs={{0,16},{16,0},{8,24},{24,8},{32,48},{48,32},{40,56},{56,40},{64,80... | collective-permute-start | bytes 786440 | tf_op jit(solution)/shard_map/ppermute | solution.py:18
  402.4 9.1 %collective-permute-start.78 = (bf16[512,256]{0,1:T(8,128)(2,1)S(1)}, bf16[512,256]{0,1:T(8,128)(2,1)S(1)}, u32[]{:S(2)}, u32[]{:S(2)}) collective-permute-start(bf16[512,256]{0,1:T(8,128)(2,1)S(1)} %fusion.55), channel_id=1, source_target_pairs={{0,64},{64,0},{8,72},{72,8},{16,80},{80,16},{24,88},{88,24},{32,96... | collective-permute-start | bytes 786440 | tf_op jit(solution)/shard_map/ppermute | solution.py:18
  413.8 7.6 %collective-permute-start.79 = (bf16[2,2,128,256]{2,3,0,1:T(8,128)(2,1)S(1)}, bf16[2,2,128,256]{2,3,0,1:T(8,128)(2,1)S(1)}, u32[]{:S(2)}, u32[]{:S(2)}) collective-permute-start(bf16[2,2,128,256]{2,3,0,1:T(8,128)(2,1)S(1)} %bitcast.224), channel_id=1, source_target_pairs={{0,1},{1,0},{2,3},{3,2},{4,5},{5,4},{6,7},{7,6},{8,9},{9,8},{10,11... | collective-permute-start | bytes 786440 | tf_op jit(solution)/shard_map/ppermute | solution.py:18
  449.9 7.6 %collective-permute-start.86 = (bf16[512,256]{0,1:T(8,128)(2,1)S(1)}, bf16[512,256]{0,1:T(8,128)(2,1)S(1)}, u32[]{:S(2)}, u32[]{:S(2)}) collective-permute-start(bf16[512,256]{0,1:T(8,128)(2,1)S(1)} %get-tuple-element.80), channel_id=1, source_target_pairs={{0,8},{8,0},{16,24},{24,16},{32,40},{40,32},{48,56},{56,48},{64,72... | collective-permute-start | bytes 786440 | tf_op jit(solution)/shard_map/ppermute | solution.py:18
  457.5 10.5 %collective-permute-start.87 = (bf16[512,256]{0,1:T(8,128)(2,1)S(1)}, bf16[512,256]{0,1:T(8,128)(2,1)S(1)}, u32[]{:S(2)}, u32[]{:S(2)}) collective-permute-start(bf16[512,256]{0,1:T(8,128)(2,1)S(1)} %fusion.56), channel_id=1, source_target_pairs={{0,16},{16,0},{8,24},{24,8},{32,48},{48,32},{40,56},{56,40},{64,80... | collective-permute-start | bytes 786440 | tf_op jit(solution)/shard_map/ppermute | solution.py:18
  494.2 7.8 %collective-permute-start.93 = (bf16[512,256]{0,1:T(8,128)(2,1)S(1)}, bf16[512,256]{0,1:T(8,128)(2,1)S(1)}, u32[]{:S(2)}, u32[]{:S(2)}) collective-permute-start(bf16[512,256]{0,1:T(8,128)(2,1)S(1)} %fusion.43), channel_id=1, source_target_pairs={{0,2},{2,0},{1,3},{3,1},{4,6},{6,4},{5,7},{7,5},{8,10},{10,8},{9,1... | collective-permute-start | bytes 786440 | tf_op jit(solution)/shard_map/ppermute | solution.py:18
  502.0 8.2 %collective-permute-start.94 = (bf16[512,256]{0,1:T(8,128)(2,1)S(1)}, bf16[512,256]{0,1:T(8,128)(2,1)S(1)}, u32[]{:S(2)}, u32[]{:S(2)}) collective-permute-start(bf16[512,256]{0,1:T(8,128)(2,1)S(1)} %add_convert_fusion.5), channel_id=1, source_target_pairs={{0,4},{4,0},{1,5},{5,1},{2,6},{6,2},{3,7},{7,3},{8,12},{12,8},{9,1... | collective-permute-start | bytes 786440 | tf_op jit(solution)/shard_map/ppermute | solution.py:18
  523.0 8.2 %collective-permute-start.97 = (bf16[512,256]{0,1:T(8,128)(2,1)S(1)}, bf16[512,256]{0,1:T(8,128)(2,1)S(1)}, u32[]{:S(2)}, u32[]{:S(2)}) collective-permute-start(bf16[512,256]{0,1:T(8,128)(2,1)S(1)} %fusion.57), channel_id=1, source_target_pairs={{0,16},{16,0},{8,24},{24,8},{32,48},{48,32},{40,56},{56,40},{64,80... | collective-permute-start | bytes 786440 | tf_op jit(solution)/shard_map/ppermute | solution.py:18
  550.3 13.2 %collective-permute-start.102 = (bf16[1024,256]{0,1:T(8,128)(2,1)S(1)}, bf16[1024,256]{0,1:T(8,128)(2,1)S(1)}, u32[]{:S(2)}, u32[]{:S(2)}) collective-permute-start(bf16[1024,256]{0,1:T(8,128)(2,1)S(1)} %fusion.15), channel_id=1, source_target_pairs={{0,2},{2,0},{1,3},{3,1},{4,6},{6,4},{5,7},{7,5},{8,10},{10,8},{9,1... | collective-permute-start | bytes 1572872 | tf_op jit(solution)/shard_map/ppermute | solution.py:18
  563.7 13.8 %collective-permute-start.103 = (bf16[1024,256]{0,1:T(8,128)(2,1)S(1)}, bf16[1024,256]{0,1:T(8,128)(2,1)S(1)}, u32[]{:S(2)}, u32[]{:S(2)}) collective-permute-start(bf16[1024,256]{0,1:T(8,128)(2,1)S(1)} %add_convert_fusion.1), channel_id=1, source_target_pairs={{0,4},{4,0},{1,5},{5,1},{2,6},{6,2},{3,7},{7,3},{8,12},{12,8},{9,1... | collective-permute-start | bytes 1572872 | tf_op jit(solution)/shard_map/ppermute | solution.py:18
  (118 other events, 970.5 us)

commit v9 on v8

--- a/solution.py
+++ b/solution.py
@@ -148,6 +148,20 @@
         )
         offset += count
     return sibling
+
+
+def sum_solution_halved(summand, height, position):
+    half_rows = summand.shape[0] // 2
+    upper = position & 1
+    keep = lax.dynamic_slice_in_dim(summand, upper * half_rows, half_rows, 0)
+    send = lax.dynamic_slice_in_dim(summand, (1 - upper) * half_rows, half_rows, 0)
+    summand = keep + partner(send.astype(jnp.bfloat16), "leaf", 0).astype(summand.dtype)
+    for bit_index in range(1, height):
+        summand = summand + partner(summand.astype(jnp.bfloat16), "leaf", bit_index).astype(
+            summand.dtype
+        )
+    received = partner(summand.astype(jnp.bfloat16), "leaf", 0).astype(summand.dtype)
+    return joined(position, 0, summand, received)
 
 
 def per_device(section_updates, upper_rhs, pivot_inverse, coupling, extend_lists):
@@ -237,7 +251,10 @@
             "cp,cr->pr", g_share, weight_half, preferred_element_type=jnp.float32
         )
         part_len = piv_dev // group_size
-        summed = sum_solution(solve_term, height)
+        if height == levels:
+            summed = sum_solution_halved(solve_term, height, position)
+        else:
+            summed = sum_solution(solve_term, height)
         portion = lax.dynamic_slice_in_dim(summed, member * part_len, part_len, 0)
         rows_half = summed.astype(jnp.bfloat16)
         outputs.append(portion)

time: 616 us -> 606 us (0.984)
  starting transfers between devices: 193 us -> 184 us
    ppermute x109 -> x110, starting transfers between devices: 193 us -> 184 us  [partner(): return lax.ppermute(block, axis, route)]
    ppermute x109 -> x110, waiting for transfers between devices: 322 us -> 322 us  [partner(): return lax.ppermute(block, axis, route)]
  transfers between devices with their start and end apart: 109 -> 110, of which waited for: 84 -> 85; matrix products, arithmetic and copies ran while one was open for 6% -> 6% of each run, Pallas kernels for 0% -> 0%
where the time goes in v9:
time: 606 us; the launch traced here: 596 us
  waiting for transfers between devices  322 us (53%)
  starting transfers between devices  184 us (30%)
  local copies, waits for them, and re-layouts  33.3 us (5%)
  other arithmetic  32.6 us (5%)
  matrix products  21.2 us (3%)
    ppermute x110, waiting for transfers between devices, partner(): return lax.ppermute(block, axis, route)  322 us
    ppermute x110, starting transfers between devices, partner(): return lax.ppermute(block, axis, route)  184 us
  transfers between devices with their start and end apart: 110, of which 85 were waited for; matrix products, arithmetic and copies ran while one was open for 6% of the time, Pallas kernels for 0%

profile of v9, /device:TPU:1, one launch (start us, length us, event | category | flops | bytes accessed | tf_op | source)
XLA Modules:
  0.0 595.7 jit_solution(517460822127557848)
XLA Ops:
  19.2 5.2 collective-permute-start.3
  37.4 13.0 %collective-permute-done.9 = bf16[1024,256]{0,1:T(8,128)(2,1)S(1)} collective-permute-done((bf16[1024,256]{0,1:T(8,128)(2,1)S(1)}, bf16[1024,256]{0,1:T(8,128)(2,1)S(1)}, u32[]{:S(2)}, u32[]{:S(2)}) %collective-permute-start.9) | collective-permute-done | bytes 524320 | tf_op jit(solution)/shard_map/ppermute | solution.py:18
  52.7 12.0 %collective-permute-done.10 = bf16[1024,256]{0,1:T(8,128)(2,1)S(1)} collective-permute-done((bf16[1024,256]{0,1:T(8,128)(2,1)S(1)}, bf16[1024,256]{0,1:T(8,128)(2,1)S(1)}, u32[]{:S(2)}, u32[]{:S(2)}) %collective-permute-start.10) | collective-permute-done | bytes 524320 | tf_op jit(solution)/shard_map/ppermute | solution.py:18
  78.8 5.7 collective-permute-done.13
  106.6 7.4 %collective-permute-done.21 = bf16[512,256]{0,1:T(8,128)(2,1)S(1)} collective-permute-done((bf16[512,256]{0,1:T(8,128)(2,1)S(1)}, bf16[512,256]{0,1:T(8,128)(2,1)S(1)}, u32[]{:S(2)}, u32[]{:S(2)}) %collective-permute-start.21) | collective-permute-done | bytes 262176 | tf_op jit(solution)/shard_map/ppermute | solution.py:18
  116.9 5.3 collective-permute-done.22
  137.9 4.6 collective-permute-done.26
  150.4 5.3 collective-permute-start.29
  170.9 4.6 collective-permute-done.35
  193.7 10.8 %collective-permute-done.40 = bf16[512,256]{1,0:T(8,128)(2,1)S(1)} collective-permute-done((bf16[512,256]{1,0:T(8,128)(2,1)S(1)}, bf16[512,256]{1,0:T(8,128)(2,1)S(1)}, u32[]{:S(2)}, u32[]{:S(2)}) %collective-permute-start.40) | collective-permute-done | bytes 262176 | tf_op jit(solution)/shard_map/ppermute | solution.py:18
  232.1 5.3 collective-permute-done.49
  253.8 6.1 %collective-permute-start.54 = (bf16[384,256]{1,0:T(8,128)(2,1)S(1)}, bf16[384,256]{1,0:T(8,128)(2,1)S(1)}, u32[]{:S(2)}, u32[]{:S(2)}) collective-permute-start(bf16[384,256]{1,0:T(8,128)(2,1)S(1)} %pad_maximum_fusion.16), channel_id=1, source_target_pairs={{0,128},{128,0},{8,136},{136,8},{16,144},{144,16},{24,152},{152,24... | collective-permute-start | bytes 589832 | tf_op jit(solution)/shard_map/ppermute | solution.py:18
  270.3 11.8 %collective-permute-start.57 = (bf16[1,512,256]{2,1,0:T(8,128)(2,1)S(1)}, bf16[1,512,256]{2,1,0:T(8,128)(2,1)S(1)}, u32[]{:S(2)}, u32[]{:S(2)}) collective-permute-start(bf16[1,512,256]{2,1,0:T(8,128)(2,1)S(1)} %pad_maximum_fusion.14), channel_id=1, source_target_pairs={{0,1},{1,0},{2,3},{3,2},{4,5},{5,4},{6,7},{7,6},{8,9},{9,8},{10,11... | collective-permute-start | bytes 786440 | tf_op jit(solution)/shard_map/ppermute | solution.py:18
  315.4 6.1 %collective-permute-done.67 = bf16[256,256]{1,0:T(8,128)(2,1)S(1)} collective-permute-done((bf16[256,256]{1,0:T(8,128)(2,1)S(1)}, bf16[256,256]{1,0:T(8,128)(2,1)S(1)}, u32[]{:S(2)}, u32[]{:S(2)}) %collective-permute-start.67) | collective-permute-done | bytes 131104 | tf_op jit(solution)/shard_map/ppermute | solution.py:18
  321.6 5.7 collective-permute-start.68
  327.3 5.1 collective-permute-done.68
  338.6 9.5 %collective-permute-start.70 = (bf16[2,2,128,256]{2,3,0,1:T(8,128)(2,1)S(1)}, bf16[2,2,128,256]{2,3,0,1:T(8,128)(2,1)S(1)}, u32[]{:S(2)}, u32[]{:S(2)}) collective-permute-start(bf16[2,2,128,256]{2,3,0,1:T(8,128)(2,1)S(1)} %bitcast.232), channel_id=1, source_target_pairs={{0,1},{1,0},{2,3},{3,2},{4,5},{5,4},{6,7},{7,6},{8,9},{9,8},{10,11... | collective-permute-start | bytes 786440 | tf_op jit(solution)/shard_map/ppermute | solution.py:18
  368.4 4.5 collective-permute-done.75
  383.7 5.6 collective-permute-done.77
  389.5 5.2 collective-permute-done.78
  395.4 13.1 %collective-permute-done.79 = bf16[512,256]{0,1:T(8,128)(2,1)S(1)} collective-permute-done((bf16[512,256]{0,1:T(8,128)(2,1)S(1)}, bf16[512,256]{0,1:T(8,128)(2,1)S(1)}, u32[]{:S(2)}, u32[]{:S(2)}) %collective-permute-start.79) | collective-permute-done | bytes 262176 | tf_op jit(solution)/shard_map/ppermute | solution.py:18
  432.9 4.6 collective-permute-done.85
  442.8 7.1 %collective-permute-done.87 = bf16[512,256]{0,1:T(8,128)(2,1)S(1)} collective-permute-done((bf16[512,256]{0,1:T(8,128)(2,1)S(1)}, bf16[512,256]{0,1:T(8,128)(2,1)S(1)}, u32[]{:S(2)}, u32[]{:S(2)}) %collective-permute-start.87) | collective-permute-done | bytes 262176 | tf_op jit(solution)/shard_map/ppermute | solution.py:18
  453.2 5.4 collective-permute-done.88
  458.8 5.9 collective-permute-done.89
  486.0 6.5 %collective-permute-done.94 = bf16[512,256]{0,1:T(8,128)(2,1)S(1)} collective-permute-done((bf16[512,256]{0,1:T(8,128)(2,1)S(1)}, bf16[512,256]{0,1:T(8,128)(2,1)S(1)}, u32[]{:S(2)}, u32[]{:S(2)}) %collective-permute-start.94) | collective-permute-done | bytes 262176 | tf_op jit(solution)/shard_map/ppermute | solution.py:18
  493.8 7.0 %collective-permute-done.95 = bf16[512,256]{0,1:T(8,128)(2,1)S(1)} collective-permute-done((bf16[512,256]{0,1:T(8,128)(2,1)S(1)}, bf16[512,256]{0,1:T(8,128)(2,1)S(1)}, u32[]{:S(2)}, u32[]{:S(2)}) %collective-permute-start.95) | collective-permute-done | bytes 262176 | tf_op jit(solution)/shard_map/ppermute | solution.py:18
  506.6 6.8 %collective-permute-done.97 = bf16[512,256]{0,1:T(8,128)(2,1)S(1)} collective-permute-done((bf16[512,256]{0,1:T(8,128)(2,1)S(1)}, bf16[512,256]{0,1:T(8,128)(2,1)S(1)}, u32[]{:S(2)}, u32[]{:S(2)}) %collective-permute-start.97) | collective-permute-done | bytes 262176 | tf_op jit(solution)/shard_map/ppermute | solution.py:18
  516.7 5.3 collective-permute-done.98
  542.0 12.2 %collective-permute-done.103 = bf16[1024,256]{0,1:T(8,128)(2,1)S(1)} collective-permute-done((bf16[1024,256]{0,1:T(8,128)(2,1)S(1)}, bf16[1024,256]{0,1:T(8,128)(2,1)S(1)}, u32[]{:S(2)}, u32[]{:S(2)}) %collective-permute-start.103) | collective-permute-done | bytes 524320 | tf_op jit(solution)/shard_map/ppermute | solution.py:18
  555.5 12.7 %collective-permute-done.104 = bf16[1024,256]{0,1:T(8,128)(2,1)S(1)} collective-permute-done((bf16[1024,256]{0,1:T(8,128)(2,1)S(1)}, bf16[1024,256]{0,1:T(8,128)(2,1)S(1)}, u32[]{:S(2)}, u32[]{:S(2)}) %collective-permute-start.104) | collective-permute-done | bytes 524320 | tf_op jit(solution)/shard_map/ppermute | solution.py:18
  573.6 6.9 %collective-permute-done.106 = bf16[512,256]{0,1:T(8,128)(2,1)S(1)} collective-permute-done((bf16[512,256]{0,1:T(8,128)(2,1)S(1)}, bf16[512,256]{0,1:T(8,128)(2,1)S(1)}, u32[]{:S(2)}, u32[]{:S(2)}) %collective-permute-start.106) | collective-permute-done | bytes 262176 | tf_op jit(solution)/shard_map/ppermute | solution.py:18
  (542 shorter events, 360.8 us)
Async XLA Ops:
  0.6 12.1 %collective-permute-start.4 = (bf16[128,256]{1,0:T(8,128)(2,1)}, bf16[128,256]{1,0:T(8,128)(2,1)S(1)}, u32[]{:S(2)}, u32[]{:S(2)}) collective-permute-start(bf16[128,256]{1,0:T(8,128)(2,1)} %param.10), channel_id=1, source_target_pairs={{0,8},{8,0},{16,24},{24,16},{32,40},{40,32},{48,56},{56,48},{64,72... | collective-permute-start | bytes 196616 | tf_op jit(solution)/shard_map/ppermute | solution.py:18
  2.8 10.2 %collective-permute-start.1 = (bf16[1,128,256]{2,1,0:T(8,128)(2,1)}, bf16[1,128,256]{2,1,0:T(8,128)(2,1)S(1)}, u32[]{:S(2)}, u32[]{:S(2)}) collective-permute-start(bf16[1,128,256]{2,1,0:T(8,128)(2,1)} %bitcast.223), channel_id=1, source_target_pairs={{0,4},{4,0},{1,5},{5,1},{2,6},{6,2},{3,7},{7,3},{8,12},{12,8},{9,1... | collective-permute-start | bytes 196616 | tf_op jit(solution)/shard_map/ppermute | solution.py:18
  9.8 17.1 %collective-permute-start = (bf16[496,256]{1,0:T(8,128)(2,1)S(1)}, bf16[496,256]{1,0:T(8,128)(2,1)S(1)}, u32[]{:S(2)}, u32[]{:S(2)}) collective-permute-start(bf16[496,256]{1,0:T(8,128)(2,1)S(1)} %constant_dynamic-update-slice_fusion), channel_id=1, source_target_pairs={{0,8},{8,0},{16,24},{24,16},{32,40},{40,32},{48,56},{56,48},{64,72... | collective-permute-start | bytes 761864 | tf_op jit(solution)/shard_map/ppermute | solution.py:18
  19.2 8.5 %collective-permute-start.3 = (bf16[1,512,256]{2,1,0:T(8,128)(2,1)S(1)}, bf16[1,512,256]{2,1,0:T(8,128)(2,1)S(1)}, u32[]{:S(2)}, u32[]{:S(2)}) collective-permute-start(bf16[1,512,256]{2,1,0:T(8,128)(2,1)S(1)} %pad_maximum_fusion.5), channel_id=1, source_target_pairs={{0,1},{1,0},{2,3},{3,2},{4,5},{5,4},{6,7},{7,6},{8,9},{9,8},{10,11... | collective-permute-start | bytes 786440 | tf_op jit(solution)/shard_map/ppermute | solution.py:18
  37.0 13.4 %collective-permute-start.9 = (bf16[1024,256]{0,1:T(8,128)(2,1)S(1)}, bf16[1024,256]{0,1:T(8,128)(2,1)S(1)}, u32[]{:S(2)}, u32[]{:S(2)}) collective-permute-start(bf16[1024,256]{0,1:T(8,128)(2,1)S(1)} %fusion.16), channel_id=1, source_target_pairs={{0,2},{2,0},{1,3},{3,1},{4,6},{6,4},{5,7},{7,5},{8,10},{10,8},{9,1... | collective-permute-start | bytes 1572872 | tf_op jit(solution)/shard_map/ppermute | solution.py:18
  50.6 14.1 %collective-permute-start.10 = (bf16[1024,256]{0,1:T(8,128)(2,1)S(1)}, bf16[1024,256]{0,1:T(8,128)(2,1)S(1)}, u32[]{:S(2)}, u32[]{:S(2)}) collective-permute-start(bf16[1024,256]{0,1:T(8,128)(2,1)S(1)} %add_convert_fusion.3), channel_id=1, source_target_pairs={{0,4},{4,0},{1,5},{5,1},{2,6},{6,2},{3,7},{7,3},{8,12},{12,8},{9,1... | collective-permute-start | bytes 1572872 | tf_op jit(solution)/shard_map/ppermute | solution.py:18
  75.0 9.5 %collective-permute-start.13 = (bf16[608,256]{1,0:T(8,128)(2,1)S(1)}, bf16[608,256]{1,0:T(8,128)(2,1)S(1)}, u32[]{:S(2)}, u32[]{:S(2)}) collective-permute-start(bf16[608,256]{1,0:T(8,128)(2,1)S(1)} %get-tuple-element.34), channel_id=1, source_target_pairs={{0,16},{16,0},{8,24},{24,8},{32,48},{48,32},{40,56},{56,40},{64,80... | collective-permute-start | bytes 933896 | tf_op jit(solution)/shard_map/ppermute | solution.py:18
  77.9 8.5 %collective-permute-start.14 = (bf16[1,128,256]{2,1,0:T(8,128)(2,1)S(1)}, bf16[1,128,256]{2,1,0:T(8,128)(2,1)S(1)}, u32[]{:S(2)}, u32[]{:S(2)}) collective-permute-start(bf16[1,128,256]{2,1,0:T(8,128)(2,1)S(1)} %bitcast.219), channel_id=1, source_target_pairs={{0,4},{4,0},{1,5},{5,1},{2,6},{6,2},{3,7},{7,3},{8,12},{12,8},{9,1... | collective-permute-start | bytes 196616 | tf_op jit(solution)/shard_map/ppermute | solution.py:18
  91.0 7.9 %collective-permute-start.16 = (bf16[1,512,256]{2,1,0:T(8,128)(2,1)S(1)}, bf16[1,512,256]{2,1,0:T(8,128)(2,1)S(1)}, u32[]{:S(2)}, u32[]{:S(2)}) collective-permute-start(bf16[1,512,256]{2,1,0:T(8,128)(2,1)S(1)} %pad_maximum_fusion.7), channel_id=1, source_target_pairs={{0,1},{1,0},{2,3},{3,2},{4,5},{5,4},{6,7},{7,6},{8,9},{9,8},{10,11... | collective-permute-start | bytes 786440 | tf_op jit(solution)/shard_map/ppermute | solution.py:18
  106.4 7.6 %collective-permute-start.21 = (bf16[512,256]{0,1:T(8,128)(2,1)S(1)}, bf16[512,256]{0,1:T(8,128)(2,1)S(1)}, u32[]{:S(2)}, u32[]{:S(2)}) collective-permute-start(bf16[512,256]{0,1:T(8,128)(2,1)S(1)} %fusion.44), channel_id=1, source_target_pairs={{0,2},{2,0},{1,3},{3,1},{4,6},{6,4},{5,7},{7,5},{8,10},{10,8},{9,1... | collective-permute-start | bytes 786440 | tf_op jit(solution)/shard_map/ppermute | solution.py:18
  114.0 8.2 %collective-permute-start.22 = (bf16[512,256]{0,1:T(8,128)(2,1)S(1)}, bf16[512,256]{0,1:T(8,128)(2,1)S(1)}, u32[]{:S(2)}, u32[]{:S(2)}) collective-permute-start(bf16[512,256]{0,1:T(8,128)(2,1)S(1)} %add_convert_fusion.7), channel_id=1, source_target_pairs={{0,4},{4,0},{1,5},{5,1},{2,6},{6,2},{3,7},{7,3},{8,12},{12,8},{9,1... | collective-permute-start | bytes 786440 | tf_op jit(solution)/shard_map/ppermute | solution.py:18
  147.8 7.9 %collective-permute-start.31 = (bf16[1,256,256]{2,1,0:T(8,128)(2,1)S(1)}, bf16[1,256,256]{2,1,0:T(8,128)(2,1)S(1)}, u32[]{:S(2)}, u32[]{:S(2)}) collective-permute-start(bf16[1,256,256]{2,1,0:T(8,128)(2,1)S(1)} %pad_maximum_fusion.22), channel_id=1, source_target_pairs={{0,2},{2,0},{1,3},{3,1},{4,6},{6,4},{5,7},{7,5},{8,10},{10,8},{9,1... | collective-permute-start | bytes 393224 | tf_op jit(solution)/shard_map/ppermute | solution.py:18
  150.4 8.4 %collective-permute-start.29 = (bf16[1,512,256]{2,1,0:T(8,128)(2,1)S(1)}, bf16[1,512,256]{2,1,0:T(8,128)(2,1)S(1)}, u32[]{:S(2)}, u32[]{:S(2)}) collective-permute-start(bf16[1,512,256]{2,1,0:T(8,128)(2,1)S(1)} %pad_maximum_fusion.9), channel_id=1, source_target_pairs={{0,1},{1,0},{2,3},{3,2},{4,5},{5,4},{6,7},{7,6},{8,9},{9,8},{10,11... | collective-permute-start | bytes 786440 | tf_op jit(solution)/shard_map/ppermute | solution.py:18
  190.6 13.9 %collective-permute-start.40 = (bf16[512,256]{1,0:T(8,128)(2,1)S(1)}, bf16[512,256]{1,0:T(8,128)(2,1)S(1)}, u32[]{:S(2)}, u32[]{:S(2)}) collective-permute-start(bf16[512,256]{1,0:T(8,128)(2,1)S(1)} %pad_maximum_fusion.11), channel_id=1, source_target_pairs={{0,64},{64,0},{8,72},{72,8},{16,80},{80,16},{24,88},{88,24},{32,96... | collective-permute-start | bytes 786440 | tf_op jit(solution)/shard_map/ppermute | solution.py:18
  193.7 11.5 %collective-permute-start.41 = (bf16[1,128,256]{2,1,0:T(8,128)(2,1)S(1)}, bf16[1,128,256]{2,1,0:T(8,128)(2,1)S(1)}, u32[]{:S(2)}, u32[]{:S(2)}) collective-permute-start(bf16[1,128,256]{2,1,0:T(8,128)(2,1)S(1)} %bitcast.215), channel_id=1, source_target_pairs={{0,4},{4,0},{1,5},{5,1},{2,6},{6,2},{3,7},{7,3},{8,12},{12,8},{9,1... | collective-permute-start | bytes 196616 | tf_op jit(solution)/shard_map/ppermute | solution.py:18
  210.1 10.5 %collective-permute-start.43 = (bf16[1,512,256]{2,1,0:T(8,128)(2,1)S(1)}, bf16[1,512,256]{2,1,0:T(8,128)(2,1)S(1)}, u32[]{:S(2)}, u32[]{:S(2)}) collective-permute-start(bf16[1,512,256]{2,1,0:T(8,128)(2,1)S(1)} %pad_maximum_fusion.12), channel_id=1, source_target_pairs={{0,1},{1,0},{2,3},{3,2},{4,5},{5,4},{6,7},{7,6},{8,9},{9,8},{10,11... | collective-permute-start | bytes 786440 | tf_op jit(solution)/shard_map/ppermute | solution.py:18
  253.8 10.0 %collective-permute-start.54 = (bf16[384,256]{1,0:T(8,128)(2,1)S(1)}, bf16[384,256]{1,0:T(8,128)(2,1)S(1)}, u32[]{:S(2)}, u32[]{:S(2)}) collective-permute-start(bf16[384,256]{1,0:T(8,128)(2,1)S(1)} %pad_maximum_fusion.16), channel_id=1, source_target_pairs={{0,128},{128,0},{8,136},{136,8},{16,144},{144,16},{24,152},{152,24... | collective-permute-start | bytes 589832 | tf_op jit(solution)/shard_map/ppermute | solution.py:18
  268.4 13.7 %collective-permute-start.59 = (bf16[1,256,256]{2,1,0:T(8,128)(2,1)S(1)}, bf16[1,256,256]{2,1,0:T(8,128)(2,1)S(1)}, u32[]{:S(2)}, u32[]{:S(2)}) collective-permute-start(bf16[1,256,256]{2,1,0:T(8,128)(2,1)S(1)} %pad_maximum_fusion.26), channel_id=1, source_target_pairs={{0,2},{2,0},{1,3},{3,1},{4,6},{6,4},{5,7},{7,5},{8,10},{10,8},{9,1... | collective-permute-start | bytes 393224 | tf_op jit(solution)/shard_map/ppermute | solution.py:18
  270.3 15.6 %collective-permute-start.57 = (bf16[1,512,256]{2,1,0:T(8,128)(2,1)S(1)}, bf16[1,512,256]{2,1,0:T(8,128)(2,1)S(1)}, u32[]{:S(2)}, u32[]{:S(2)}) collective-permute-start(bf16[1,512,256]{2,1,0:T(8,128)(2,1)S(1)} %pad_maximum_fusion.14), channel_id=1, source_target_pairs={{0,1},{1,0},{2,3},{3,2},{4,5},{5,4},{6,7},{7,6},{8,9},{9,8},{10,11... | collective-permute-start | bytes 786440 | tf_op jit(solution)/shard_map/ppermute | solution.py:18
  321.6 10.9 %collective-permute-start.68 = (bf16[256,256]{1,0:T(8,128)(2,1)S(1)}, bf16[256,256]{1,0:T(8,128)(2,1)S(1)}, u32[]{:S(2)}, u32[]{:S(2)}) collective-permute-start(bf16[256,256]{1,0:T(8,128)(2,1)S(1)} %fusion.89), channel_id=1, source_target_pairs={{0,128},{128,0},{8,136},{136,8},{16,144},{144,16},{24,152},{152,24... | collective-permute-start | bytes 393224 | tf_op jit(solution)/shard_map/ppermute | solution.py:18
  338.6 10.6 %collective-permute-start.70 = (bf16[2,2,128,256]{2,3,0,1:T(8,128)(2,1)S(1)}, bf16[2,2,128,256]{2,3,0,1:T(8,128)(2,1)S(1)}, u32[]{:S(2)}, u32[]{:S(2)}) collective-permute-start(bf16[2,2,128,256]{2,3,0,1:T(8,128)(2,1)S(1)} %bitcast.232), channel_id=1, source_target_pairs={{0,1},{1,0},{2,3},{3,2},{4,5},{5,4},{6,7},{7,6},{8,9},{9,8},{10,11... | collective-permute-start | bytes 786440 | tf_op jit(solution)/shard_map/ppermute | solution.py:18
  380.2 9.1 %collective-permute-start.77 = (bf16[512,256]{0,1:T(8,128)(2,1)S(1)}, bf16[512,256]{0,1:T(8,128)(2,1)S(1)}, u32[]{:S(2)}, u32[]{:S(2)}) collective-permute-start(bf16[512,256]{0,1:T(8,128)(2,1)S(1)} %fusion.52), channel_id=1, source_target_pairs={{0,16},{16,0},{8,24},{24,8},{32,48},{48,32},{40,56},{56,40},{64,80... | collective-permute-start | bytes 786440 | tf_op jit(solution)/shard_map/ppermute | solution.py:18
  394.9 13.6 %collective-permute-start.79 = (bf16[512,256]{0,1:T(8,128)(2,1)S(1)}, bf16[512,256]{0,1:T(8,128)(2,1)S(1)}, u32[]{:S(2)}, u32[]{:S(2)}) collective-permute-start(bf16[512,256]{0,1:T(8,128)(2,1)S(1)} %fusion.53), channel_id=1, source_target_pairs={{0,64},{64,0},{8,72},{72,8},{16,80},{80,16},{24,88},{88,24},{32,96... | collective-permute-start | bytes 786440 | tf_op jit(solution)/shard_map/ppermute | solution.py:18
  442.3 7.6 %collective-permute-start.87 = (bf16[512,256]{0,1:T(8,128)(2,1)S(1)}, bf16[512,256]{0,1:T(8,128)(2,1)S(1)}, u32[]{:S(2)}, u32[]{:S(2)}) collective-permute-start(bf16[512,256]{0,1:T(8,128)(2,1)S(1)} %get-tuple-element.80), channel_id=1, source_target_pairs={{0,8},{8,0},{16,24},{24,16},{32,40},{40,32},{48,56},{56,48},{64,72... | collective-permute-start | bytes 786440 | tf_op jit(solution)/shard_map/ppermute | solution.py:18
  450.0 8.6 %collective-permute-start.88 = (bf16[512,256]{0,1:T(8,128)(2,1)S(1)}, bf16[512,256]{0,1:T(8,128)(2,1)S(1)}, u32[]{:S(2)}, u32[]{:S(2)}) collective-permute-start(bf16[512,256]{0,1:T(8,128)(2,1)S(1)} %fusion.54), channel_id=1, source_target_pairs={{0,16},{16,0},{8,24},{24,8},{32,48},{48,32},{40,56},{56,40},{64,80... | collective-permute-start | bytes 786440 | tf_op jit(solution)/shard_map/ppermute | solution.py:18
  484.7 7.8 %collective-permute-start.94 = (bf16[512,256]{0,1:T(8,128)(2,1)S(1)}, bf16[512,256]{0,1:T(8,128)(2,1)S(1)}, u32[]{:S(2)}, u32[]{:S(2)}) collective-permute-start(bf16[512,256]{0,1:T(8,128)(2,1)S(1)} %fusion.43), channel_id=1, source_target_pairs={{0,2},{2,0},{1,3},{3,1},{4,6},{6,4},{5,7},{7,5},{8,10},{10,8},{9,1... | collective-permute-start | bytes 786440 | tf_op jit(solution)/shard_map/ppermute | solution.py:18
  492.5 8.2 %collective-permute-start.95 = (bf16[512,256]{0,1:T(8,128)(2,1)S(1)}, bf16[512,256]{0,1:T(8,128)(2,1)S(1)}, u32[]{:S(2)}, u32[]{:S(2)}) collective-permute-start(bf16[512,256]{0,1:T(8,128)(2,1)S(1)} %add_convert_fusion.5), channel_id=1, source_target_pairs={{0,4},{4,0},{1,5},{5,1},{2,6},{6,2},{3,7},{7,3},{8,12},{12,8},{9,1... | collective-permute-start | bytes 786440 | tf_op jit(solution)/shard_map/ppermute | solution.py:18
  505.8 7.6 %collective-permute-start.97 = (bf16[512,256]{0,1:T(8,128)(2,1)S(1)}, bf16[512,256]{0,1:T(8,128)(2,1)S(1)}, u32[]{:S(2)}, u32[]{:S(2)}) collective-permute-start(bf16[512,256]{0,1:T(8,128)(2,1)S(1)} %get-tuple-element.82), channel_id=1, source_target_pairs={{0,8},{8,0},{16,24},{24,16},{32,40},{40,32},{48,56},{56,48},{64,72... | collective-permute-start | bytes 786440 | tf_op jit(solution)/shard_map/ppermute | solution.py:18
  513.5 8.4 %collective-permute-start.98 = (bf16[512,256]{0,1:T(8,128)(2,1)S(1)}, bf16[512,256]{0,1:T(8,128)(2,1)S(1)}, u32[]{:S(2)}, u32[]{:S(2)}) collective-permute-start(bf16[512,256]{0,1:T(8,128)(2,1)S(1)} %fusion.55), channel_id=1, source_target_pairs={{0,16},{16,0},{8,24},{24,8},{32,48},{48,32},{40,56},{56,40},{64,80... | collective-permute-start | bytes 786440 | tf_op jit(solution)/shard_map/ppermute | solution.py:18
  541.0 13.2 %collective-permute-start.103 = (bf16[1024,256]{0,1:T(8,128)(2,1)S(1)}, bf16[1024,256]{0,1:T(8,128)(2,1)S(1)}, u32[]{:S(2)}, u32[]{:S(2)}) collective-permute-start(bf16[1024,256]{0,1:T(8,128)(2,1)S(1)} %fusion.15), channel_id=1, source_target_pairs={{0,2},{2,0},{1,3},{3,1},{4,6},{6,4},{5,7},{7,5},{8,10},{10,8},{9,1... | collective-permute-start | bytes 1572872 | tf_op jit(solution)/shard_map/ppermute | solution.py:18
  554.4 13.8 %collective-permute-start.104 = (bf16[1024,256]{0,1:T(8,128)(2,1)S(1)}, bf16[1024,256]{0,1:T(8,128)(2,1)S(1)}, u32[]{:S(2)}, u32[]{:S(2)}) collective-permute-start(bf16[1024,256]{0,1:T(8,128)(2,1)S(1)} %add_convert_fusion.1), channel_id=1, source_target_pairs={{0,4},{4,0},{1,5},{5,1},{2,6},{6,2},{3,7},{7,3},{8,12},{12,8},{9,1... | collective-permute-start | bytes 1572872 | tf_op jit(solution)/shard_map/ppermute | solution.py:18
  572.9 7.6 %collective-permute-start.106 = (bf16[512,256]{0,1:T(8,128)(2,1)S(1)}, bf16[512,256]{0,1:T(8,128)(2,1)S(1)}, u32[]{:S(2)}, u32[]{:S(2)}) collective-permute-start(bf16[512,256]{0,1:T(8,128)(2,1)S(1)} %get-tuple-element.84), channel_id=1, source_target_pairs={{0,8},{8,0},{16,24},{24,16},{32,40},{40,32},{48,56},{56,48},{64,72... | collective-permute-start | bytes 786440 | tf_op jit(solution)/shard_map/ppermute | solution.py:18
  (119 other events, 968.3 us)

commit v10 on v9

--- a/solution.py
+++ b/solution.py
@@ -251,7 +251,7 @@
             "cp,cr->pr", g_share, weight_half, preferred_element_type=jnp.float32
         )
         part_len = piv_dev // group_size
-        if height == levels:
+        if height >= levels - 1:
             summed = sum_solution_halved(solve_term, height, position)
         else:
             summed = sum_solution(solve_term, height)

time: 606 us -> 604 us (level)
    ppermute x110 -> x111, waiting for transfers between devices: 322 us -> 319 us  [partner(): return lax.ppermute(block, axis, route)]
    ppermute x110 -> x111, starting transfers between devices: 184 us -> 185 us  [partner(): return lax.ppermute(block, axis, route)]
  transfers between devices with their start and end apart: 110 -> 111, of which waited for: 85 -> 86; matrix products, arithmetic and copies ran while one was open for 6% -> 6% of each run, Pallas kernels for 0% -> 0%
where the time goes in v10:
time: 604 us; the launch traced here: 593 us
  waiting for transfers between devices  319 us (53%)
  starting transfers between devices  185 us (31%)
  local copies, waits for them, and re-layouts  32.7 us (5%)
  other arithmetic  32.5 us (5%)
  matrix products  21.3 us (4%)
    ppermute x111, waiting for transfers between devices, partner(): return lax.ppermute(block, axis, route)  319 us
    ppermute x111, starting transfers between devices, partner(): return lax.ppermute(block, axis, route)  185 us
  transfers between devices with their start and end apart: 111, of which 86 were waited for; matrix products, arithmetic and copies ran while one was open for 6% of the time, Pallas kernels for 0%

profile of v10, /device:TPU:1, one launch (start us, length us, event | category | flops | bytes accessed | tf_op | source)
XLA Modules:
  0.0 593.2 jit_solution(6381511446146316210)
XLA Ops:
  19.2 5.2 collective-permute-start.3
  37.4 13.0 %collective-permute-done.9 = bf16[1024,256]{0,1:T(8,128)(2,1)S(1)} collective-permute-done((bf16[1024,256]{0,1:T(8,128)(2,1)S(1)}, bf16[1024,256]{0,1:T(8,128)(2,1)S(1)}, u32[]{:S(2)}, u32[]{:S(2)}) %collective-permute-start.9) | collective-permute-done | bytes 524320 | tf_op jit(solution)/shard_map/ppermute | solution.py:18
  52.7 12.0 %collective-permute-done.10 = bf16[1024,256]{0,1:T(8,128)(2,1)S(1)} collective-permute-done((bf16[1024,256]{0,1:T(8,128)(2,1)S(1)}, bf16[1024,256]{0,1:T(8,128)(2,1)S(1)}, u32[]{:S(2)}, u32[]{:S(2)}) %collective-permute-start.10) | collective-permute-done | bytes 524320 | tf_op jit(solution)/shard_map/ppermute | solution.py:18
  78.8 5.7 collective-permute-done.13
  106.6 7.4 %collective-permute-done.21 = bf16[512,256]{0,1:T(8,128)(2,1)S(1)} collective-permute-done((bf16[512,256]{0,1:T(8,128)(2,1)S(1)}, bf16[512,256]{0,1:T(8,128)(2,1)S(1)}, u32[]{:S(2)}, u32[]{:S(2)}) %collective-permute-start.21) | collective-permute-done | bytes 262176 | tf_op jit(solution)/shard_map/ppermute | solution.py:18
  117.0 5.3 collective-permute-done.22
  137.9 4.6 collective-permute-done.26
  150.5 5.5 collective-permute-start.29
  171.0 4.6 collective-permute-done.35
  193.8 10.8 %collective-permute-done.40 = bf16[512,256]{1,0:T(8,128)(2,1)S(1)} collective-permute-done((bf16[512,256]{1,0:T(8,128)(2,1)S(1)}, bf16[512,256]{1,0:T(8,128)(2,1)S(1)}, u32[]{:S(2)}, u32[]{:S(2)}) %collective-permute-start.40) | collective-permute-done | bytes 262176 | tf_op jit(solution)/shard_map/ppermute | solution.py:18
  210.1 4.4 collective-permute-start.43
  231.9 5.3 collective-permute-done.49
  253.6 6.1 %collective-permute-start.54 = (bf16[384,256]{1,0:T(8,128)(2,1)S(1)}, bf16[384,256]{1,0:T(8,128)(2,1)S(1)}, u32[]{:S(2)}, u32[]{:S(2)}) collective-permute-start(bf16[384,256]{1,0:T(8,128)(2,1)S(1)} %pad_maximum_fusion.16), channel_id=1, source_target_pairs={{0,128},{128,0},{8,136},{136,8},{16,144},{144,16},{24,152},{152,24... | collective-permute-start | bytes 589832 | tf_op jit(solution)/shard_map/ppermute | solution.py:18
  270.1 11.8 %collective-permute-start.57 = (bf16[1,512,256]{2,1,0:T(8,128)(2,1)S(1)}, bf16[1,512,256]{2,1,0:T(8,128)(2,1)S(1)}, u32[]{:S(2)}, u32[]{:S(2)}) collective-permute-start(bf16[1,512,256]{2,1,0:T(8,128)(2,1)S(1)} %pad_maximum_fusion.14), channel_id=1, source_target_pairs={{0,1},{1,0},{2,3},{3,2},{4,5},{5,4},{6,7},{7,6},{8,9},{9,8},{10,11... | collective-permute-start | bytes 786440 | tf_op jit(solution)/shard_map/ppermute | solution.py:18
  296.1 4.4 collective-permute-done.63
  315.4 6.1 %collective-permute-done.67 = bf16[256,256]{1,0:T(8,128)(2,1)S(1)} collective-permute-done((bf16[256,256]{1,0:T(8,128)(2,1)S(1)}, bf16[256,256]{1,0:T(8,128)(2,1)S(1)}, u32[]{:S(2)}, u32[]{:S(2)}) %collective-permute-start.67) | collective-permute-done | bytes 131104 | tf_op jit(solution)/shard_map/ppermute | solution.py:18
  321.6 5.7 collective-permute-start.68
  327.3 5.1 collective-permute-done.68
  338.5 9.5 %collective-permute-start.70 = (bf16[2,2,128,256]{3,2,0,1:T(8,128)(2,1)S(1)}, bf16[2,2,128,256]{3,2,0,1:T(8,128)(2,1)S(1)}, u32[]{:S(2)}, u32[]{:S(2)}) collective-permute-start(bf16[2,2,128,256]{3,2,0,1:T(8,128)(2,1)S(1)} %bitcast.247), channel_id=1, source_target_pairs={{0,1},{1,0},{2,3},{3,2},{4,5},{5,4},{6,7},{7,6},{8,9},{9,8},{10,11... | collective-permute-start | bytes 786440 | tf_op jit(solution)/shard_map/ppermute | solution.py:18
  368.3 4.5 collective-permute-done.75
  389.3 5.8 collective-permute-done.79
  401.6 7.4 %collective-permute-start.81 = (bf16[2,2,128,256]{2,3,0,1:T(8,128)(2,1)S(1)}, bf16[2,2,128,256]{2,3,0,1:T(8,128)(2,1)S(1)}, u32[]{:S(2)}, u32[]{:S(2)}) collective-permute-start(bf16[2,2,128,256]{2,3,0,1:T(8,128)(2,1)S(1)} %bitcast.248), channel_id=1, source_target_pairs={{0,1},{1,0},{2,3},{3,2},{4,5},{5,4},{6,7},{7,6},{8,9},{9,8},{10,11... | collective-permute-start | bytes 786440 | tf_op jit(solution)/shard_map/ppermute | solution.py:18
  440.4 6.3 %collective-permute-done.88 = bf16[512,256]{0,1:T(8,128)(2,1)S(1)} collective-permute-done((bf16[512,256]{0,1:T(8,128)(2,1)S(1)}, bf16[512,256]{0,1:T(8,128)(2,1)S(1)}, u32[]{:S(2)}, u32[]{:S(2)}) %collective-permute-start.88) | collective-permute-done | bytes 262176 | tf_op jit(solution)/shard_map/ppermute | solution.py:18
  450.4 5.7 collective-permute-done.89
  456.3 6.3 %collective-permute-done.90 = bf16[512,256]{0,1:T(8,128)(2,1)S(1)} collective-permute-done((bf16[512,256]{0,1:T(8,128)(2,1)S(1)}, bf16[512,256]{0,1:T(8,128)(2,1)S(1)}, u32[]{:S(2)}, u32[]{:S(2)}) %collective-permute-start.90) | collective-permute-done | bytes 262176 | tf_op jit(solution)/shard_map/ppermute | solution.py:18
  483.2 6.8 %collective-permute-done.95 = bf16[512,256]{0,1:T(8,128)(2,1)S(1)} collective-permute-done((bf16[512,256]{0,1:T(8,128)(2,1)S(1)}, bf16[512,256]{0,1:T(8,128)(2,1)S(1)}, u32[]{:S(2)}, u32[]{:S(2)}) %collective-permute-start.95) | collective-permute-done | bytes 262176 | tf_op jit(solution)/shard_map/ppermute | solution.py:18
  490.4 7.9 %collective-permute-done.96 = bf16[512,256]{0,1:T(8,128)(2,1)S(1)} collective-permute-done((bf16[512,256]{0,1:T(8,128)(2,1)S(1)}, bf16[512,256]{0,1:T(8,128)(2,1)S(1)}, u32[]{:S(2)}, u32[]{:S(2)}) %collective-permute-start.96) | collective-permute-done | bytes 262176 | tf_op jit(solution)/shard_map/ppermute | solution.py:18
  503.6 7.4 %collective-permute-done.98 = bf16[512,256]{0,1:T(8,128)(2,1)S(1)} collective-permute-done((bf16[512,256]{0,1:T(8,128)(2,1)S(1)}, bf16[512,256]{0,1:T(8,128)(2,1)S(1)}, u32[]{:S(2)}, u32[]{:S(2)}) %collective-permute-start.98) | collective-permute-done | bytes 262176 | tf_op jit(solution)/shard_map/ppermute | solution.py:18
  513.9 5.5 collective-permute-done.99
  539.2 12.4 %collective-permute-done.104 = bf16[1024,256]{0,1:T(8,128)(2,1)S(1)} collective-permute-done((bf16[1024,256]{0,1:T(8,128)(2,1)S(1)}, bf16[1024,256]{0,1:T(8,128)(2,1)S(1)}, u32[]{:S(2)}, u32[]{:S(2)}) %collective-permute-start.104) | collective-permute-done | bytes 524320 | tf_op jit(solution)/shard_map/ppermute | solution.py:18
  552.2 13.5 %collective-permute-done.105 = bf16[1024,256]{0,1:T(8,128)(2,1)S(1)} collective-permute-done((bf16[1024,256]{0,1:T(8,128)(2,1)S(1)}, bf16[1024,256]{0,1:T(8,128)(2,1)S(1)}, u32[]{:S(2)}, u32[]{:S(2)}) %collective-permute-start.105) | collective-permute-done | bytes 524320 | tf_op jit(solution)/shard_map/ppermute | solution.py:18
  570.5 7.4 %collective-permute-done.107 = bf16[512,256]{0,1:T(8,128)(2,1)S(1)} collective-permute-done((bf16[512,256]{0,1:T(8,128)(2,1)S(1)}, bf16[512,256]{0,1:T(8,128)(2,1)S(1)}, u32[]{:S(2)}, u32[]{:S(2)}) %collective-permute-start.107) | collective-permute-done | bytes 262176 | tf_op jit(solution)/shard_map/ppermute | solution.py:18
  (546 shorter events, 360.8 us)
Async XLA Ops:
  0.6 12.1 %collective-permute-start.4 = (bf16[128,256]{1,0:T(8,128)(2,1)}, bf16[128,256]{1,0:T(8,128)(2,1)S(1)}, u32[]{:S(2)}, u32[]{:S(2)}) collective-permute-start(bf16[128,256]{1,0:T(8,128)(2,1)} %param.10), channel_id=1, source_target_pairs={{0,8},{8,0},{16,24},{24,16},{32,40},{40,32},{48,56},{56,48},{64,72... | collective-permute-start | bytes 196616 | tf_op jit(solution)/shard_map/ppermute | solution.py:18
  2.8 10.2 %collective-permute-start.1 = (bf16[1,128,256]{2,1,0:T(8,128)(2,1)}, bf16[1,128,256]{2,1,0:T(8,128)(2,1)S(1)}, u32[]{:S(2)}, u32[]{:S(2)}) collective-permute-start(bf16[1,128,256]{2,1,0:T(8,128)(2,1)} %bitcast.238), channel_id=1, source_target_pairs={{0,4},{4,0},{1,5},{5,1},{2,6},{6,2},{3,7},{7,3},{8,12},{12,8},{9,1... | collective-permute-start | bytes 196616 | tf_op jit(solution)/shard_map/ppermute | solution.py:18
  9.8 17.1 %collective-permute-start = (bf16[496,256]{1,0:T(8,128)(2,1)S(1)}, bf16[496,256]{1,0:T(8,128)(2,1)S(1)}, u32[]{:S(2)}, u32[]{:S(2)}) collective-permute-start(bf16[496,256]{1,0:T(8,128)(2,1)S(1)} %constant_dynamic-update-slice_fusion), channel_id=1, source_target_pairs={{0,8},{8,0},{16,24},{24,16},{32,40},{40,32},{48,56},{56,48},{64,72... | collective-permute-start | bytes 761864 | tf_op jit(solution)/shard_map/ppermute | solution.py:18
  17.5 6.9 %collective-permute-start.6 = (bf16[1,256,256]{2,1,0:T(8,128)(2,1)S(1)}, bf16[1,256,256]{2,1,0:T(8,128)(2,1)S(1)}, u32[]{:S(2)}, u32[]{:S(2)}) collective-permute-start(bf16[1,256,256]{2,1,0:T(8,128)(2,1)S(1)} %pad_maximum_fusion.18), channel_id=1, source_target_pairs={{0,2},{2,0},{1,3},{3,1},{4,6},{6,4},{5,7},{7,5},{8,10},{10,8},{9,1... | collective-permute-start | bytes 393224 | tf_op jit(solution)/shard_map/ppermute | solution.py:18
  19.2 8.5 %collective-permute-start.3 = (bf16[1,512,256]{2,1,0:T(8,128)(2,1)S(1)}, bf16[1,512,256]{2,1,0:T(8,128)(2,1)S(1)}, u32[]{:S(2)}, u32[]{:S(2)}) collective-permute-start(bf16[1,512,256]{2,1,0:T(8,128)(2,1)S(1)} %pad_maximum_fusion.5), channel_id=1, source_target_pairs={{0,1},{1,0},{2,3},{3,2},{4,5},{5,4},{6,7},{7,6},{8,9},{9,8},{10,11... | collective-permute-start | bytes 786440 | tf_op jit(solution)/shard_map/ppermute | solution.py:18
  37.0 13.4 %collective-permute-start.9 = (bf16[1024,256]{0,1:T(8,128)(2,1)S(1)}, bf16[1024,256]{0,1:T(8,128)(2,1)S(1)}, u32[]{:S(2)}, u32[]{:S(2)}) collective-permute-start(bf16[1024,256]{0,1:T(8,128)(2,1)S(1)} %fusion.16), channel_id=1, source_target_pairs={{0,2},{2,0},{1,3},{3,1},{4,6},{6,4},{5,7},{7,5},{8,10},{10,8},{9,1... | collective-permute-start | bytes 1572872 | tf_op jit(solution)/shard_map/ppermute | solution.py:18
  50.6 14.1 %collective-permute-start.10 = (bf16[1024,256]{0,1:T(8,128)(2,1)S(1)}, bf16[1024,256]{0,1:T(8,128)(2,1)S(1)}, u32[]{:S(2)}, u32[]{:S(2)}) collective-permute-start(bf16[1024,256]{0,1:T(8,128)(2,1)S(1)} %add_convert_fusion.3), channel_id=1, source_target_pairs={{0,4},{4,0},{1,5},{5,1},{2,6},{6,2},{3,7},{7,3},{8,12},{12,8},{9,1... | collective-permute-start | bytes 1572872 | tf_op jit(solution)/shard_map/ppermute | solution.py:18
  75.0 9.5 %collective-permute-start.13 = (bf16[608,256]{1,0:T(8,128)(2,1)S(1)}, bf16[608,256]{1,0:T(8,128)(2,1)S(1)}, u32[]{:S(2)}, u32[]{:S(2)}) collective-permute-start(bf16[608,256]{1,0:T(8,128)(2,1)S(1)} %get-tuple-element.36), channel_id=1, source_target_pairs={{0,16},{16,0},{8,24},{24,8},{32,48},{48,32},{40,56},{56,40},{64,80... | collective-permute-start | bytes 933896 | tf_op jit(solution)/shard_map/ppermute | solution.py:18
  77.9 8.5 %collective-permute-start.14 = (bf16[1,128,256]{2,1,0:T(8,128)(2,1)S(1)}, bf16[1,128,256]{2,1,0:T(8,128)(2,1)S(1)}, u32[]{:S(2)}, u32[]{:S(2)}) collective-permute-start(bf16[1,128,256]{2,1,0:T(8,128)(2,1)S(1)} %bitcast.234), channel_id=1, source_target_pairs={{0,4},{4,0},{1,5},{5,1},{2,6},{6,2},{3,7},{7,3},{8,12},{12,8},{9,1... | collective-permute-start | bytes 196616 | tf_op jit(solution)/shard_map/ppermute | solution.py:18
  91.1 7.9 %collective-permute-start.16 = (bf16[1,512,256]{2,1,0:T(8,128)(2,1)S(1)}, bf16[1,512,256]{2,1,0:T(8,128)(2,1)S(1)}, u32[]{:S(2)}, u32[]{:S(2)}) collective-permute-start(bf16[1,512,256]{2,1,0:T(8,128)(2,1)S(1)} %pad_maximum_fusion.7), channel_id=1, source_target_pairs={{0,1},{1,0},{2,3},{3,2},{4,5},{5,4},{6,7},{7,6},{8,9},{9,8},{10,11... | collective-permute-start | bytes 786440 | tf_op jit(solution)/shard_map/ppermute | solution.py:18
  106.4 7.6 %collective-permute-start.21 = (bf16[512,256]{0,1:T(8,128)(2,1)S(1)}, bf16[512,256]{0,1:T(8,128)(2,1)S(1)}, u32[]{:S(2)}, u32[]{:S(2)}) collective-permute-start(bf16[512,256]{0,1:T(8,128)(2,1)S(1)} %fusion.44), channel_id=1, source_target_pairs={{0,2},{2,0},{1,3},{3,1},{4,6},{6,4},{5,7},{7,5},{8,10},{10,8},{9,1... | collective-permute-start | bytes 786440 | tf_op jit(solution)/shard_map/ppermute | solution.py:18
  114.0 8.2 %collective-permute-start.22 = (bf16[512,256]{0,1:T(8,128)(2,1)S(1)}, bf16[512,256]{0,1:T(8,128)(2,1)S(1)}, u32[]{:S(2)}, u32[]{:S(2)}) collective-permute-start(bf16[512,256]{0,1:T(8,128)(2,1)S(1)} %add_convert_fusion.7), channel_id=1, source_target_pairs={{0,4},{4,0},{1,5},{5,1},{2,6},{6,2},{3,7},{7,3},{8,12},{12,8},{9,1... | collective-permute-start | bytes 786440 | tf_op jit(solution)/shard_map/ppermute | solution.py:18
  147.9 8.1 %collective-permute-start.31 = (bf16[1,256,256]{2,1,0:T(8,128)(2,1)S(1)}, bf16[1,256,256]{2,1,0:T(8,128)(2,1)S(1)}, u32[]{:S(2)}, u32[]{:S(2)}) collective-permute-start(bf16[1,256,256]{2,1,0:T(8,128)(2,1)S(1)} %pad_maximum_fusion.22), channel_id=1, source_target_pairs={{0,2},{2,0},{1,3},{3,1},{4,6},{6,4},{5,7},{7,5},{8,10},{10,8},{9,1... | collective-permute-start | bytes 393224 | tf_op jit(solution)/shard_map/ppermute | solution.py:18
  150.5 8.4 %collective-permute-start.29 = (bf16[1,512,256]{2,1,0:T(8,128)(2,1)S(1)}, bf16[1,512,256]{2,1,0:T(8,128)(2,1)S(1)}, u32[]{:S(2)}, u32[]{:S(2)}) collective-permute-start(bf16[1,512,256]{2,1,0:T(8,128)(2,1)S(1)} %pad_maximum_fusion.9), channel_id=1, source_target_pairs={{0,1},{1,0},{2,3},{3,2},{4,5},{5,4},{6,7},{7,6},{8,9},{9,8},{10,11... | collective-permute-start | bytes 786440 | tf_op jit(solution)/shard_map/ppermute | solution.py:18
  190.7 13.9 %collective-permute-start.40 = (bf16[512,256]{1,0:T(8,128)(2,1)S(1)}, bf16[512,256]{1,0:T(8,128)(2,1)S(1)}, u32[]{:S(2)}, u32[]{:S(2)}) collective-permute-start(bf16[512,256]{1,0:T(8,128)(2,1)S(1)} %pad_maximum_fusion.11), channel_id=1, source_target_pairs={{0,64},{64,0},{8,72},{72,8},{16,80},{80,16},{24,88},{88,24},{32,96... | collective-permute-start | bytes 786440 | tf_op jit(solution)/shard_map/ppermute | solution.py:18
  193.8 11.5 %collective-permute-start.41 = (bf16[1,128,256]{2,1,0:T(8,128)(2,1)S(1)}, bf16[1,128,256]{2,1,0:T(8,128)(2,1)S(1)}, u32[]{:S(2)}, u32[]{:S(2)}) collective-permute-start(bf16[1,128,256]{2,1,0:T(8,128)(2,1)S(1)} %bitcast.230), channel_id=1, source_target_pairs={{0,4},{4,0},{1,5},{5,1},{2,6},{6,2},{3,7},{7,3},{8,12},{12,8},{9,1... | collective-permute-start | bytes 196616 | tf_op jit(solution)/shard_map/ppermute | solution.py:18
  210.1 10.2 %collective-permute-start.43 = (bf16[1,512,256]{2,1,0:T(8,128)(2,1)S(1)}, bf16[1,512,256]{2,1,0:T(8,128)(2,1)S(1)}, u32[]{:S(2)}, u32[]{:S(2)}) collective-permute-start(bf16[1,512,256]{2,1,0:T(8,128)(2,1)S(1)} %pad_maximum_fusion.12), channel_id=1, source_target_pairs={{0,1},{1,0},{2,3},{3,2},{4,5},{5,4},{6,7},{7,6},{8,9},{9,8},{10,11... | collective-permute-start | bytes 786440 | tf_op jit(solution)/shard_map/ppermute | solution.py:18
  253.6 10.0 %collective-permute-start.54 = (bf16[384,256]{1,0:T(8,128)(2,1)S(1)}, bf16[384,256]{1,0:T(8,128)(2,1)S(1)}, u32[]{:S(2)}, u32[]{:S(2)}) collective-permute-start(bf16[384,256]{1,0:T(8,128)(2,1)S(1)} %pad_maximum_fusion.16), channel_id=1, source_target_pairs={{0,128},{128,0},{8,136},{136,8},{16,144},{144,16},{24,152},{152,24... | collective-permute-start | bytes 589832 | tf_op jit(solution)/shard_map/ppermute | solution.py:18
  268.2 13.8 %collective-permute-start.59 = (bf16[1,256,256]{2,1,0:T(8,128)(2,1)S(1)}, bf16[1,256,256]{2,1,0:T(8,128)(2,1)S(1)}, u32[]{:S(2)}, u32[]{:S(2)}) collective-permute-start(bf16[1,256,256]{2,1,0:T(8,128)(2,1)S(1)} %pad_maximum_fusion.26), channel_id=1, source_target_pairs={{0,2},{2,0},{1,3},{3,1},{4,6},{6,4},{5,7},{7,5},{8,10},{10,8},{9,1... | collective-permute-start | bytes 393224 | tf_op jit(solution)/shard_map/ppermute | solution.py:18
  270.1 15.6 %collective-permute-start.57 = (bf16[1,512,256]{2,1,0:T(8,128)(2,1)S(1)}, bf16[1,512,256]{2,1,0:T(8,128)(2,1)S(1)}, u32[]{:S(2)}, u32[]{:S(2)}) collective-permute-start(bf16[1,512,256]{2,1,0:T(8,128)(2,1)S(1)} %pad_maximum_fusion.14), channel_id=1, source_target_pairs={{0,1},{1,0},{2,3},{3,2},{4,5},{5,4},{6,7},{7,6},{8,9},{9,8},{10,11... | collective-permute-start | bytes 786440 | tf_op jit(solution)/shard_map/ppermute | solution.py:18
  321.6 10.9 %collective-permute-start.68 = (bf16[256,256]{1,0:T(8,128)(2,1)S(1)}, bf16[256,256]{1,0:T(8,128)(2,1)S(1)}, u32[]{:S(2)}, u32[]{:S(2)}) collective-permute-start(bf16[256,256]{1,0:T(8,128)(2,1)S(1)} %fusion.88), channel_id=1, source_target_pairs={{0,128},{128,0},{8,136},{136,8},{16,144},{144,16},{24,152},{152,24... | collective-permute-start | bytes 393224 | tf_op jit(solution)/shard_map/ppermute | solution.py:18
  338.5 10.6 %collective-permute-start.70 = (bf16[2,2,128,256]{3,2,0,1:T(8,128)(2,1)S(1)}, bf16[2,2,128,256]{3,2,0,1:T(8,128)(2,1)S(1)}, u32[]{:S(2)}, u32[]{:S(2)}) collective-permute-start(bf16[2,2,128,256]{3,2,0,1:T(8,128)(2,1)S(1)} %bitcast.247), channel_id=1, source_target_pairs={{0,1},{1,0},{2,3},{3,2},{4,5},{5,4},{6,7},{7,6},{8,9},{9,8},{10,11... | collective-permute-start | bytes 786440 | tf_op jit(solution)/shard_map/ppermute | solution.py:18
  401.6 8.5 %collective-permute-start.81 = (bf16[2,2,128,256]{2,3,0,1:T(8,128)(2,1)S(1)}, bf16[2,2,128,256]{2,3,0,1:T(8,128)(2,1)S(1)}, u32[]{:S(2)}, u32[]{:S(2)}) collective-permute-start(bf16[2,2,128,256]{2,3,0,1:T(8,128)(2,1)S(1)} %bitcast.248), channel_id=1, source_target_pairs={{0,1},{1,0},{2,3},{3,2},{4,5},{5,4},{6,7},{7,6},{8,9},{9,8},{10,11... | collective-permute-start | bytes 786440 | tf_op jit(solution)/shard_map/ppermute | solution.py:18
  438.6 8.1 %collective-permute-start.88 = (bf16[512,256]{0,1:T(8,128)(2,1)S(1)}, bf16[512,256]{0,1:T(8,128)(2,1)S(1)}, u32[]{:S(2)}, u32[]{:S(2)}) collective-permute-start(bf16[512,256]{0,1:T(8,128)(2,1)S(1)} %get-tuple-element.80), channel_id=1, source_target_pairs={{0,8},{8,0},{16,24},{24,16},{32,40},{40,32},{48,56},{56,48},{64,72... | collective-permute-start | bytes 786440 | tf_op jit(solution)/shard_map/ppermute | solution.py:18
  446.8 9.3 %collective-permute-start.89 = (bf16[512,256]{0,1:T(8,128)(2,1)S(1)}, bf16[512,256]{0,1:T(8,128)(2,1)S(1)}, u32[]{:S(2)}, u32[]{:S(2)}) collective-permute-start(bf16[512,256]{0,1:T(8,128)(2,1)S(1)} %fusion.52), channel_id=1, source_target_pairs={{0,16},{16,0},{8,24},{24,8},{32,48},{48,32},{40,56},{56,40},{64,80... | collective-permute-start | bytes 786440 | tf_op jit(solution)/shard_map/ppermute | solution.py:18
  482.2 7.8 %collective-permute-start.95 = (bf16[512,256]{0,1:T(8,128)(2,1)S(1)}, bf16[512,256]{0,1:T(8,128)(2,1)S(1)}, u32[]{:S(2)}, u32[]{:S(2)}) collective-permute-start(bf16[512,256]{0,1:T(8,128)(2,1)S(1)} %fusion.43), channel_id=1, source_target_pairs={{0,2},{2,0},{1,3},{3,1},{4,6},{6,4},{5,7},{7,5},{8,10},{10,8},{9,1... | collective-permute-start | bytes 786440 | tf_op jit(solution)/shard_map/ppermute | solution.py:18
  490.1 8.2 %collective-permute-start.96 = (bf16[512,256]{0,1:T(8,128)(2,1)S(1)}, bf16[512,256]{0,1:T(8,128)(2,1)S(1)}, u32[]{:S(2)}, u32[]{:S(2)}) collective-permute-start(bf16[512,256]{0,1:T(8,128)(2,1)S(1)} %add_convert_fusion.5), channel_id=1, source_target_pairs={{0,4},{4,0},{1,5},{5,1},{2,6},{6,2},{3,7},{7,3},{8,12},{12,8},{9,1... | collective-permute-start | bytes 786440 | tf_op jit(solution)/shard_map/ppermute | solution.py:18
  503.4 7.6 %collective-permute-start.98 = (bf16[512,256]{0,1:T(8,128)(2,1)S(1)}, bf16[512,256]{0,1:T(8,128)(2,1)S(1)}, u32[]{:S(2)}, u32[]{:S(2)}) collective-permute-start(bf16[512,256]{0,1:T(8,128)(2,1)S(1)} %get-tuple-element.82), channel_id=1, source_target_pairs={{0,8},{8,0},{16,24},{24,16},{32,40},{40,32},{48,56},{56,48},{64,72... | collective-permute-start | bytes 786440 | tf_op jit(solution)/shard_map/ppermute | solution.py:18
  511.1 8.2 %collective-permute-start.99 = (bf16[512,256]{0,1:T(8,128)(2,1)S(1)}, bf16[512,256]{0,1:T(8,128)(2,1)S(1)}, u32[]{:S(2)}, u32[]{:S(2)}) collective-permute-start(bf16[512,256]{0,1:T(8,128)(2,1)S(1)} %fusion.53), channel_id=1, source_target_pairs={{0,16},{16,0},{8,24},{24,8},{32,48},{48,32},{40,56},{56,40},{64,80... | collective-permute-start | bytes 786440 | tf_op jit(solution)/shard_map/ppermute | solution.py:18
  538.5 13.2 %collective-permute-start.104 = (bf16[1024,256]{0,1:T(8,128)(2,1)S(1)}, bf16[1024,256]{0,1:T(8,128)(2,1)S(1)}, u32[]{:S(2)}, u32[]{:S(2)}) collective-permute-start(bf16[1024,256]{0,1:T(8,128)(2,1)S(1)} %fusion.15), channel_id=1, source_target_pairs={{0,2},{2,0},{1,3},{3,1},{4,6},{6,4},{5,7},{7,5},{8,10},{10,8},{9,1... | collective-permute-start | bytes 1572872 | tf_op jit(solution)/shard_map/ppermute | solution.py:18
  551.8 13.8 %collective-permute-start.105 = (bf16[1024,256]{0,1:T(8,128)(2,1)S(1)}, bf16[1024,256]{0,1:T(8,128)(2,1)S(1)}, u32[]{:S(2)}, u32[]{:S(2)}) collective-permute-start(bf16[1024,256]{0,1:T(8,128)(2,1)S(1)} %add_convert_fusion.1), channel_id=1, source_target_pairs={{0,4},{4,0},{1,5},{5,1},{2,6},{6,2},{3,7},{7,3},{8,12},{12,8},{9,1... | collective-permute-start | bytes 1572872 | tf_op jit(solution)/shard_map/ppermute | solution.py:18
  570.4 7.6 %collective-permute-start.107 = (bf16[512,256]{0,1:T(8,128)(2,1)S(1)}, bf16[512,256]{0,1:T(8,128)(2,1)S(1)}, u32[]{:S(2)}, u32[]{:S(2)}) collective-permute-start(bf16[512,256]{0,1:T(8,128)(2,1)S(1)} %get-tuple-element.84), channel_id=1, source_target_pairs={{0,8},{8,0},{16,24},{24,16},{32,40},{40,32},{48,56},{56,48},{64,72... | collective-permute-start | bytes 786440 | tf_op jit(solution)/shard_map/ppermute | solution.py:18
  (120 other events, 968.6 us)
